TPU v7x, 32 devices: a whole 2x2x4 slice. The times are simulated.
32 devices in a mesh: half: 2 (over x), grp: 4 (over z), tile: 4 (over y, core).
Axes of the slice: x: 2, y: 2, z: 4, core: 2. Of those that a mesh axis runs over, the one named last changes fastest.
Arguments:
- core_tensor: bfloat16 [256, 96, 160], P(('half', 'grp', 'tile')), may hold values from -0.109375 to 0.109375
- term_operators: bfloat16 [32, 8, 8, 8], P(('half', 'grp', 'tile')), may hold values from -2 to 2
- block_terms: int32 [32, 8], P(('half', 'grp', 'tile')), may hold values from 0 to 8, as said below
- orbitals: bfloat16 [1024, 256, 256], P(('half', 'grp'), 'tile'), may hold values from -6 to 6
- potential: float32 [2, 8, 1024, 256], P(None, None, ('half', 'grp'), 'tile'), may hold values from -2.5 to 2.5
- kinetic: bfloat16 [1024, 1024], replicated, may hold values from -0.1875 to 0.1875
Outputs:
- h_orbitals: bfloat16 [1024, 256, 256], P(('half', 'grp'), 'tile')
Inputs may be any that keep to these rules, and one draw needn't show every extreme that they name: `block_terms`: each row lists distinct terms in its first slots and 8 in all later slots; every row lists at least one term, and some row lists 8 terms.
All inputs are finite; a program needn't handle non-finite values.
Results may differ from a plain program's by a relative error of at most 0.0056.
Values may be sent and summed in bfloat16 or wider, within the bound.
No kernel may reach another device: no remote copies, remote signals or barrier semaphores. Data moves between devices by JAX's collectives and lax.ppermute only.
A program may use at most 128 MiB of HBM per device.

v0:
```python
import jax
import jax.numpy as jnp
from jax import lax
from jax.sharding import PartitionSpec as P

TERMS = 8


def slot_sums(core_tensor, term_operators, block_terms):
    rows_tile, width_b, width_a = core_tensor.shape
    flat_core = core_tensor.reshape(rows_tile, width_b * width_a)
    listed = block_terms[0]
    live_slots = jnp.sum((listed < TERMS).astype(jnp.int32))
    labels = jnp.arange(TERMS, dtype=jnp.int32)

    def add_slot(slot_index, running):
        sum_a, sum_b = running
        operator = term_operators[0, slot_index]
        mixed_core = jnp.einsum(
            "rs,rq->sq", operator, flat_core, preferred_element_type=jnp.float32
        )
        mixed_core = mixed_core.astype(jnp.bfloat16).reshape(rows_tile, width_b, width_a)
        gram_a = jnp.einsum(
            "rba,rbc->ac", core_tensor, mixed_core, preferred_element_type=jnp.float32
        )
        gram_b = jnp.einsum(
            "rba,rda->bd", core_tensor, mixed_core, preferred_element_type=jnp.float32
        )
        chosen = (labels == listed[slot_index]).astype(jnp.float32)
        return (sum_a + chosen[:, None, None] * gram_a, sum_b + chosen[:, None, None] * gram_b)

    start_sums = (
        jnp.zeros((TERMS, width_a, width_a), jnp.float32),
        jnp.zeros((TERMS, width_b, width_b), jnp.float32),
    )
    return lax.fori_loop(0, live_slots, add_slot, start_sums)


def point_action(points, weights, stack_a, stack_b):
    width_a = stack_a.shape[0]
    width_b = stack_b.shape[0]
    count_points = points.shape[0]
    prod_a = jnp.dot(points[:, :width_a], stack_a, preferred_element_type=jnp.float32).reshape(
        count_points, TERMS, width_a
    )
    prod_b = jnp.dot(points[:, width_a:], stack_b, preferred_element_type=jnp.float32).reshape(
        count_points, TERMS, width_b
    )
    act_a = jnp.sum(prod_a * weights[0].T[:, :, None], axis=1)
    act_b = jnp.sum(prod_b * weights[1].T[:, :, None], axis=1)
    return jnp.concatenate([act_a, act_b], axis=1)


def kinetic_columns(kinetic, orbitals):
    rows_x, rows_y, width_all = orbitals.shape
    halves = lax.axis_size("half")
    members = lax.axis_size("grp")
    groups = halves * members
    columns = rows_y * width_all // groups
    pieces = orbitals.reshape(rows_x, groups, columns)
    applied = jnp.einsum(
        "xz,zik->xik",
        kinetic,
        lax.all_to_all(pieces, ("half", "grp"), split_axis=1, concat_axis=0, tiled=True),
        preferred_element_type=jnp.float32,
    )
    applied = applied.astype(jnp.bfloat16)
    returned = lax.all_to_all(applied, ("half", "grp"), split_axis=0, concat_axis=1, tiled=True)
    return returned.reshape(rows_x, rows_y, width_all)


def body(core_tensor, term_operators, block_terms, orbitals, potential, kinetic):
    sum_a, sum_b = slot_sums(core_tensor, term_operators, block_terms)
    total_a, total_b = lax.psum((sum_a, sum_b), ("half", "grp", "tile"))
    mean_a = total_a.astype(jnp.bfloat16)
    mean_b = total_b.astype(jnp.bfloat16)
    kinetic_part = kinetic_columns(kinetic, orbitals)
    rows_x, rows_y, width_all = orbitals.shape
    width_a = mean_a.shape[1]
    width_b = mean_b.shape[1]
    stack_a = jnp.transpose(mean_a, (1, 0, 2)).reshape(width_a, TERMS * width_a)
    stack_b = jnp.transpose(mean_b, (1, 0, 2)).reshape(width_b, TERMS * width_b)
    points = orbitals.reshape(rows_x * rows_y, width_all)
    weights = potential.reshape(2, TERMS, rows_x * rows_y)
    action = point_action(points, weights, stack_a, stack_b).reshape(rows_x, rows_y, width_all)
    return (kinetic_part.astype(jnp.float32) + action).astype(jnp.bfloat16)


def solution(mesh):
    return jax.shard_map(
        body,
        mesh=mesh,
        in_specs=(
            P(("half", "grp", "tile"), None, None),
            P(("half", "grp", "tile"), None, None, None),
            P(("half", "grp", "tile"), None),
            P(("half", "grp"), "tile", None),
            P(None, None, ("half", "grp"), "tile"),
            P(),
        ),
        out_specs=P(("half", "grp"), "tile", None),
        check_vma=False,
    )
```

profile of v0, /device:TPU:0, one launch (start us, length us, event | category | flops | bytes accessed | tf_op | source)
XLA Modules:
  0.0 330.5 jit_solution(8414382545134291300)
XLA Ops:
  0.0 7.0 %copy.53 = bf16[128,64,256]{0,2,1:T(8,128)(2,1)} copy(bf16[128,64,256]{2,1,0:T(8,128)(2,1)} %param.11) | data formatting | bytes 8388608 | tf_op args[3]
  7.0 7.4 %all-to-all-start = ((bf16[128,8,2048]{0,2,1:T(8,128)(2,1)}), bf16[128,8,2048]{0,2,1:T(8,128)(2,1)}, u32[]{:S(2)}, u32[]{:S(2)}) async-start(bf16[128,8,2048]{0,2,1:T(8,128)(2,1)} %bitcast.84), calls=%async_computation | async-start | bytes 8388608 | tf_op jit(solution)/shard_map/all_to_all | solution.py:64
  17.7 17.9 %while.13 = (s32[]{:T(128)}, f32[8,160,160]{2,1,0:T(8,128)}, f32[8,96,96]{2,1,0:T(8,128)S(1)}, s32[]{:T(128)}, s32[8]{0:T(128)S(1)}, /*index=5*/bf16[1,8,8,8]{3,...) while((s32[]{:T(128)}, f32[8,160,160]{2,1,0:T(8,128)}, ...), condition=%wide.region_2.0_spmd.clone, body=%wide.region_1.0_spmd.clone.sunk | while | flops 65560596 | bytes 4753667 | solution.py:36
  23.3 2.6 multiply_add_fusion.4
  31.9 2.6 multiply_add_fusion.4
  35.6 120.4 %all-reduce.2 = (bf16[8,96,96]{2,1,0:T(8,128)(2,1)}, bf16[8,160,160]{2,1,0:T(8,128)(2,1)}) all-reduce(f32[8,96,96]{2,1,0:T(8,128)S(1)} %get-tuple-element.55, f32[8,160,160]{2,1,0:T(8,128)} %get-tuple-element.54), channel_id=1, replica_groups=mesh['half'=2,'grp'=4,'tile'=4] {'half','grp','tile'}, use_global_device_ids=true, to_apply=%region_5.0 | all-reduce | flops 278528 | bytes 1671168 | tf_op jit(solution)/shard_map/psum | solution.py:74
  156.1 1.5 copy.58
  158.2 1.8 fusion.10
  164.3 6.4 %copy.54 = bf16[8,128,1,2048]{3,1,0,2:T(8,128)(2,1)} copy(bf16[8,128,1,2048]{1,3,0,2:T(8,128)(2,1)} %bitcast.2) | data formatting | bytes 8388608 | tf_op jit(solution)/shard_map/all_to_all | solution.py:64
  170.7 8.2 %convert_bitcast_fusion = bf16[1024,1,2048]{2,0,1:T(8,128)(2,1)} fusion(bf16[1024,1024]{1,0:T(8,128)(2,1)S(1)} %copy-done, bf16[1024,2048]{1,0:T(8,128)(2,1)} %bitcast.85), kind=kOutput, calls=%fused_computation.17 | convolution fusion | flops 4297064448 | bytes 10485760 | tf_op jit(solution)/shard_map/xz,zik->xik/dot_general | solution.py:61
  179.4 6.8 %reduce = bf16[1024,2048]{1,0:T(8,128)(2,1)} reduce(bf16[1024,1,2048]{2,0,1:T(8,128)(2,1)} %convert_bitcast_fusion, bf16[]{:T(256)} %broadcast.13), dimensions={1}, to_apply=%copy.55.reduce_sub_computation | reduce | bytes 8388610 | tf_op jit(solution)/shard_map/convert_element_type | solution.py:67
  186.2 7.8 %reshape.66 = bf16[8,2,131072]{2,1,0:T(2,128)(2,1)} reshape(bf16[1024,2048]{1,0:T(8,128)(2,1)} %reduce) | data formatting | bytes 8388608
  194.0 4.9 %all-to-all-start.1 = ((bf16[8,2,131072]{2,1,0:T(2,128)(2,1)}), bf16[8,2,131072]{2,1,0:T(2,128)(2,1)}, u32[]{:S(2)}, u32[]{:S(2)}) async-start(bf16[8,2,131072]{2,1,0:T(2,128)(2,1)} %reshape.66), calls=%async_computation.1 | async-start | bytes 8388608 | tf_op jit(solution)/shard_map/all_to_all | solution.py:68
  198.9 11.9 %fusion.7 = f32[768,8192]{1,0:T(8,128)} fusion(bf16[96,768]{1,0:T(8,128)(2,1)S(1)} %copy-done.4, bf16[8192,256]{1,0:T(8,128)(2,1)} %bitcast.82), kind=kOutput, calls=%fused_computation.18 | convolution fusion | flops 1207959552 | bytes 27410432 | tf_op jit(solution)/shard_map/dot_general | solution.py:46
  210.8 11.6 %multiply_reduce_fusion.1 = f32[8192,96]{0,1:T(8,128)} fusion(f32[8192,8,96]{0,2,1:T(8,128)} %bitcast.78, f32[8192,8]{0,1:T(8,128)S(1)} %bitcast.87), kind=kLoop, calls=%fused_computation.11 | loop fusion | flops 11796480 | bytes 28573696 | tf_op jit(solution)/shard_map/reduce_sum | solution.py:50
  222.4 18.4 %fusion.5 = f32[1280,8192]{1,0:T(8,128)} fusion(bf16[160,1280]{1,0:T(8,128)(2,1)S(1)} %reshape.55, bf16[8192,256]{1,0:T(8,128)(2,1)} %bitcast.83), kind=kOutput, calls=%fused_computation.15 | convolution fusion | flops 3355443200 | bytes 46546944 | tf_op jit(solution)/shard_map/dot_general | solution.py:43
  240.8 18.2 %multiply_reduce_fusion = f32[8192,160]{0,1:T(8,128)} fusion(f32[8192,8,160]{0,2,1:T(8,128)} %bitcast.77, f32[8192,8]{0,1:T(8,128)S(1)} %bitcast.86), kind=kLoop, calls=%fused_computation.10 | loop fusion | flops 19660800 | bytes 47448064 | tf_op jit(solution)/shard_map/reduce_sum | solution.py:49
  259.0 7.6 %pad_maximum_fusion = f32[8192,256]{0,1:T(8,128)} fusion(f32[8192,96]{0,1:T(8,128)} %multiply_reduce_fusion.1, f32[8192,160]{0,1:T(8,128)} %multiply_reduce_fusion), kind=kLoop, calls=%fused_computation.12 | loop fusion | flops 2097152 | bytes 16777216 | tf_op jit(solution)/shard_map/concatenate | solution.py:51
  266.6 9.0 %copy.62 = f32[8192,256]{1,0:T(8,128)} copy(f32[8192,256]{0,1:T(8,128)} %pad_maximum_fusion) | data formatting | bytes 16777216 | tf_op jit(solution)/shard_map/concatenate | solution.py:51
  275.6 15.8 %all-to-all-done.1 = bf16[8,2,131072]{2,1,0:T(2,128)(2,1)} async-done(((bf16[8,2,131072]{2,1,0:T(2,128)(2,1)}), bf16[8,2,131072]{2,1,0:T(2,128)(2,1)}, u32[]{:S(2)}, u32[]{:S(2)}) %all-to-all-start.1) | async-done | bytes 4194336 | tf_op jit(solution)/shard_map/all_to_all | solution.py:68
  291.4 8.9 %reshape.67 = bf16[1024,1,2048]{2,1,0:T(2,128)(2,1)} reshape(bf16[8,2,131072]{2,1,0:T(2,128)(2,1)} %all-to-all-done.1) | data formatting | bytes 8388608
  300.2 11.5 %copy.66 = f32[8,128,1,2048]{3,0,1,2:T(8,128)} copy(bf16[8,128,1,2048]{3,2,1,0:T(2,128)(2,1)} %bitcast.80) | data formatting | bytes 12582912 | tf_op jit(solution)/shard_map/convert_element_type | solution.py:86
  311.7 9.3 %reshape.61 = f32[128,64,256]{2,1,0:T(8,128)} reshape(f32[128,8,1,2048]{3,1,0,2:T(8,128)} %bitcast.81) | data formatting | bytes 16777216 | tf_op jit(solution)/shard_map/convert_element_type | solution.py:86
  321.0 9.5 %add_convert_fusion = bf16[128,64,256]{2,1,0:T(8,128)(2,1)} fusion(f32[128,64,256]{2,1,0:T(8,128)} %reshape.61, f32[128,64,256]{2,1,0:T(8,128)} %bitcast.79), kind=kLoop, calls=%fused_computation.14 | loop fusion | flops 4194304 | bytes 20971520 | tf_op jit(solution)/shard_map/convert_element_type | solution.py:86
  (44 shorter events, 19.6 us)
Async XLA Ops:
  0.0 170.7 %copy-start = (bf16[1024,1024]{1,0:T(8,128)(2,1)S(1)}, bf16[1024,1024]{1,0:T(8,128)(2,1)}, u32[]{:S(2)}) copy-start(bf16[1024,1024]{1,0:T(8,128)(2,1)} %param.13) | copy-start | bytes 6291460
  7.0 7.4 %copy-start.2 = (bf16[8,96,160]{1,2,0:T(8,128)(2,1)S(1)}, bf16[8,96,160]{1,2,0:T(8,128)(2,1)}, u32[]{:S(2)}) copy-start(bf16[8,96,160]{1,2,0:T(8,128)(2,1)} %param.8) | copy-start | bytes 737284
  7.0 8.9 %copy-start.5 = (s32[1,8]{1,0:T(1,128)S(1)}, s32[1,8]{1,0:T(1,128)}, u32[]{:S(2)}) copy-start(s32[1,8]{1,0:T(1,128)} %param.10) | copy-start | bytes 100
  7.0 157.3 %all-to-all-start = ((bf16[128,8,2048]{0,2,1:T(8,128)(2,1)}), bf16[128,8,2048]{0,2,1:T(8,128)(2,1)}, u32[]{:S(2)}, u32[]{:S(2)}) async-start(bf16[128,8,2048]{0,2,1:T(8,128)(2,1)} %bitcast.84), calls=%async_computation | async-start | bytes 8388608 | tf_op jit(solution)/shard_map/all_to_all | solution.py:64
  194.0 4.9 %copy-start.4 = (bf16[96,768]{1,0:T(8,128)(2,1)S(1)}, bf16[96,768]{1,0:T(8,128)(2,1)}, u32[]{:S(2)}) copy-start(bf16[96,768]{1,0:T(8,128)(2,1)} %reshape.58) | copy-start | bytes 442372
  194.0 97.4 %all-to-all-start.1 = ((bf16[8,2,131072]{2,1,0:T(2,128)(2,1)}), bf16[8,2,131072]{2,1,0:T(2,128)(2,1)}, u32[]{:S(2)}, u32[]{:S(2)}) async-start(bf16[8,2,131072]{2,1,0:T(2,128)(2,1)} %reshape.66), calls=%async_computation.1 | async-start | bytes 8388608 | tf_op jit(solution)/shard_map/all_to_all | solution.py:68
  198.9 11.9 %copy-start.3 = (f32[8,8192]{1,0:T(8,128)S(1)}, f32[8,8192]{1,0:T(8,128)}, u32[]{:S(2)}) copy-start(f32[8,8192]{1,0:T(8,128)} %squeeze.17) | copy-start | bytes 786436
  321.0 9.5 %copy-start.1 = (bf16[1024,1024]{1,0:T(8,128)(2,1)S(1)}, bf16[1024,1024]{1,0:T(8,128)(2,1)}, u32[]{:S(2)}) copy-start(bf16[1024,1024]{1,0:T(8,128)(2,1)} %param.13) | copy-start | bytes 6291460
where the time goes:
time: 333 us; the launch traced here: 330 us
  blocking collectives  120 us (36%)
  local copies, waits for them, and re-layouts  75.6 us (23%)
  other arithmetic  61 us (18%)
  matrix products  43.4 us (13%)
  waiting for transfers between devices  15.8 us (5%)
  starting transfers between devices  12.3 us (4%)
    psum x1, blocking collectives, body(): total_a, total_b = lax.psum((sum_a, sum_b), ('half', 'grp', 'tile'))  120 us
    unnamed x16, local copies, waits for them, and re-layouts  23.9 us
    convert_element_type x2, local copies, waits for them, and re-layouts, body(): return (kinetic_part.astype(jnp.float32) + action).astype(jnp.bfloat16)  20.7 us
    dot_general x1, matrix products, point_action(): jnp.dot(points[:, :width_a], stack_a, preferred_element_type=jnp.float32)  18.4 us
    reduce_sum x1, other arithmetic, point_action(): act_a = jnp.sum(prod_a * weights[0].T[:, :, None], axis=1)  18.2 us
    all_to_all x1, waiting for transfers between devices, kinetic_columns(): lax.all_to_all(applied, ('half', 'grp'), split_axis=0, concat_axis=1, til...  15.8 us
    dot_general x1, matrix products, point_action(): jnp.dot(points[:, width_a:], stack_b, preferred_element_type=jnp.float32)  11.9 us
    reduce_sum x1, other arithmetic, point_action(): act_b = jnp.sum(prod_b * weights[1].T[:, :, None], axis=1)  11.6 us
  transfers between devices with their start and end apart: 2, of which 1 were waited for; matrix products, arithmetic and copies ran while one was open for 32% of the time, Pallas kernels for 0%

commit v1 on v0

v1 whole, which is shorter than its diff:
```python
import functools

import jax
import jax.numpy as jnp
from jax import lax
from jax.experimental import pallas as pl
from jax.experimental.pallas import tpu as pltpu
from jax.sharding import PartitionSpec as P


TERMS = 8
GROUP = ("half", "grp")
SIDE = 16
BF = jnp.bfloat16
F32 = jnp.float32


def slot_sums(core_tensor, term_operators, block_terms):
    rows_tile, width_b, width_a = core_tensor.shape
    flat_core = core_tensor.reshape(rows_tile, width_b * width_a)
    listed = block_terms[0]
    live_slots = jnp.sum((listed < TERMS).astype(jnp.int32))
    labels = jnp.arange(TERMS, dtype=jnp.int32)

    def add_slot(slot_index, running):
        sum_a, sum_b = running
        operator = term_operators[0, slot_index]
        mixed_core = jnp.einsum("rs,rq->sq", operator, flat_core, preferred_element_type=F32)
        mixed_core = mixed_core.astype(BF).reshape(rows_tile, width_b, width_a)
        gram_a = jnp.einsum("rba,rbc->ac", core_tensor, mixed_core, preferred_element_type=F32)
        gram_b = jnp.einsum("rba,rda->bd", core_tensor, mixed_core, preferred_element_type=F32)
        chosen = (labels == listed[slot_index]).astype(F32)
        return (sum_a + chosen[:, None, None] * gram_a, sum_b + chosen[:, None, None] * gram_b)

    start_sums = (
        jnp.zeros((TERMS, width_a, width_a), F32),
        jnp.zeros((TERMS, width_b, width_b), F32),
    )
    return lax.fori_loop(0, live_slots, add_slot, start_sums)


def point_action(points, weights, stack_a, stack_b):
    width_a = stack_a.shape[0]
    width_b = stack_b.shape[0]
    count_points = points.shape[0]
    prod_a = jnp.dot(points[:, :width_a], stack_a, preferred_element_type=F32).reshape(
        count_points, TERMS, width_a
    )
    prod_b = jnp.dot(points[:, width_a:], stack_b, preferred_element_type=F32).reshape(
        count_points, TERMS, width_b
    )
    act_a = jnp.sum(prod_a * weights[0].T[:, :, None], axis=1)
    act_b = jnp.sum(prod_b * weights[1].T[:, :, None], axis=1)
    return jnp.concatenate([act_a, act_b], axis=1)


def kinetic_columns(kinetic, orbitals):
    rows_x, rows_y, width_all = orbitals.shape
    groups = lax.axis_size("half") * lax.axis_size("grp")
    columns = rows_y * width_all // groups
    pieces = orbitals.reshape(rows_x, groups, columns)
    applied = jnp.einsum(
        "xz,zik->xik",
        kinetic,
        lax.all_to_all(pieces, GROUP, split_axis=1, concat_axis=0, tiled=True),
        preferred_element_type=F32,
    )
    applied = applied.astype(BF)
    returned = lax.all_to_all(applied, GROUP, split_axis=0, concat_axis=1, tiled=True)
    return returned.reshape(rows_x, rows_y, width_all)


def plain_body(core_tensor, term_operators, block_terms, orbitals, potential, kinetic):
    sum_a, sum_b = slot_sums(core_tensor, term_operators, block_terms)
    total_a, total_b = lax.psum((sum_a, sum_b), ("half", "grp", "tile"))
    mean_a = total_a.astype(BF)
    mean_b = total_b.astype(BF)
    kinetic_part = kinetic_columns(kinetic, orbitals)
    rows_x, rows_y, width_all = orbitals.shape
    width_a = mean_a.shape[1]
    width_b = mean_b.shape[1]
    stack_a = jnp.transpose(mean_a, (1, 0, 2)).reshape(width_a, TERMS * width_a)
    stack_b = jnp.transpose(mean_b, (1, 0, 2)).reshape(width_b, TERMS * width_b)
    points = orbitals.reshape(rows_x * rows_y, width_all)
    weights = potential.reshape(2, TERMS, rows_x * rows_y)
    action = point_action(points, weights, stack_a, stack_b).reshape(rows_x, rows_y, width_all)
    return (kinetic_part.astype(F32) + action).astype(BF)


VMEM = pl.BlockSpec(memory_space=pltpu.VMEM)
SMEM = pl.BlockSpec(memory_space=pltpu.SMEM)


def swap_matrix():
    count = SIDE * SIDE
    row = lax.broadcasted_iota(jnp.int32, (count, count), 0)
    col = lax.broadcasted_iota(jnp.int32, (count, count), 1)
    hit = (row // SIDE == col % SIDE) & (row % SIDE == col // SIDE)
    return jnp.where(hit, 1.0, 0.0).astype(BF)


def slot_kernel(terms_ref, oper_ref, core_ref, out_ref, core_f, core_t, core_p, mixed):
    rows, width_b, width_a = core_ref.shape
    width = out_ref.shape[2]
    slots = terms_ref.shape[1]
    out_ref[...] = jnp.zeros_like(out_ref)
    mixed[...] = jnp.zeros_like(mixed)
    core_p[...] = jnp.zeros_like(core_p)
    core_p[:, :, :width_a] = core_ref[...]
    core_f[...] = core_p[...].astype(F32)
    core_t[...] = jnp.transpose(core_f[...].reshape(rows * width_b, width)).astype(BF)
    live = jnp.int32(0)
    for slot in range(slots):
        live = live + (terms_ref[0, slot] < TERMS).astype(jnp.int32)

    def one_slot(slot, carry):
        def one_block(block, inner):
            start = pl.multiple_of(block * 16, 16)
            source = [core_f[r, pl.ds(start, 16), :] for r in range(rows)]
            for q in range(rows):
                total = source[0] * oper_ref[slot, q]
                for r in range(1, rows):
                    total = total + source[r] * oper_ref[slot, r * rows + q]
                mixed[q, pl.ds(width_a + start, 16), :] = total.astype(BF)
            return inner

        lax.fori_loop(0, width_b // 16, one_block, 0)
        flat = mixed[:, width_a:, :].reshape(rows * width_b, width)
        gram_a = jnp.dot(core_t[:width_a, :], flat, preferred_element_type=F32)
        gram_b = jnp.zeros((width_b, width), F32)
        for q in range(rows):
            gram_b = gram_b + lax.dot_general(
                core_p[q], mixed[q], (((1,), (1,)), ((), ())), preferred_element_type=F32
            )
        term = terms_ref[0, slot]
        out_ref[term, :width_b, :] = (gram_a[:width_b] + gram_b).astype(BF)
        out_ref[term, width_b:, :] = gram_a[width_b:].astype(BF)
        return carry

    lax.fori_loop(0, live, one_slot, 0)


def tile_mean_fields(core_tensor, term_operators, block_terms):
    rows, width_b, width_a = core_tensor.shape
    slots = block_terms.shape[1]
    width = width_a + width_b
    operators = term_operators.astype(F32).reshape(slots, rows * rows)
    return pl.pallas_call(
        slot_kernel,
        out_shape=jax.ShapeDtypeStruct((TERMS, width_a, width), BF),
        in_specs=[SMEM, SMEM, VMEM],
        out_specs=VMEM,
        scratch_shapes=[
            pltpu.VMEM((rows, width_b, width), F32),
            pltpu.VMEM((width, rows * width_b), BF),
            pltpu.VMEM((rows, width_b, width), BF),
            pltpu.VMEM((rows, width, width), BF),
        ],
        cost_estimate=pl.CostEstimate(flops=10**9, bytes_accessed=2 * 10**6, transcendentals=0),
        name="slot_sums",
    )(block_terms, operators, core_tensor)


def exchange(array, axes, flip):
    count = lax.axis_size(axes)
    return lax.ppermute(array, axes, [(i, i ^ flip) for i in range(count)])


def scatter_sum(array, axes, place, flips):
    rows = array.shape[0] // (len(flips) + 1)

    def block(index):
        return lax.dynamic_slice_in_dim(array, index * rows, rows, 0)

    arrived = [exchange(block(place ^ own), axes, flip) for flip, own in flips]
    total = block(place).astype(F32)
    for part in arrived:
        total = total + part.astype(F32)
    return total.astype(BF)


def gather_blocks(array, axes, place, flips):
    rows = array.shape[0]
    whole = jnp.zeros((rows * (len(flips) + 1),) + array.shape[1:], array.dtype)
    arrived = [(own, exchange(array, axes, flip)) for flip, own in flips]
    whole = lax.dynamic_update_slice_in_dim(whole, array, place * rows, 0)
    for own, part in arrived:
        whole = lax.dynamic_update_slice_in_dim(whole, part, (place ^ own) * rows, 0)
    return whole


def bit_flips(bits):
    flips = []
    for own in range(1, 1 << len(bits)):
        flip = sum(1 << bit for at, bit in enumerate(bits) if own >> at & 1)
        flips.append((flip, own))
    return flips


def place_of(index, bits):
    place = jnp.int32(0)
    for at, bit in enumerate(bits):
        place = place | (((index >> bit) & 1) << at)
    return place


def total_mean_fields(partial):
    terms, width_a, width = partial.shape
    group_index = lax.axis_index(GROUP)
    tile_index = lax.axis_index("tile")
    tile_bits = list(range(lax.axis_size("tile").bit_length() - 1))
    group_bits = list(range(lax.axis_size(GROUP).bit_length() - 1))
    far = lax.axis_size("grp").bit_length() - 2
    stages = [("tile", tile_index, tile_bits)]
    stages.append((GROUP, group_index, [bit for bit in group_bits if bit != far]))
    stages.append((GROUP, group_index, [far]))
    array = partial.reshape(terms * width_a, width)
    for axes, index, bits in stages:
        array = scatter_sum(array, axes, place_of(index, bits), bit_flips(bits))
    for axes, index, bits in reversed(stages):
        array = gather_blocks(array, axes, place_of(index, bits), bit_flips(bits))
    return array.reshape(terms, width_a, width)


def action_kernel(points_ref, weight_ref, mean_ref, out_ref, blocks):
    width_a = mean_ref.shape[1]
    rows, width = points_ref.shape
    width_b = width - width_a

    @pl.when(pl.program_id(0) == 0)
    def _():
        lane = lax.broadcasted_iota(jnp.int32, (width_a, width), 1)
        for term in range(TERMS):
            packed = mean_ref[term].astype(F32)
            blocks[term, :width_a, :] = jnp.where(lane < width_a, packed, 0.0).astype(BF)
            blocks[term, width_a:, :] = jnp.where(
                lane[:width_b] < width_a, 0.0, packed[:width_b]
            ).astype(BF)

    step = 256
    for start in range(0, rows, step):
        points = points_ref[start : start + step, :]
        lane = lax.broadcasted_iota(jnp.int32, (step, width), 1)
        total = jnp.zeros((step, width), F32)
        for term in range(TERMS):
            prod = jnp.dot(points, blocks[term], preferred_element_type=F32)
            on_a = weight_ref[start : start + step, term : term + 1]
            on_b = weight_ref[start : start + step, TERMS + term : TERMS + term + 1]
            weight = jnp.where(lane < width_a, on_a, on_b)
            total = total + prod * weight
        out_ref[start : start + step, :] = total


def action_of(orbitals, potential, mean):
    rows_x, rows_y, width = orbitals.shape
    count = rows_x * rows_y
    points = orbitals.reshape(count, width)
    weights = potential.reshape(2 * TERMS, count).T
    step = 512
    action = pl.pallas_call(
        action_kernel,
        grid=(count // step,),
        out_shape=jax.ShapeDtypeStruct((count, width), F32),
        in_specs=[
            pl.BlockSpec((step, width), lambda i: (i, 0)),
            pl.BlockSpec((step, 2 * TERMS), lambda i: (i, 0)),
            pl.BlockSpec(mean.shape, lambda i: (0, 0, 0)),
        ],
        out_specs=pl.BlockSpec((step, width), lambda i: (i, 0)),
        scratch_shapes=[pltpu.VMEM((TERMS, width, width), BF)],
        cost_estimate=pl.CostEstimate(
            flops=2 * count * width * width * TERMS, bytes_accessed=2 * 10**7, transcendentals=0
        ),
        name="action",
    )(points, weights, mean)
    return action.reshape(rows_x, rows_y, width)


def split_kernel(groups, me_ref, orb_ref, *refs):
    outs, rows = refs[:groups], refs[groups]
    rows_x, chunk, width = orb_ref.shape
    per = chunk // groups
    swap = swap_matrix()
    for start in range(0, rows_x, SIDE):
        block = orb_ref[start : start + SIDE].reshape(SIDE * SIDE, width)
        turned = jnp.dot(swap, block, preferred_element_type=F32).astype(BF)
        rows[:, start : start + SIDE, :] = turned.reshape(SIDE, SIDE, width)
    me = me_ref[0]
    for flip in range(groups):
        outs[flip][...] = rows[pl.ds((me ^ flip) * per, per)]


def split_chunk(me, orbitals, chunk_index, chunk, groups):
    rows_x, _, width = orbitals.shape
    piece = (chunk // groups, rows_x, width)
    return pl.pallas_call(
        functools.partial(split_kernel, groups),
        grid=(1,),
        out_shape=[jax.ShapeDtypeStruct(piece, BF)] * groups,
        in_specs=[SMEM, pl.BlockSpec((rows_x, chunk, width), lambda i: (0, chunk_index, 0))],
        out_specs=[pl.BlockSpec(piece, lambda i: (0, 0, 0))] * groups,
        scratch_shapes=[pltpu.VMEM((chunk, rows_x, width), BF)],
        cost_estimate=pl.CostEstimate(
            flops=2 * rows_x * chunk * width * SIDE * SIDE,
            bytes_accessed=4 * rows_x * chunk * width,
            transcendentals=0,
        ),
        name="split",
    )(me, orbitals)


def apply_kernel(groups, me_ref, kin_ref, *refs):
    pieces, outs = refs[:groups], refs[groups : 2 * groups]
    gathered, result = refs[2 * groups :]
    per, rows_x, _ = pieces[0].shape
    size_x = kin_ref.shape[0]
    me = me_ref[0]
    step = 256
    for row in range(per):
        for flip in range(groups):
            start = pl.multiple_of((me ^ flip) * rows_x, rows_x)
            gathered[row, pl.ds(start, rows_x), :] = pieces[flip][row]
        for start in range(0, size_x, step):
            applied = jnp.dot(
                kin_ref[start : start + step, :], gathered[row], preferred_element_type=F32
            )
            result[row, start : start + step, :] = applied.astype(BF)
        for flip in range(groups):
            start = pl.multiple_of((me ^ flip) * rows_x, rows_x)
            outs[flip][row] = result[row, pl.ds(start, rows_x), :]


def apply_chunk(me, kinetic, pieces):
    groups = len(pieces)
    per, rows_x, width = pieces[0].shape
    size_x = kinetic.shape[0]
    return pl.pallas_call(
        functools.partial(apply_kernel, groups),
        out_shape=[jax.ShapeDtypeStruct((per, rows_x, width), BF)] * groups,
        in_specs=[SMEM, VMEM] + [VMEM] * groups,
        out_specs=[VMEM] * groups,
        scratch_shapes=[pltpu.VMEM((per, size_x, width), BF)] * 2,
        cost_estimate=pl.CostEstimate(
            flops=2 * size_x * size_x * per * width, bytes_accessed=4 * 10**6, transcendentals=0
        ),
        name="apply",
    )(me, kinetic, *pieces)


def join_kernel(groups, me_ref, action_ref, *refs):
    pieces = refs[:groups]
    out_ref, rows = refs[-2:]
    per = pieces[0].shape[0]
    step_x, _, width = out_ref.shape
    me = me_ref[0]
    for flip in range(groups):
        rows[pl.ds((me ^ flip) * per, per)] = pieces[flip][...]
    swap = swap_matrix()
    for start in range(0, step_x, SIDE):
        block = rows[:, start : start + SIDE, :].reshape(SIDE * SIDE, width)
        turned = jnp.dot(swap, block, preferred_element_type=F32).reshape(SIDE, SIDE, width)
        out_ref[start : start + SIDE] = (turned + action_ref[start : start + SIDE]).astype(BF)


def join_chunk(me, action, pieces, chunk_index, before):
    groups = len(pieces)
    per, rows_x, width = pieces[0].shape
    chunk = per * groups
    rows_y = action.shape[1]
    step_x = 32
    first = before is None
    block = pl.BlockSpec((step_x, chunk, width), lambda i: (i, chunk_index, 0))
    in_specs = [SMEM, block] + [pl.BlockSpec((per, step_x, width), lambda i: (0, i, 0))] * groups
    operands = [me, action, *pieces]
    aliases = {}
    if not first:
        in_specs.append(pl.BlockSpec(memory_space=pl.ANY))
        aliases = {len(operands): 0}
        operands.append(before)
    return pl.pallas_call(
        functools.partial(join_kernel, groups),
        grid=(rows_x // step_x,),
        out_shape=jax.ShapeDtypeStruct((rows_x, rows_y, width), BF),
        in_specs=in_specs,
        out_specs=block,
        scratch_shapes=[pltpu.VMEM((chunk, step_x, width), BF)],
        input_output_aliases=aliases,
        cost_estimate=pl.CostEstimate(
            flops=2 * rows_x * chunk * width * SIDE * SIDE,
            bytes_accessed=8 * rows_x * chunk * width,
            transcendentals=0,
        ),
        name="join",
    )(*operands)


def exchange_all(pieces):
    groups = len(pieces)
    far = lax.axis_size("grp") // 2
    order = sorted(range(1, groups), key=lambda flip: (flip & far == 0, flip))
    arrived = list(pieces)
    for flip in order:
        arrived[flip] = exchange(pieces[flip], GROUP, flip)
    return arrived


def chunked_body(core_tensor, term_operators, block_terms, orbitals, potential, kinetic):
    _, rows_y, _ = orbitals.shape
    groups = lax.axis_size(GROUP)
    chunk = SIDE
    chunks = rows_y // chunk
    me = lax.axis_index(GROUP).astype(jnp.int32).reshape(1)
    returned = []
    for index in range(chunks):
        pieces = split_chunk(me, orbitals, index, chunk, groups)
        pieces = exchange_all(pieces)
        pieces = apply_chunk(me, kinetic, pieces)
        returned.append(exchange_all(pieces))
    partial = tile_mean_fields(core_tensor, term_operators, block_terms)
    mean = total_mean_fields(partial)
    action = action_of(orbitals, potential, mean)
    result = None
    for index in range(chunks):
        result = join_chunk(me, action, returned[index], index, result)
    return result


def fits(core_tensor, orbitals, mesh):
    rows_x, rows_y, width = orbitals
    groups = mesh.shape["half"] * mesh.shape["grp"]
    tiles = mesh.shape["tile"]
    _, width_b, width_a = core_tensor
    return (
        mesh.shape["half"] == 2
        and mesh.shape["grp"] >= 2
        and groups & (groups - 1) == 0
        and tiles & (tiles - 1) == 0
        and tiles > 1
        and SIDE % groups == 0
        and rows_y % SIDE == 0
        and rows_x % 128 == 0
        and width == width_a + width_b
        and width % 256 == 0
        and width_b % 16 == 0
        and width_a % 16 == 0
        and width_b <= width_a
        and TERMS * width_a % (groups * tiles * 8) == 0
    )


def solution(mesh):
    specs = (
        P(("half", "grp", "tile"), None, None),
        P(("half", "grp", "tile"), None, None, None),
        P(("half", "grp", "tile"), None),
        P(("half", "grp"), "tile", None),
        P(None, None, ("half", "grp"), "tile"),
        P(),
    )

    def build(body):
        return jax.shard_map(body, mesh=mesh, in_specs=specs, out_specs=specs[3], check_vma=False)

    def whole(core_tensor, term_operators, block_terms, orbitals, potential, kinetic):
        args = (core_tensor, term_operators, block_terms, orbitals, potential, kinetic)
        size_x, size_y, width = orbitals.shape
        rows_x = size_x // (mesh.shape["half"] * mesh.shape["grp"])
        rows_y = size_y // mesh.shape["tile"]
        if not fits(core_tensor.shape, (rows_x, rows_y, width), mesh):
            return build(plain_body)(*args)
        return build(chunked_body)(*args)

    return whole
```

time: 333 us -> 253 us (0.76)
  blocking collectives: 120 us -> 0 us
  starting transfers between devices: 12.3 us -> 129 us
  Pallas kernels: 0 us -> 71.3 us
  local copies, waits for them, and re-layouts: 75.6 us -> 7.54 us
  other arithmetic: 61 us -> 1.03 us
  matrix products: 43.4 us -> 0 us
  waiting for transfers between devices: 15.8 us -> 41.7 us
    ppermute x0 -> x70, starting transfers between devices: none -> 129 us  [exchange(): return lax.ppermute(array, axes, [(i, i ^ flip) for i in range(count)])]
    psum x1 -> x0, blocking collectives: 120 us -> none  [body(): total_a, total_b = lax.psum((sum_a, sum_b), ('half', 'grp', 'tile'))]
    pallas_call x0 -> x14, Pallas kernels: none -> 71.3 us  [the longest x1 22.7 us: action_of(): pl.pallas_call(action_kernel, grid=(count // step,), out_shape=jax.ShapeD...]
    dot_general x9 -> x0, matrix products: 43.4 us -> none  [the longest x1 18.4 us: point_action(): jnp.dot(points[:, :width_a], stack_a, preferred_element_type=jnp.float32)]
    ppermute x0 -> x70, waiting for transfers between devices: none -> 41.7 us  [exchange(): return lax.ppermute(array, axes, [(i, i ^ flip) for i in range(count)])]
    reduce_sum x3 -> x0, other arithmetic: 30.4 us -> none  [the longest x1 18.2 us: point_action(): act_a = jnp.sum(prod_a * weights[0].T[:, :, None], axis=1)]
    unnamed x16 -> x150, local copies, waits for them, and re-layouts: 23.9 us -> 2.38 us
    convert_element_type x3 -> x0, local copies, waits for them, and re-layouts: 21.3 us -> none  [the longest x2 20.7 us: body(): return (kinetic_part.astype(jnp.float32) + action).astype(jnp.bfloat16)]
  transfers between devices with their start and end apart: 2 -> 70, of which waited for: 1 -> 13; matrix products, arithmetic and copies ran while one was open for 32% -> 3% of each run, Pallas kernels for 0% -> 26%
where the time goes in v1:
time: 253 us; the launch traced here: 251 us
  starting transfers between devices  129 us (51%)
  Pallas kernels  71.3 us (28%)
  waiting for transfers between devices  41.7 us (16%)
  local copies, waits for them, and re-layouts  7.54 us (3%)
    ppermute x70, starting transfers between devices, exchange(): return lax.ppermute(array, axes, [(i, i ^ flip) for i in range(count)])  129 us
    ppermute x70, waiting for transfers between devices, exchange(): return lax.ppermute(array, axes, [(i, i ^ flip) for i in range(count)])  41.7 us
    pallas_call x1, Pallas kernels, action_of(): pl.pallas_call(action_kernel, grid=(count // step,), out_shape=jax.ShapeD...  22.7 us
    pallas_call x4, Pallas kernels, apply_chunk(): pl.pallas_call(functools.partial(apply_kernel, groups), out_shape=[jax.Sh...  17.1 us
    pallas_call x4, Pallas kernels, join_chunk(): pl.pallas_call(functools.partial(join_kernel, groups), grid=(rows_x // st...  16.4 us
    pallas_call x4, Pallas kernels, split_chunk(): pl.pallas_call(functools.partial(split_kernel, groups), grid=(1,), out_sh...  10.9 us
  transfers between devices with their start and end apart: 70, of which 13 were waited for; matrix products, arithmetic and copies ran while one was open for 3% of the time, Pallas kernels for 26%

profile of v1, /device:TPU:0, one launch (start us, length us, event | category | flops | bytes accessed | tf_op | source)
XLA Modules:
  0.0 251.2 jit_solution(15214596146030955127)
XLA Ops:
  10.0 4.2 %slot_sums.1 = bf16[8,160,256]{2,1,0:T(8,128)(2,1)} custom-call(s32[1,8]{1,0:T(1,128)} %terms_ref.1, f32[8,64]{1,0:T(8,128)} %reshape.32.oper_ref, bf16[8,96,160]{2,1,0:T(8,128)(2,1)} %copy.14.core_ref), custom_call_target="tpu_custom_call" | custom-call | flops 1000000000 | bytes 2000000 | tf_op jit(solution)/shard_map/slot_sums/pallas_call | solution.py:148
  15.5 5.6 %collective-permute-start.1 = (bf16[320,256]{1,0:T(8,128)(2,1)S(1)}, bf16[320,256]{1,0:T(8,128)(2,1)S(1)}, u32[]{:S(2)}, u32[]{:S(2)}) collective-permute-start(bf16[320,256]{1,0:T(8,128)(2,1)S(1)} %get-tuple-element.137), channel_id=1, source_target_pairs={{0,2},{1,3},{2,0},{3,1},{4,6},{5,7},{6,4},{7,5},{8,10},{9,11},{10,... | collective-permute-start | bytes 491528 | tf_op jit(solution)/shard_map/ppermute | solution.py:166
  39.9 4.4 %collective-permute-done.61.refs_6_ = bf16[2,128,256]{2,1,0:T(8,128)(2,1)S(1)} collective-permute-done((bf16[2,128,256]{2,1,0:T(8,128)(2,1)S(1)}, bf16[2,128,256]{2,1,0:T(8,128)(2,1)S(1)}, u32[]{:S(2)}, u32[]{:S(2)}) %collective-permute-start.61) | collective-permute-done | bytes 131104 | tf_op jit(solution)/shard_map/ppermute | solution.py:166
  46.5 6.7 %collective-permute-start.3 = (bf16[80,256]{1,0:T(8,128)(2,1)S(1)}, bf16[80,256]{1,0:T(8,128)(2,1)S(1)}, u32[]{:S(2)}, u32[]{:S(2)}) collective-permute-start(bf16[80,256]{1,0:T(8,128)(2,1)S(1)} %get-tuple-element.138), channel_id=1, source_target_pairs={{0,4},{4,0},{8,12},{12,8},{16,20},{20,16},{24,28},{28,24},{1,5},{5... | collective-permute-start | bytes 122888 | tf_op jit(solution)/shard_map/ppermute | solution.py:166
  71.5 6.7 %collective-permute-done.47.refs_6_ = bf16[2,128,256]{2,1,0:T(8,128)(2,1)S(1)} collective-permute-done((bf16[2,128,256]{2,1,0:T(8,128)(2,1)S(1)}, bf16[2,128,256]{2,1,0:T(8,128)(2,1)S(1)}, u32[]{:S(2)}, u32[]{:S(2)}) %collective-permute-start.47) | collective-permute-done | bytes 131104 | tf_op jit(solution)/shard_map/ppermute | solution.py:166
  78.5 6.5 %collective-permute-start.32 = (bf16[2,128,256]{2,1,0:T(8,128)(2,1)S(1)}, bf16[2,128,256]{2,1,0:T(8,128)(2,1)S(1)}, u32[]{:S(2)}, u32[]{:S(2)}) collective-permute-start(bf16[2,128,256]{2,1,0:T(8,128)(2,1)S(1)} %copy-done.72), channel_id=1, source_target_pairs={{0,20},{4,16},{8,28},{12,24},{16,4},{20,0},{24,12},{28,8},{1,21},{... | collective-permute-start | bytes 393224 | tf_op jit(solution)/shard_map/ppermute | solution.py:166
  89.5 4.3 %apply.7 = (bf16[2,128,256]{2,1,0:T(8,128)(2,1)}, bf16[2,128,256]{2,1,0:T(8,128)(2,1)}, bf16[2,128,256]{2,1,0:T(8,128)(2,1)}, bf16[2,128,256]{2,1,0:T(8,128)(2,1...) custom-call(s32[1]{0:T(128)} %bitcast.me_ref, ...), custom_call_target="tpu_custom_call" | custom-call | flops 1073741824 | bytes 4000000 | tf_op jit(solution)/shard_map/apply/pallas_call | solution.py:337
  102.8 5.8 %collective-permute-start.18 = (bf16[2,128,256]{2,1,0:T(8,128)(2,1)S(1)}, bf16[2,128,256]{2,1,0:T(8,128)(2,1)S(1)}, u32[]{:S(2)}, u32[]{:S(2)}) collective-permute-start(bf16[2,128,256]{2,1,0:T(8,128)(2,1)S(1)} %copy-done.55), channel_id=1, source_target_pairs={{0,20},{4,16},{8,28},{12,24},{16,4},{20,0},{24,12},{28,8},{1,21},{... | collective-permute-start | bytes 393224 | tf_op jit(solution)/shard_map/ppermute | solution.py:166
  113.9 4.3 %apply.6 = (bf16[2,128,256]{2,1,0:T(8,128)(2,1)}, bf16[2,128,256]{2,1,0:T(8,128)(2,1)}, bf16[2,128,256]{2,1,0:T(8,128)(2,1)}, bf16[2,128,256]{2,1,0:T(8,128)(2,1...) custom-call(s32[1]{0:T(128)} %bitcast.me_ref, ...), custom_call_target="tpu_custom_call" | custom-call | flops 1073741824 | bytes 4000000 | tf_op jit(solution)/shard_map/apply/pallas_call | solution.py:337
  124.1 3.3 %collective-permute-done.20.refs_7_ = bf16[2,128,256]{2,1,0:T(8,128)(2,1)S(1)} collective-permute-done((bf16[2,128,256]{2,1,0:T(8,128)(2,1)S(1)}, bf16[2,128,256]{2,1,0:T(8,128)(2,1)S(1)}, u32[]{:S(2)}, u32[]{:S(2)}) %collective-permute-start.20) | collective-permute-done | bytes 131104 | tf_op jit(solution)/shard_map/ppermute | solution.py:166
  127.5 3.8 %collective-permute-start.67 = (bf16[2,128,256]{2,1,0:T(8,128)(2,1)S(1)}, bf16[2,128,256]{2,1,0:T(8,128)(2,1)S(1)}, u32[]{:S(2)}, u32[]{:S(2)}) collective-permute-start(bf16[2,128,256]{2,1,0:T(8,128)(2,1)S(1)} %copy-done.57), channel_id=1, source_target_pairs={{0,20},{4,16},{8,28},{12,24},{16,4},{20,0},{24,12},{28,8},{1,21},{... | collective-permute-start | bytes 393224 | tf_op jit(solution)/shard_map/ppermute | solution.py:166
  131.2 5.7 %collective-permute-done.64.refs_2_ = bf16[2,128,256]{2,1,0:T(8,128)(2,1)S(1)} collective-permute-done((bf16[2,128,256]{2,1,0:T(8,128)(2,1)}, bf16[2,128,256]{2,1,0:T(8,128)(2,1)S(1)}, u32[]{:S(2)}, u32[]{:S(2)}) %collective-permute-start.64) | collective-permute-done | bytes 131104 | tf_op jit(solution)/shard_map/ppermute | solution.py:166
  141.1 3.7 %collective-permute-start.10 = (bf16[80,256]{1,0:T(8,128)(2,1)S(1)}, bf16[80,256]{1,0:T(8,128)(2,1)S(1)}, u32[]{:S(2)}, u32[]{:S(2)}) collective-permute-start(bf16[80,256]{1,0:T(8,128)(2,1)S(1)} %constant_dynamic-update-slice_fusion.8), channel_id=1, source_target_pairs={{0,20},{4,16},{8,28},{12,24},{16,4},{20,0},{24,12},{28,8},{1,21},{... | collective-permute-start | bytes 122888 | tf_op jit(solution)/shard_map/ppermute | solution.py:166
  153.3 4.3 %apply.5 = (bf16[2,128,256]{2,1,0:T(8,128)(2,1)}, bf16[2,128,256]{2,1,0:T(8,128)(2,1)}, bf16[2,128,256]{2,1,0:T(8,128)(2,1)}, bf16[2,128,256]{2,1,0:T(8,128)(2,1...) custom-call(s32[1]{0:T(128)} %bitcast.me_ref, ...), custom_call_target="tpu_custom_call" | custom-call | flops 1073741824 | bytes 4000000 | tf_op jit(solution)/shard_map/apply/pallas_call | solution.py:337
  167.2 4.3 %apply.4 = (bf16[2,128,256]{2,1,0:T(8,128)(2,1)}, bf16[2,128,256]{2,1,0:T(8,128)(2,1)}, bf16[2,128,256]{2,1,0:T(8,128)(2,1)}, bf16[2,128,256]{2,1,0:T(8,128)(2,1...) custom-call(s32[1]{0:T(128)} %bitcast.me_ref, ...), custom_call_target="tpu_custom_call" | custom-call | flops 1073741824 | bytes 4000000 | tf_op jit(solution)/shard_map/apply/pallas_call | solution.py:337
  177.3 7.0 %collective-permute-done.36.refs_2_ = bf16[2,128,256]{2,1,0:T(8,128)(2,1)S(1)} collective-permute-done((bf16[2,128,256]{2,1,0:T(8,128)(2,1)}, bf16[2,128,256]{2,1,0:T(8,128)(2,1)S(1)}, u32[]{:S(2)}, u32[]{:S(2)}) %collective-permute-start.36) | collective-permute-done | bytes 131104 | tf_op jit(solution)/shard_map/ppermute | solution.py:166
  184.4 3.7 %collective-permute-start.40 = (bf16[2,128,256]{2,1,0:T(8,128)(2,1)}, bf16[2,128,256]{2,1,0:T(8,128)(2,1)S(1)}, u32[]{:S(2)}, u32[]{:S(2)}) collective-permute-start(bf16[2,128,256]{2,1,0:T(8,128)(2,1)} %get-tuple-element.99), channel_id=1, source_target_pairs={{0,24},{4,28},{8,16},{12,20},{16,8},{20,12},{24,0},{28,4},{1,25},{... | collective-permute-start | bytes 393224 | tf_op jit(solution)/shard_map/ppermute | solution.py:166
  194.9 3.6 %collective-permute-done.40.refs_6_ = bf16[2,128,256]{2,1,0:T(8,128)(2,1)S(1)} collective-permute-done((bf16[2,128,256]{2,1,0:T(8,128)(2,1)}, bf16[2,128,256]{2,1,0:T(8,128)(2,1)S(1)}, u32[]{:S(2)}, u32[]{:S(2)}) %collective-permute-start.40) | collective-permute-done | bytes 131104 | tf_op jit(solution)/shard_map/ppermute | solution.py:166
  199.2 8.4 %collective-permute-start.25 = (bf16[2,128,256]{2,1,0:T(8,128)(2,1)}, bf16[2,128,256]{2,1,0:T(8,128)(2,1)S(1)}, u32[]{:S(2)}, u32[]{:S(2)}) collective-permute-start(bf16[2,128,256]{2,1,0:T(8,128)(2,1)} %get-tuple-element.82), channel_id=1, source_target_pairs={{0,20},{4,16},{8,28},{12,24},{16,4},{20,0},{24,12},{28,8},{1,21},{... | collective-permute-start | bytes 393224 | tf_op jit(solution)/shard_map/ppermute | solution.py:166
  211.1 22.7 %action.1 = f32[8192,256]{1,0:T(8,128)} custom-call(bf16[8192,256]{1,0:T(8,128)(2,1)} %bitcast.14, f32[8192,16]{1,0:T(8,128)} %bitcast.15, bf16[8,160,256]{2,1,0:T(8,128)(2,1)} %bitcast.16), custom_call_target="tpu_custom_call" | custom-call | flops 8589934592 | bytes 20000000 | tf_op jit(solution)/shard_map/action/pallas_call | solution.py:260
  233.9 4.1 %join.4.refs_8_ = bf16[128,64,256]{2,1,0:T(8,128)(2,1)} custom-call(s32[1]{0:T(128)} %bitcast.me_ref, f32[128,64,256]{2,1,0:T(8,128)} %bitcast.10, bf16[2,128,256]{2,1,0:T(8,128)(2,1)} %get-tuple-element.125.refs_0_, bf16[2,128,256]{2,1,0:T(8,128)(2,1)} %copy-done.3, bf16[2,128,256]{2,1,0:T(8,128)(2,1)} %copy-done.4, bf16[2,128,256]{2,1,0:T(8,128)(2,1)} %copy-done.5, ...), custom_call_target="tpu_custom_call" | custom-call | flops 268435456 | bytes 4194304 | tf_op jit(solution)/shard_map/join/pallas_call | solution.py:380
  238.0 4.1 %join.5.refs_8_ = bf16[128,64,256]{2,1,0:T(8,128)(2,1)} custom-call(s32[1]{0:T(128)} %bitcast.me_ref, f32[128,64,256]{2,1,0:T(8,128)} %bitcast.11, bf16[2,128,256]{2,1,0:T(8,128)(2,1)} %get-tuple-element.109.refs_0_, bf16[2,128,256]{2,1,0:T(8,128)(2,1)} %copy-done.10, bf16[2,128,256]{2,1,0:T(8,128)(2,1)} %copy-done.11, ...), custom_call_target="tpu_custom_call", output_to_operand_aliasing={{}: (10, {})} | custom-call | flops 268435456 | bytes 4194304 | tf_op jit(solution)/shard_map/join/pallas_call | solution.py:380
  242.1 4.1 %join.6.refs_8_ = bf16[128,64,256]{2,1,0:T(8,128)(2,1)} custom-call(s32[1]{0:T(128)} %bitcast.me_ref, f32[128,64,256]{2,1,0:T(8,128)} %bitcast.12, bf16[2,128,256]{2,1,0:T(8,128)(2,1)} %get-tuple-element.93.refs_0_, bf16[2,128,256]{2,1,0:T(8,128)(2,1)} %collective-permute-done.35.refs_1_, ...), custom_call_target="tpu_custom_call", output_to_operand_aliasing={{}: (10, {})} | custom-call | flops 268435456 | bytes 4194304 | tf_op jit(solution)/shard_map/join/pallas_call | solution.py:380
  247.1 4.1 %join.7 = bf16[128,64,256]{2,1,0:T(8,128)(2,1)} custom-call(s32[1]{0:T(128)} %bitcast.me_ref, f32[128,64,256]{2,1,0:T(8,128)} %bitcast.13, bf16[2,128,256]{2,1,0:T(8,128)(2,1)} %get-tuple-element.77.refs_0_, bf16[2,128,256]{2,1,0:T(8,128)(2,1)} %copy-done.18, bf16[2,128,256]{2,1,0:T(8,128)(2,1)} %copy-done.20, ...), custom_call_target="tpu_custom_call", output_to_operand_aliasing={{}: (10, {})} | custom-call | flops 268435456 | bytes 4194304 | tf_op jit(solution)/shard_map/join/pallas_call | solution.py:380
  (301 shorter events, 114.9 us)
Async XLA Ops:
  2.7 18.4 %collective-permute-start.56 = (bf16[2,128,256]{2,1,0:T(8,128)(2,1)}, bf16[2,128,256]{2,1,0:T(8,128)(2,1)S(1)}, u32[]{:S(2)}, u32[]{:S(2)}) collective-permute-start(bf16[2,128,256]{2,1,0:T(8,128)(2,1)} %get-tuple-element.118), channel_id=1, source_target_pairs={{0,4},{4,0},{8,12},{12,8},{16,20},{20,16},{24,28},{28,24},{1,5},{5... | collective-permute-start | bytes 393224 | tf_op jit(solution)/shard_map/ppermute | solution.py:166
  15.5 19.0 %collective-permute-start.1 = (bf16[320,256]{1,0:T(8,128)(2,1)S(1)}, bf16[320,256]{1,0:T(8,128)(2,1)S(1)}, u32[]{:S(2)}, u32[]{:S(2)}) collective-permute-start(bf16[320,256]{1,0:T(8,128)(2,1)S(1)} %get-tuple-element.137), channel_id=1, source_target_pairs={{0,2},{1,3},{2,0},{3,1},{4,6},{5,7},{6,4},{7,5},{8,10},{9,11},{10,... | collective-permute-start | bytes 491528 | tf_op jit(solution)/shard_map/ppermute | solution.py:166
  34.5 18.8 %collective-permute-start.42 = (bf16[2,128,256]{2,1,0:T(8,128)(2,1)}, bf16[2,128,256]{2,1,0:T(8,128)(2,1)S(1)}, u32[]{:S(2)}, u32[]{:S(2)}) collective-permute-start(bf16[2,128,256]{2,1,0:T(8,128)(2,1)} %get-tuple-element.102), channel_id=1, source_target_pairs={{0,4},{4,0},{8,12},{12,8},{16,20},{20,16},{24,28},{28,24},{1,5},{5... | collective-permute-start | bytes 393224 | tf_op jit(solution)/shard_map/ppermute | solution.py:166
  34.9 20.9 %collective-permute-start.43 = (bf16[2,128,256]{2,1,0:T(8,128)(2,1)}, bf16[2,128,256]{2,1,0:T(8,128)(2,1)S(1)}, u32[]{:S(2)}, u32[]{:S(2)}) collective-permute-start(bf16[2,128,256]{2,1,0:T(8,128)(2,1)} %get-tuple-element.103), channel_id=1, source_target_pairs={{0,8},{4,12},{8,0},{12,4},{16,24},{20,28},{24,16},{28,20},{1,9},{5... | collective-permute-start | bytes 393224 | tf_op jit(solution)/shard_map/ppermute | solution.py:166
  37.6 23.9 %collective-permute-start.44 = (bf16[2,128,256]{2,1,0:T(8,128)(2,1)}, bf16[2,128,256]{2,1,0:T(8,128)(2,1)S(1)}, u32[]{:S(2)}, u32[]{:S(2)}) collective-permute-start(bf16[2,128,256]{2,1,0:T(8,128)(2,1)} %get-tuple-element.104), channel_id=1, source_target_pairs={{0,12},{4,8},{8,4},{12,0},{16,28},{20,24},{24,20},{28,16},{1,13},{... | collective-permute-start | bytes 393224 | tf_op jit(solution)/shard_map/ppermute | solution.py:166
  44.3 20.0 %collective-permute-start.45 = (bf16[2,128,256]{2,1,0:T(8,128)(2,1)}, bf16[2,128,256]{2,1,0:T(8,128)(2,1)S(1)}, u32[]{:S(2)}, u32[]{:S(2)}) collective-permute-start(bf16[2,128,256]{2,1,0:T(8,128)(2,1)} %get-tuple-element.105), channel_id=1, source_target_pairs={{0,16},{4,20},{8,24},{12,28},{16,0},{20,4},{24,8},{28,12},{1,17},{... | collective-permute-start | bytes 393224 | tf_op jit(solution)/shard_map/ppermute | solution.py:166
  46.5 18.0 %collective-permute-start.3 = (bf16[80,256]{1,0:T(8,128)(2,1)S(1)}, bf16[80,256]{1,0:T(8,128)(2,1)S(1)}, u32[]{:S(2)}, u32[]{:S(2)}) collective-permute-start(bf16[80,256]{1,0:T(8,128)(2,1)S(1)} %get-tuple-element.138), channel_id=1, source_target_pairs={{0,4},{4,0},{8,12},{12,8},{16,20},{20,16},{24,28},{28,24},{1,5},{5... | collective-permute-start | bytes 122888 | tf_op jit(solution)/shard_map/ppermute | solution.py:166
  67.0 18.0 %collective-permute-start.28 = (bf16[2,128,256]{2,1,0:T(8,128)(2,1)S(1)}, bf16[2,128,256]{2,1,0:T(8,128)(2,1)S(1)}, u32[]{:S(2)}, u32[]{:S(2)}) collective-permute-start(bf16[2,128,256]{2,1,0:T(8,128)(2,1)S(1)} %copy-done.73), channel_id=1, source_target_pairs={{0,4},{4,0},{8,12},{12,8},{16,20},{20,16},{24,28},{28,24},{1,5},{5... | collective-permute-start | bytes 393224 | tf_op jit(solution)/shard_map/ppermute | solution.py:166
  68.9 17.5 %collective-permute-start.29 = (bf16[2,128,256]{2,1,0:T(8,128)(2,1)}, bf16[2,128,256]{2,1,0:T(8,128)(2,1)S(1)}, u32[]{:S(2)}, u32[]{:S(2)}) collective-permute-start(bf16[2,128,256]{2,1,0:T(8,128)(2,1)} %get-tuple-element.87), channel_id=1, source_target_pairs={{0,8},{4,12},{8,0},{12,4},{16,24},{20,28},{24,16},{28,20},{1,9},{5... | collective-permute-start | bytes 393224 | tf_op jit(solution)/shard_map/ppermute | solution.py:166
  69.7 24.1 %collective-permute-start.30 = (bf16[2,128,256]{2,1,0:T(8,128)(2,1)}, bf16[2,128,256]{2,1,0:T(8,128)(2,1)S(1)}, u32[]{:S(2)}, u32[]{:S(2)}) collective-permute-start(bf16[2,128,256]{2,1,0:T(8,128)(2,1)} %get-tuple-element.88), channel_id=1, source_target_pairs={{0,12},{4,8},{8,4},{12,0},{16,28},{20,24},{24,20},{28,16},{1,13},{... | collective-permute-start | bytes 393224 | tf_op jit(solution)/shard_map/ppermute | solution.py:166
  78.2 17.0 %collective-permute-start.31 = (bf16[2,128,256]{2,1,0:T(8,128)(2,1)}, bf16[2,128,256]{2,1,0:T(8,128)(2,1)S(1)}, u32[]{:S(2)}, u32[]{:S(2)}) collective-permute-start(bf16[2,128,256]{2,1,0:T(8,128)(2,1)} %get-tuple-element.89), channel_id=1, source_target_pairs={{0,16},{4,20},{8,24},{12,28},{16,0},{20,4},{24,8},{28,12},{1,17},{... | collective-permute-start | bytes 393224 | tf_op jit(solution)/shard_map/ppermute | solution.py:166
  97.7 20.5 %collective-permute-start.16 = (bf16[2,128,256]{2,1,0:T(8,128)(2,1)}, bf16[2,128,256]{2,1,0:T(8,128)(2,1)S(1)}, u32[]{:S(2)}, u32[]{:S(2)}) collective-permute-start(bf16[2,128,256]{2,1,0:T(8,128)(2,1)} %get-tuple-element.72), channel_id=1, source_target_pairs={{0,12},{4,8},{8,4},{12,0},{16,28},{20,24},{24,20},{28,16},{1,13},{... | collective-permute-start | bytes 393224 | tf_op jit(solution)/shard_map/ppermute | solution.py:166
  99.7 19.0 %collective-permute-start.17 = (bf16[2,128,256]{2,1,0:T(8,128)(2,1)S(1)}, bf16[2,128,256]{2,1,0:T(8,128)(2,1)S(1)}, u32[]{:S(2)}, u32[]{:S(2)}) collective-permute-start(bf16[2,128,256]{2,1,0:T(8,128)(2,1)S(1)} %copy-done.59), channel_id=1, source_target_pairs={{0,16},{4,20},{8,24},{12,28},{16,0},{20,4},{24,8},{28,12},{1,17},{... | collective-permute-start | bytes 393224 | tf_op jit(solution)/shard_map/ppermute | solution.py:166
  102.8 19.0 %collective-permute-start.18 = (bf16[2,128,256]{2,1,0:T(8,128)(2,1)S(1)}, bf16[2,128,256]{2,1,0:T(8,128)(2,1)S(1)}, u32[]{:S(2)}, u32[]{:S(2)}) collective-permute-start(bf16[2,128,256]{2,1,0:T(8,128)(2,1)S(1)} %copy-done.55), channel_id=1, source_target_pairs={{0,20},{4,16},{8,28},{12,24},{16,4},{20,0},{24,12},{28,8},{1,21},{... | collective-permute-start | bytes 393224 | tf_op jit(solution)/shard_map/ppermute | solution.py:166
  127.4 17.4 %collective-permute-start.66 = (bf16[2,128,256]{2,1,0:T(8,128)(2,1)}, bf16[2,128,256]{2,1,0:T(8,128)(2,1)S(1)}, u32[]{:S(2)}, u32[]{:S(2)}) collective-permute-start(bf16[2,128,256]{2,1,0:T(8,128)(2,1)} %get-tuple-element.129), channel_id=1, source_target_pairs={{0,16},{4,20},{8,24},{12,28},{16,0},{20,4},{24,8},{28,12},{1,17},{... | collective-permute-start | bytes 393224 | tf_op jit(solution)/shard_map/ppermute | solution.py:166
  127.5 17.6 %collective-permute-start.67 = (bf16[2,128,256]{2,1,0:T(8,128)(2,1)S(1)}, bf16[2,128,256]{2,1,0:T(8,128)(2,1)S(1)}, u32[]{:S(2)}, u32[]{:S(2)}) collective-permute-start(bf16[2,128,256]{2,1,0:T(8,128)(2,1)S(1)} %copy-done.57), channel_id=1, source_target_pairs={{0,20},{4,16},{8,28},{12,24},{16,4},{20,0},{24,12},{28,8},{1,21},{... | collective-permute-start | bytes 393224 | tf_op jit(solution)/shard_map/ppermute | solution.py:166
  153.2 24.0 %collective-permute-start.11 = (bf16[320,256]{1,0:T(8,128)(2,1)S(1)}, bf16[320,256]{1,0:T(8,128)(2,1)S(1)}, u32[]{:S(2)}, u32[]{:S(2)}) collective-permute-start(bf16[320,256]{1,0:T(8,128)(2,1)S(1)} %constant_dynamic-update-slice_fusion.4), channel_id=1, source_target_pairs={{0,1},{1,0},{2,3},{3,2},{4,5},{5,4},{6,7},{7,6},{8,9},{9,8},{10,11... | collective-permute-start | bytes 491528 | tf_op jit(solution)/shard_map/ppermute | solution.py:166
  190.4 17.1 %collective-permute-start.21 = (bf16[2,128,256]{2,1,0:T(8,128)(2,1)}, bf16[2,128,256]{2,1,0:T(8,128)(2,1)S(1)}, u32[]{:S(2)}, u32[]{:S(2)}) collective-permute-start(bf16[2,128,256]{2,1,0:T(8,128)(2,1)} %get-tuple-element.78), channel_id=1, source_target_pairs={{0,4},{4,0},{8,12},{12,8},{16,20},{20,16},{24,28},{28,24},{1,5},{5... | collective-permute-start | bytes 393224 | tf_op jit(solution)/shard_map/ppermute | solution.py:166
  190.4 18.5 %collective-permute-start.22 = (bf16[2,128,256]{2,1,0:T(8,128)(2,1)}, bf16[2,128,256]{2,1,0:T(8,128)(2,1)S(1)}, u32[]{:S(2)}, u32[]{:S(2)}) collective-permute-start(bf16[2,128,256]{2,1,0:T(8,128)(2,1)} %get-tuple-element.79), channel_id=1, source_target_pairs={{0,8},{4,12},{8,0},{12,4},{16,24},{20,28},{24,16},{28,20},{1,9},{5... | collective-permute-start | bytes 393224 | tf_op jit(solution)/shard_map/ppermute | solution.py:166
  193.0 53.2 %collective-permute-start.23 = (bf16[2,128,256]{2,1,0:T(8,128)(2,1)}, bf16[2,128,256]{2,1,0:T(8,128)(2,1)S(1)}, u32[]{:S(2)}, u32[]{:S(2)}) collective-permute-start(bf16[2,128,256]{2,1,0:T(8,128)(2,1)} %get-tuple-element.80), channel_id=1, source_target_pairs={{0,12},{4,8},{8,4},{12,0},{16,28},{20,24},{24,20},{28,16},{1,13},{... | collective-permute-start | bytes 393224 | tf_op jit(solution)/shard_map/ppermute | solution.py:166
  198.5 47.6 %collective-permute-start.24 = (bf16[2,128,256]{2,1,0:T(8,128)(2,1)}, bf16[2,128,256]{2,1,0:T(8,128)(2,1)S(1)}, u32[]{:S(2)}, u32[]{:S(2)}) collective-permute-start(bf16[2,128,256]{2,1,0:T(8,128)(2,1)} %get-tuple-element.81), channel_id=1, source_target_pairs={{0,16},{4,20},{8,24},{12,28},{16,0},{20,4},{24,8},{28,12},{1,17},{... | collective-permute-start | bytes 393224 | tf_op jit(solution)/shard_map/ppermute | solution.py:166
  199.2 47.0 %collective-permute-start.25 = (bf16[2,128,256]{2,1,0:T(8,128)(2,1)}, bf16[2,128,256]{2,1,0:T(8,128)(2,1)S(1)}, u32[]{:S(2)}, u32[]{:S(2)}) collective-permute-start(bf16[2,128,256]{2,1,0:T(8,128)(2,1)} %get-tuple-element.82), channel_id=1, source_target_pairs={{0,20},{4,16},{8,28},{12,24},{16,4},{20,0},{24,12},{28,8},{1,21},{... | collective-permute-start | bytes 393224 | tf_op jit(solution)/shard_map/ppermute | solution.py:166
  207.5 38.7 %collective-permute-start.26 = (bf16[2,128,256]{2,1,0:T(8,128)(2,1)}, bf16[2,128,256]{2,1,0:T(8,128)(2,1)S(1)}, u32[]{:S(2)}, u32[]{:S(2)}) collective-permute-start(bf16[2,128,256]{2,1,0:T(8,128)(2,1)} %get-tuple-element.83), channel_id=1, source_target_pairs={{0,24},{4,28},{8,16},{12,20},{16,8},{20,12},{24,0},{28,4},{1,25},{... | collective-permute-start | bytes 393224 | tf_op jit(solution)/shard_map/ppermute | solution.py:166
  208.9 37.3 %collective-permute-start.27 = (bf16[2,128,256]{2,1,0:T(8,128)(2,1)}, bf16[2,128,256]{2,1,0:T(8,128)(2,1)S(1)}, u32[]{:S(2)}, u32[]{:S(2)}) collective-permute-start(bf16[2,128,256]{2,1,0:T(8,128)(2,1)} %get-tuple-element.84), channel_id=1, source_target_pairs={{0,28},{4,24},{8,20},{12,16},{16,12},{20,8},{24,4},{28,0},{1,29},{... | collective-permute-start | bytes 393224 | tf_op jit(solution)/shard_map/ppermute | solution.py:166
  (120 other events, 2504.1 us)

commit v2 on v1

--- a/solution.py
+++ b/solution.py
@@ -204,22 +204,23 @@
     return place
 
 
-def total_mean_fields(partial):
+def total_mean_fields(partial, potential):
     terms, width_a, width = partial.shape
     group_index = lax.axis_index(GROUP)
     tile_index = lax.axis_index("tile")
     tile_bits = list(range(lax.axis_size("tile").bit_length() - 1))
     group_bits = list(range(lax.axis_size(GROUP).bit_length() - 1))
     far = lax.axis_size("grp").bit_length() - 2
-    stages = [("tile", tile_index, tile_bits)]
-    stages.append((GROUP, group_index, [bit for bit in group_bits if bit != far]))
-    stages.append((GROUP, group_index, [far]))
+    near = [bit for bit in group_bits if bit != far]
+    stages = [("tile", tile_index, tile_bits), (GROUP, group_index, near)]
     array = partial.reshape(terms * width_a, width)
     for axes, index, bits in stages:
         array = scatter_sum(array, axes, place_of(index, bits), bit_flips(bits))
+    array = (array.astype(F32) + exchange(array, GROUP, 1 << far).astype(F32)).astype(BF)
     for axes, index, bits in reversed(stages):
         array = gather_blocks(array, axes, place_of(index, bits), bit_flips(bits))
-    return array.reshape(terms, width_a, width)
+        array, potential = lax.optimization_barrier((array, potential))
+    return array.reshape(terms, width_a, width), potential
 
 
 def action_kernel(points_ref, weight_ref, mean_ref, out_ref, blocks):
@@ -240,22 +241,24 @@
     step = 256
     for start in range(0, rows, step):
         points = points_ref[start : start + step, :]
-        lane = lax.broadcasted_iota(jnp.int32, (step, width), 1)
-        total = jnp.zeros((step, width), F32)
+        on_a = lax.broadcasted_iota(jnp.int32, (step, width), 1) < width_a
+        scaled = []
         for term in range(TERMS):
-            prod = jnp.dot(points, blocks[term], preferred_element_type=F32)
-            on_a = weight_ref[start : start + step, term : term + 1]
-            on_b = weight_ref[start : start + step, TERMS + term : TERMS + term + 1]
-            weight = jnp.where(lane < width_a, on_a, on_b)
-            total = total + prod * weight
-        out_ref[start : start + step, :] = total
+            weight_a = weight_ref[start : start + step, term : term + 1]
+            weight_b = weight_ref[start : start + step, TERMS + term : TERMS + term + 1]
+            scaled.append(points * jnp.where(on_a, weight_a, weight_b))
+        out_ref[start : start + step, :] = jnp.dot(
+            jnp.concatenate(scaled, axis=1),
+            blocks[...].reshape(TERMS * width, width),
+            preferred_element_type=F32,
+        )
 
 
 def action_of(orbitals, potential, mean):
     rows_x, rows_y, width = orbitals.shape
     count = rows_x * rows_y
     points = orbitals.reshape(count, width)
-    weights = potential.reshape(2 * TERMS, count).T
+    weights = potential.reshape(2 * TERMS, count).T.astype(BF)
     step = 512
     action = pl.pallas_call(
         action_kernel,
@@ -278,10 +281,10 @@
 
 def split_kernel(groups, me_ref, orb_ref, *refs):
     outs, rows = refs[:groups], refs[groups]
-    rows_x, chunk, width = orb_ref.shape
-    per = chunk // groups
+    step_x, side, width = orb_ref.shape
+    per = side // groups
     swap = swap_matrix()
-    for start in range(0, rows_x, SIDE):
+    for start in range(0, step_x, SIDE):
         block = orb_ref[start : start + SIDE].reshape(SIDE * SIDE, width)
         turned = jnp.dot(swap, block, preferred_element_type=F32).astype(BF)
         rows[:, start : start + SIDE, :] = turned.reshape(SIDE, SIDE, width)
@@ -290,16 +293,16 @@
         outs[flip][...] = rows[pl.ds((me ^ flip) * per, per)]
 
 
-def split_chunk(me, orbitals, chunk_index, chunk, groups):
+def split_chunk(me, orbitals, first_row, chunk, groups):
     rows_x, _, width = orbitals.shape
-    piece = (chunk // groups, rows_x, width)
+    first, per, step_x = first_row // SIDE, SIDE // groups, rows_x // 2
     return pl.pallas_call(
         functools.partial(split_kernel, groups),
-        grid=(1,),
-        out_shape=[jax.ShapeDtypeStruct(piece, BF)] * groups,
-        in_specs=[SMEM, pl.BlockSpec((rows_x, chunk, width), lambda i: (0, chunk_index, 0))],
-        out_specs=[pl.BlockSpec(piece, lambda i: (0, 0, 0))] * groups,
-        scratch_shapes=[pltpu.VMEM((chunk, rows_x, width), BF)],
+        grid=(chunk // SIDE, rows_x // step_x),
+        out_shape=[jax.ShapeDtypeStruct((chunk // groups, rows_x, width), BF)] * groups,
+        in_specs=[SMEM, pl.BlockSpec((step_x, SIDE, width), lambda p, i: (i, first + p, 0))],
+        out_specs=[pl.BlockSpec((per, step_x, width), lambda p, i: (p, i, 0))] * groups,
+        scratch_shapes=[pltpu.VMEM((SIDE, step_x, width), BF)],
         cost_estimate=pl.CostEstimate(
             flops=2 * rows_x * chunk * width * SIDE * SIDE,
             bytes_accessed=4 * rows_x * chunk * width,
@@ -312,34 +315,36 @@
 def apply_kernel(groups, me_ref, kin_ref, *refs):
     pieces, outs = refs[:groups], refs[groups : 2 * groups]
     gathered, result = refs[2 * groups :]
-    per, rows_x, _ = pieces[0].shape
+    _, rows_x, _ = pieces[0].shape
     size_x = kin_ref.shape[0]
     me = me_ref[0]
-    step = 256
-    for row in range(per):
-        for flip in range(groups):
-            start = pl.multiple_of((me ^ flip) * rows_x, rows_x)
-            gathered[row, pl.ds(start, rows_x), :] = pieces[flip][row]
-        for start in range(0, size_x, step):
-            applied = jnp.dot(
-                kin_ref[start : start + step, :], gathered[row], preferred_element_type=F32
-            )
-            result[row, start : start + step, :] = applied.astype(BF)
-        for flip in range(groups):
-            start = pl.multiple_of((me ^ flip) * rows_x, rows_x)
-            outs[flip][row] = result[row, pl.ds(start, rows_x), :]
+    for flip in range(groups):
+        start = pl.multiple_of((me ^ flip) * rows_x, rows_x)
+        gathered[pl.ds(start, rows_x), :] = pieces[flip][0]
+    step = 512
+    for start in range(0, size_x, step):
+        applied = jnp.dot(
+            kin_ref[start : start + step, :], gathered[...], preferred_element_type=F32
+        )
+        result[start : start + step, :] = applied.astype(BF)
+    for flip in range(groups):
+        start = pl.multiple_of((me ^ flip) * rows_x, rows_x)
+        outs[flip][0] = result[pl.ds(start, rows_x), :]
 
 
 def apply_chunk(me, kinetic, pieces):
     groups = len(pieces)
     per, rows_x, width = pieces[0].shape
     size_x = kinetic.shape[0]
+    block = pl.BlockSpec((1, rows_x, width), lambda i: (i, 0, 0))
+    whole = pl.BlockSpec((size_x, size_x), lambda i: (0, 0), pipeline_mode=pl.Buffered(1))
     return pl.pallas_call(
         functools.partial(apply_kernel, groups),
+        grid=(per,),
         out_shape=[jax.ShapeDtypeStruct((per, rows_x, width), BF)] * groups,
-        in_specs=[SMEM, VMEM] + [VMEM] * groups,
-        out_specs=[VMEM] * groups,
-        scratch_shapes=[pltpu.VMEM((per, size_x, width), BF)] * 2,
+        in_specs=[SMEM, whole] + [block] * groups,
+        out_specs=[block] * groups,
+        scratch_shapes=[pltpu.VMEM((size_x, width), BF)] * 2,
         cost_estimate=pl.CostEstimate(
             flops=2 * size_x * size_x * per * width, bytes_accessed=4 * 10**6, transcendentals=0
         ),
@@ -362,28 +367,27 @@
         out_ref[start : start + SIDE] = (turned + action_ref[start : start + SIDE]).astype(BF)
 
 
-def join_chunk(me, action, pieces, chunk_index, before):
+def join_chunk(me, action, pieces, first_row, before):
     groups = len(pieces)
-    per, rows_x, width = pieces[0].shape
-    chunk = per * groups
+    _, rows_x, width = pieces[0].shape
+    chunk = pieces[0].shape[0] * groups
     rows_y = action.shape[1]
-    step_x = 32
-    first = before is None
-    block = pl.BlockSpec((step_x, chunk, width), lambda i: (i, chunk_index, 0))
-    in_specs = [SMEM, block] + [pl.BlockSpec((per, step_x, width), lambda i: (0, i, 0))] * groups
+    first, per, step_x = first_row // SIDE, SIDE // groups, rows_x // 2
+    block = pl.BlockSpec((step_x, SIDE, width), lambda p, i: (i, first + p, 0))
+    in_specs = [SMEM, block] + [pl.BlockSpec((per, step_x, width), lambda p, i: (p, i, 0))] * groups
     operands = [me, action, *pieces]
     aliases = {}
-    if not first:
+    if before is not None:
         in_specs.append(pl.BlockSpec(memory_space=pl.ANY))
         aliases = {len(operands): 0}
         operands.append(before)
     return pl.pallas_call(
         functools.partial(join_kernel, groups),
-        grid=(rows_x // step_x,),
+        grid=(chunk // SIDE, rows_x // step_x),
         out_shape=jax.ShapeDtypeStruct((rows_x, rows_y, width), BF),
         in_specs=in_specs,
         out_specs=block,
-        scratch_shapes=[pltpu.VMEM((chunk, step_x, width), BF)],
+        scratch_shapes=[pltpu.VMEM((SIDE, step_x, width), BF)],
         input_output_aliases=aliases,
         cost_estimate=pl.CostEstimate(
             flops=2 * rows_x * chunk * width * SIDE * SIDE,
@@ -404,24 +408,30 @@
     return arrived
 
 
+def chunk_sizes(rows_y):
+    if rows_y < 3 * SIDE:
+        return [SIDE] * (rows_y // SIDE)
+    return [rows_y - 2 * SIDE, SIDE, SIDE]
+
+
 def chunked_body(core_tensor, term_operators, block_terms, orbitals, potential, kinetic):
     _, rows_y, _ = orbitals.shape
     groups = lax.axis_size(GROUP)
-    chunk = SIDE
-    chunks = rows_y // chunk
+    sizes = chunk_sizes(rows_y)
+    first_rows = [sum(sizes[:index]) for index in range(len(sizes))]
     me = lax.axis_index(GROUP).astype(jnp.int32).reshape(1)
     returned = []
-    for index in range(chunks):
-        pieces = split_chunk(me, orbitals, index, chunk, groups)
+    for first, size in zip(first_rows, sizes):
+        pieces = split_chunk(me, orbitals, first, size, groups)
         pieces = exchange_all(pieces)
         pieces = apply_chunk(me, kinetic, pieces)
         returned.append(exchange_all(pieces))
     partial = tile_mean_fields(core_tensor, term_operators, block_terms)
-    mean = total_mean_fields(partial)
+    mean, potential = total_mean_fields(partial, potential)
     action = action_of(orbitals, potential, mean)
     result = None
-    for index in range(chunks):
-        result = join_chunk(me, action, returned[index], index, result)
+    for index, first in enumerate(first_rows):
+        result = join_chunk(me, action, returned[index], first, result)
     return result
 
 

time: 253 us -> 258 us (1.020)
  the two profiles are of different devices: /device:TPU:0 before, /device:TPU:12 now
where the time goes in v2:
time: 258 us; the launch traced here: 257 us
  waiting for transfers between devices  103 us (40%)
  starting transfers between devices  79.3 us (31%)
  Pallas kernels  65.7 us (25%)
  local copies, waits for them, and re-layouts  7.02 us (3%)
    ppermute x55, waiting for transfers between devices, exchange(): return lax.ppermute(array, axes, [(i, i ^ flip) for i in range(count)])  103 us
    ppermute x55, starting transfers between devices, exchange(): return lax.ppermute(array, axes, [(i, i ^ flip) for i in range(count)])  79.3 us
    pallas_call x1, Pallas kernels, action_of(): pl.pallas_call(action_kernel, grid=(count // step,), out_shape=jax.ShapeD...  25.5 us
    pallas_call x3, Pallas kernels, apply_chunk(): pl.pallas_call(functools.partial(apply_kernel, groups), grid=(per,), out_...  15.4 us
    pallas_call x3, Pallas kernels, join_chunk(): pl.pallas_call(functools.partial(join_kernel, groups), grid=(chunk // SID...  11 us
    pallas_call x3, Pallas kernels, split_chunk(): pl.pallas_call(functools.partial(split_kernel, groups), grid=(chunk // SI...  9.7 us
  transfers between devices with their start and end apart: 55, of which 17 were waited for; matrix products, arithmetic and copies ran while one was open for 3% of the time, Pallas kernels for 23%

profile of v2, /device:TPU:12, one launch (start us, length us, event | category | flops | bytes accessed | tf_op | source)
XLA Modules:
  0.0 257.0 jit_solution(9100867529364802129)
XLA Ops:
  7.9 4.2 %slot_sums.1 = bf16[8,160,256]{2,1,0:T(8,128)(2,1)} custom-call(s32[1,8]{1,0:T(1,128)} %terms_ref.1, f32[8,64]{1,0:T(8,128)} %reshape.30.oper_ref, bf16[8,96,160]{2,1,0:T(8,128)(2,1)} %copy.11.core_ref), custom_call_target="tpu_custom_call" | custom-call | flops 1000000000 | bytes 2000000 | tf_op jit(solution)/shard_map/slot_sums/pallas_call | solution.py:148
  26.1 6.0 %collective-permute-start.32 = (bf16[2,128,256]{2,1,0:T(8,128)(2,1)S(1)}, bf16[2,128,256]{2,1,0:T(8,128)(2,1)S(1)}, u32[]{:S(2)}, u32[]{:S(2)}) collective-permute-start(bf16[2,128,256]{2,1,0:T(8,128)(2,1)S(1)} %copy-done.41), channel_id=1, source_target_pairs={{0,24},{4,28},{8,16},{12,20},{16,8},{20,12},{24,0},{28,4},{1,25},{... | collective-permute-start | bytes 393224 | tf_op jit(solution)/shard_map/ppermute | solution.py:166
  36.8 4.7 %collective-permute-done.32.refs_6_ = bf16[2,128,256]{2,1,0:T(8,128)(2,1)S(1)} collective-permute-done((bf16[2,128,256]{2,1,0:T(8,128)(2,1)S(1)}, bf16[2,128,256]{2,1,0:T(8,128)(2,1)S(1)}, u32[]{:S(2)}, u32[]{:S(2)}) %collective-permute-start.32) | collective-permute-done | bytes 131104 | tf_op jit(solution)/shard_map/ppermute | solution.py:166
  41.7 8.2 %collective-permute-done.33.refs_7_ = bf16[2,128,256]{2,1,0:T(8,128)(2,1)S(1)} collective-permute-done((bf16[2,128,256]{2,1,0:T(8,128)(2,1)S(1)}, bf16[2,128,256]{2,1,0:T(8,128)(2,1)S(1)}, u32[]{:S(2)}, u32[]{:S(2)}) %collective-permute-start.33) | collective-permute-done | bytes 131104 | tf_op jit(solution)/shard_map/ppermute | solution.py:166
  54.4 4.4 %split.5 = (bf16[4,128,256]{2,1,0:T(8,128)(2,1)}, bf16[4,128,256]{2,1,0:T(8,128)(2,1)}, bf16[4,128,256]{2,1,0:T(8,128)(2,1)}, bf16[4,128,256]{2,1,0:T(8,128)(2,1...) custom-call(s32[1]{0:T(128)} %bitcast.me_ref, ...), custom_call_target="tpu_custom_call" | custom-call | flops 536870912 | bytes 4194304 | tf_op jit(solution)/shard_map/split/pallas_call | solution.py:299
  63.0 5.1 %collective-permute-start.18 = (bf16[2,128,256]{2,1,0:T(8,128)(2,1)}, bf16[2,128,256]{2,1,0:T(8,128)(2,1)S(1)}, u32[]{:S(2)}, u32[]{:S(2)}) collective-permute-start(bf16[2,128,256]{2,1,0:T(8,128)(2,1)} %get-tuple-element.67), channel_id=1, source_target_pairs={{0,24},{4,28},{8,16},{12,20},{16,8},{20,12},{24,0},{28,4},{1,25},{... | collective-permute-start | bytes 393224 | tf_op jit(solution)/shard_map/ppermute | solution.py:166
  68.1 27.2 %collective-permute-done.18.refs_6_ = bf16[2,128,256]{2,1,0:T(8,128)(2,1)S(1)} collective-permute-done((bf16[2,128,256]{2,1,0:T(8,128)(2,1)}, bf16[2,128,256]{2,1,0:T(8,128)(2,1)S(1)}, u32[]{:S(2)}, u32[]{:S(2)}) %collective-permute-start.18) | collective-permute-done | bytes 131104 | tf_op jit(solution)/shard_map/ppermute | solution.py:166
  95.3 4.5 %collective-permute-start.6 = (bf16[80,256]{1,0:T(8,128)(2,1)S(1)}, bf16[80,256]{1,0:T(8,128)(2,1)S(1)}, u32[]{:S(2)}, u32[]{:S(2)}) collective-permute-start(bf16[80,256]{1,0:T(8,128)(2,1)S(1)} %add_convert_fusion.2), channel_id=1, source_target_pairs={{0,8},{4,12},{8,0},{12,4},{16,24},{20,28},{24,16},{28,20},{1,9},{5... | collective-permute-start | bytes 122888 | tf_op jit(solution)/shard_map/ppermute | solution.py:166
  99.8 4.4 %apply.4 = (bf16[2,128,256]{2,1,0:T(8,128)(2,1)}, bf16[2,128,256]{2,1,0:T(8,128)(2,1)}, bf16[2,128,256]{2,1,0:T(8,128)(2,1)}, bf16[2,128,256]{2,1,0:T(8,128)(2,1...) custom-call(s32[1]{0:T(128)} %bitcast.me_ref, ...), custom_call_target="tpu_custom_call" | custom-call | flops 1073741824 | bytes 4000000 | tf_op jit(solution)/shard_map/apply/pallas_call | solution.py:341
  106.9 3.4 %collective-permute-start.47 = (bf16[4,128,256]{2,1,0:T(8,128)(2,1)S(1)}, bf16[4,128,256]{2,1,0:T(8,128)(2,1)}, u32[]{:S(2)}, u32[]{:S(2)}) collective-permute-start(bf16[4,128,256]{2,1,0:T(8,128)(2,1)S(1)} %copy-done.27), channel_id=1, source_target_pairs={{0,28},{4,24},{8,20},{12,16},{16,12},{20,8},{24,4},{28,0},{1,29},{... | collective-permute-start | bytes 786440 | tf_op jit(solution)/shard_map/ppermute | solution.py:166
  110.4 4.4 %apply.3 = (bf16[2,128,256]{2,1,0:T(8,128)(2,1)}, bf16[2,128,256]{2,1,0:T(8,128)(2,1)}, bf16[2,128,256]{2,1,0:T(8,128)(2,1)}, bf16[2,128,256]{2,1,0:T(8,128)(2,1...) custom-call(s32[1]{0:T(128)} %bitcast.me_ref, ...), custom_call_target="tpu_custom_call" | custom-call | flops 1073741824 | bytes 4000000 | tf_op jit(solution)/shard_map/apply/pallas_call | solution.py:341
  115.0 6.6 %collective-permute-done.44.refs_4_ = bf16[4,128,256]{2,1,0:T(8,128)(2,1)S(1)} collective-permute-done((bf16[4,128,256]{2,1,0:T(8,128)(2,1)}, bf16[4,128,256]{2,1,0:T(8,128)(2,1)S(1)}, u32[]{:S(2)}, u32[]{:S(2)}) %collective-permute-start.44) | collective-permute-done | bytes 262176 | tf_op jit(solution)/shard_map/ppermute | solution.py:166
  124.5 6.1 %collective-permute-done.46.refs_6_ = bf16[4,128,256]{2,1,0:T(8,128)(2,1)S(1)} collective-permute-done((bf16[4,128,256]{2,1,0:T(8,128)(2,1)S(1)}, bf16[4,128,256]{2,1,0:T(8,128)(2,1)S(1)}, u32[]{:S(2)}, u32[]{:S(2)}) %collective-permute-start.46) | collective-permute-done | bytes 262176 | tf_op jit(solution)/shard_map/ppermute | solution.py:166
  130.7 7.4 %collective-permute-done.47.refs_7_ = bf16[4,128,256]{2,1,0:T(8,128)(2,1)} collective-permute-done((bf16[4,128,256]{2,1,0:T(8,128)(2,1)S(1)}, bf16[4,128,256]{2,1,0:T(8,128)(2,1)}, u32[]{:S(2)}, u32[]{:S(2)}) %collective-permute-start.47) | collective-permute-done | bytes 262176 | tf_op jit(solution)/shard_map/ppermute | solution.py:166
  140.6 6.5 %apply.5 = (bf16[4,128,256]{2,1,0:T(8,128)(2,1)}, bf16[4,128,256]{2,1,0:T(8,128)(2,1)}, bf16[4,128,256]{2,1,0:T(8,128)(2,1)}, bf16[4,128,256]{2,1,0:T(8,128)(2,1...) custom-call(s32[1]{0:T(128)} %bitcast.me_ref, ...), custom_call_target="tpu_custom_call" | custom-call | flops 2147483648 | bytes 4000000 | tf_op jit(solution)/shard_map/apply/pallas_call | solution.py:341
  153.9 3.4 %collective-permute-start.9 = (bf16[80,256]{1,0:T(8,128)(2,1)S(1)}, bf16[80,256]{1,0:T(8,128)(2,1)S(1)}, u32[]{:S(2)}, u32[]{:S(2)}) collective-permute-start(bf16[80,256]{1,0:T(8,128)(2,1)S(1)} %get-tuple-element.110), channel_id=1, source_target_pairs={{0,20},{4,16},{8,28},{12,24},{16,4},{20,0},{24,12},{28,8},{1,21},{... | collective-permute-start | bytes 122888 | tf_op jit(solution)/shard_map/ppermute | solution.py:166
  157.8 6.9 %collective-permute-done.9 = bf16[80,256]{1,0:T(8,128)(2,1)S(1)} collective-permute-done((bf16[80,256]{1,0:T(8,128)(2,1)S(1)}, bf16[80,256]{1,0:T(8,128)(2,1)S(1)}, u32[]{:S(2)}, u32[]{:S(2)}) %collective-permute-start.9) | collective-permute-done | bytes 40992 | tf_op jit(solution)/shard_map/ppermute | solution.py:166
  168.4 3.6 %collective-permute-done.11 = bf16[320,256]{1,0:T(8,128)(2,1)S(1)} collective-permute-done((bf16[320,256]{1,0:T(8,128)(2,1)S(1)}, bf16[320,256]{1,0:T(8,128)(2,1)S(1)}, u32[]{:S(2)}, u32[]{:S(2)}) %collective-permute-start.11) | collective-permute-done | bytes 163872 | tf_op jit(solution)/shard_map/ppermute | solution.py:166
  183.0 17.4 %collective-permute-done.50.refs_3_ = bf16[4,128,256]{2,1,0:T(8,128)(2,1)S(1)} collective-permute-done((bf16[4,128,256]{2,1,0:T(8,128)(2,1)}, bf16[4,128,256]{2,1,0:T(8,128)(2,1)S(1)}, u32[]{:S(2)}, u32[]{:S(2)}) %collective-permute-start.50) | collective-permute-done | bytes 262176 | tf_op jit(solution)/shard_map/ppermute | solution.py:166
  204.0 4.2 %collective-permute-start.25 = (bf16[2,128,256]{2,1,0:T(8,128)(2,1)S(1)}, bf16[2,128,256]{2,1,0:T(8,128)(2,1)S(1)}, u32[]{:S(2)}, u32[]{:S(2)}) collective-permute-start(bf16[2,128,256]{2,1,0:T(8,128)(2,1)S(1)} %copy-done.37), channel_id=1, source_target_pairs={{0,24},{4,28},{8,16},{12,20},{16,8},{20,12},{24,0},{28,4},{1,25},{... | collective-permute-start | bytes 393224 | tf_op jit(solution)/shard_map/ppermute | solution.py:166
  208.1 8.7 %collective-permute-done.54.refs_7_ = bf16[4,128,256]{2,1,0:T(8,128)(2,1)} collective-permute-done((bf16[4,128,256]{2,1,0:T(8,128)(2,1)}, bf16[4,128,256]{2,1,0:T(8,128)(2,1)}, u32[]{:S(2)}, u32[]{:S(2)}) %collective-permute-start.54) | collective-permute-done | bytes 262176 | tf_op jit(solution)/shard_map/ppermute | solution.py:166
  219.6 25.5 %action.1 = f32[8192,256]{1,0:T(8,128)} custom-call(bf16[8192,256]{1,0:T(8,128)(2,1)} %bitcast.13, bf16[8192,16]{1,0:T(8,128)(2,1)} %bitcast.14, bf16[8,160,256]{2,1,0:T(8,128)(2,1)} %bitcast.15), custom_call_target="tpu_custom_call" | custom-call | flops 8589934592 | bytes 20000000 | tf_op jit(solution)/shard_map/action/pallas_call | solution.py:263
  245.1 5.1 %join.3.refs_8_ = bf16[128,64,256]{2,1,0:T(8,128)(2,1)} custom-call(s32[1]{0:T(128)} %bitcast.me_ref, f32[128,64,256]{2,1,0:T(8,128)} %bitcast.10, bf16[4,128,256]{2,1,0:T(8,128)(2,1)} %get-tuple-element.101.refs_0_, bf16[4,128,256]{2,1,0:T(8,128)(2,1)} %copy-done.3, bf16[4,128,256]{2,1,0:T(8,128)(2,1)} %copy-done.4, bf16[4,128,256]{2,1,0:T(8,128)(2,1)} %copy-done.5, ...), custom_call_target="tpu_custom_call" | custom-call | flops 536870912 | bytes 8388608 | tf_op jit(solution)/shard_map/join/pallas_call | solution.py:384
  250.2 2.9 %join.4.refs_8_ = bf16[128,64,256]{2,1,0:T(8,128)(2,1)} custom-call(s32[1]{0:T(128)} %bitcast.me_ref, f32[128,64,256]{2,1,0:T(8,128)} %bitcast.11, bf16[2,128,256]{2,1,0:T(8,128)(2,1)} %get-tuple-element.85.refs_0_, bf16[2,128,256]{2,1,0:T(8,128)(2,1)} %copy-done.9, bf16[2,128,256]{2,1,0:T(8,128)(2,1)} %copy-done.10, ...), custom_call_target="tpu_custom_call", output_to_operand_aliasing={{}: (10, {})} | custom-call | flops 268435456 | bytes 4194304 | tf_op jit(solution)/shard_map/join/pallas_call | solution.py:384
  (233 shorter events, 75.3 us)
Async XLA Ops:
  15.3 20.4 %collective-permute-start.2 = (bf16[320,256]{1,0:T(8,128)(2,1)S(1)}, bf16[320,256]{1,0:T(8,128)(2,1)S(1)}, u32[]{:S(2)}, u32[]{:S(2)}) collective-permute-start(bf16[320,256]{1,0:T(8,128)(2,1)S(1)} %get-tuple-element.112), channel_id=1, source_target_pairs={{0,3},{1,2},{2,1},{3,0},{4,7},{5,6},{6,5},{7,4},{8,11},{9,10},{10,... | collective-permute-start | bytes 491528 | tf_op jit(solution)/shard_map/ppermute | solution.py:166
  58.9 45.7 %collective-permute-start.41 = (bf16[4,128,256]{2,1,0:T(8,128)(2,1)}, bf16[4,128,256]{2,1,0:T(8,128)(2,1)S(1)}, u32[]{:S(2)}, u32[]{:S(2)}) collective-permute-start(bf16[4,128,256]{2,1,0:T(8,128)(2,1)} %get-tuple-element.94), channel_id=1, source_target_pairs={{0,4},{4,0},{8,12},{12,8},{16,20},{20,16},{24,28},{28,24},{1,5},{5... | collective-permute-start | bytes 786440 | tf_op jit(solution)/shard_map/ppermute | solution.py:166
  60.7 46.2 %collective-permute-start.42 = (bf16[4,128,256]{2,1,0:T(8,128)(2,1)}, bf16[4,128,256]{2,1,0:T(8,128)(2,1)S(1)}, u32[]{:S(2)}, u32[]{:S(2)}) collective-permute-start(bf16[4,128,256]{2,1,0:T(8,128)(2,1)} %get-tuple-element.95), channel_id=1, source_target_pairs={{0,8},{4,12},{8,0},{12,4},{16,24},{20,28},{24,16},{28,20},{1,9},{5... | collective-permute-start | bytes 786440 | tf_op jit(solution)/shard_map/ppermute | solution.py:166
  63.0 51.8 %collective-permute-start.43 = (bf16[4,128,256]{2,1,0:T(8,128)(2,1)}, bf16[4,128,256]{2,1,0:T(8,128)(2,1)S(1)}, u32[]{:S(2)}, u32[]{:S(2)}) collective-permute-start(bf16[4,128,256]{2,1,0:T(8,128)(2,1)} %get-tuple-element.96), channel_id=1, source_target_pairs={{0,12},{4,8},{8,4},{12,0},{16,28},{20,24},{24,20},{28,16},{1,13},{... | collective-permute-start | bytes 786440 | tf_op jit(solution)/shard_map/ppermute | solution.py:166
  63.0 32.3 %collective-permute-start.18 = (bf16[2,128,256]{2,1,0:T(8,128)(2,1)}, bf16[2,128,256]{2,1,0:T(8,128)(2,1)S(1)}, u32[]{:S(2)}, u32[]{:S(2)}) collective-permute-start(bf16[2,128,256]{2,1,0:T(8,128)(2,1)} %get-tuple-element.67), channel_id=1, source_target_pairs={{0,24},{4,28},{8,16},{12,20},{16,8},{20,12},{24,0},{28,4},{1,25},{... | collective-permute-start | bytes 393224 | tf_op jit(solution)/shard_map/ppermute | solution.py:166
  68.1 36.2 %collective-permute-start.19 = (bf16[2,128,256]{2,1,0:T(8,128)(2,1)S(1)}, bf16[2,128,256]{2,1,0:T(8,128)(2,1)}, u32[]{:S(2)}, u32[]{:S(2)}) collective-permute-start(bf16[2,128,256]{2,1,0:T(8,128)(2,1)S(1)} %copy-done.51), channel_id=1, source_target_pairs={{0,28},{4,24},{8,20},{12,16},{16,12},{20,8},{24,4},{28,0},{1,29},{... | collective-permute-start | bytes 393224 | tf_op jit(solution)/shard_map/ppermute | solution.py:166
  104.6 19.9 %collective-permute-start.45 = (bf16[4,128,256]{2,1,0:T(8,128)(2,1)S(1)}, bf16[4,128,256]{2,1,0:T(8,128)(2,1)S(1)}, u32[]{:S(2)}, u32[]{:S(2)}) collective-permute-start(bf16[4,128,256]{2,1,0:T(8,128)(2,1)S(1)} %copy-done.29), channel_id=1, source_target_pairs={{0,20},{4,16},{8,28},{12,24},{16,4},{20,0},{24,12},{28,8},{1,21},{... | collective-permute-start | bytes 786440 | tf_op jit(solution)/shard_map/ppermute | solution.py:166
  104.6 26.0 %collective-permute-start.46 = (bf16[4,128,256]{2,1,0:T(8,128)(2,1)S(1)}, bf16[4,128,256]{2,1,0:T(8,128)(2,1)S(1)}, u32[]{:S(2)}, u32[]{:S(2)}) collective-permute-start(bf16[4,128,256]{2,1,0:T(8,128)(2,1)S(1)} %copy-done.28), channel_id=1, source_target_pairs={{0,24},{4,28},{8,16},{12,20},{16,8},{20,12},{24,0},{28,4},{1,25},{... | collective-permute-start | bytes 786440 | tf_op jit(solution)/shard_map/ppermute | solution.py:166
  106.9 31.1 %collective-permute-start.47 = (bf16[4,128,256]{2,1,0:T(8,128)(2,1)S(1)}, bf16[4,128,256]{2,1,0:T(8,128)(2,1)}, u32[]{:S(2)}, u32[]{:S(2)}) collective-permute-start(bf16[4,128,256]{2,1,0:T(8,128)(2,1)S(1)} %copy-done.27), channel_id=1, source_target_pairs={{0,28},{4,24},{8,20},{12,16},{16,12},{20,8},{24,4},{28,0},{1,29},{... | collective-permute-start | bytes 786440 | tf_op jit(solution)/shard_map/ppermute | solution.py:166
  114.9 23.2 %collective-permute-start.34 = (bf16[2,128,256]{2,1,0:T(8,128)(2,1)}, bf16[2,128,256]{2,1,0:T(8,128)(2,1)S(1)}, u32[]{:S(2)}, u32[]{:S(2)}) collective-permute-start(bf16[2,128,256]{2,1,0:T(8,128)(2,1)} %get-tuple-element.86), channel_id=1, source_target_pairs={{0,4},{4,0},{8,12},{12,8},{16,20},{20,16},{24,28},{28,24},{1,5},{5... | collective-permute-start | bytes 393224 | tf_op jit(solution)/shard_map/ppermute | solution.py:166
  121.6 25.6 %collective-permute-start.35 = (bf16[2,128,256]{2,1,0:T(8,128)(2,1)}, bf16[2,128,256]{2,1,0:T(8,128)(2,1)S(1)}, u32[]{:S(2)}, u32[]{:S(2)}) collective-permute-start(bf16[2,128,256]{2,1,0:T(8,128)(2,1)} %get-tuple-element.87), channel_id=1, source_target_pairs={{0,8},{4,12},{8,0},{12,4},{16,24},{20,28},{24,16},{28,20},{1,9},{5... | collective-permute-start | bytes 393224 | tf_op jit(solution)/shard_map/ppermute | solution.py:166
  124.5 26.0 %collective-permute-start.36 = (bf16[2,128,256]{2,1,0:T(8,128)(2,1)}, bf16[2,128,256]{2,1,0:T(8,128)(2,1)S(1)}, u32[]{:S(2)}, u32[]{:S(2)}) collective-permute-start(bf16[2,128,256]{2,1,0:T(8,128)(2,1)} %get-tuple-element.88), channel_id=1, source_target_pairs={{0,12},{4,8},{8,4},{12,0},{16,28},{20,24},{24,20},{28,16},{1,13},{... | collective-permute-start | bytes 393224 | tf_op jit(solution)/shard_map/ppermute | solution.py:166
  130.7 20.7 %collective-permute-start.37 = (bf16[2,128,256]{2,1,0:T(8,128)(2,1)}, bf16[2,128,256]{2,1,0:T(8,128)(2,1)S(1)}, u32[]{:S(2)}, u32[]{:S(2)}) collective-permute-start(bf16[2,128,256]{2,1,0:T(8,128)(2,1)} %get-tuple-element.89), channel_id=1, source_target_pairs={{0,16},{4,20},{8,24},{12,28},{16,0},{20,4},{24,8},{28,12},{1,17},{... | collective-permute-start | bytes 393224 | tf_op jit(solution)/shard_map/ppermute | solution.py:166
  157.4 20.0 %collective-permute-start.48 = (bf16[4,128,256]{2,1,0:T(8,128)(2,1)}, bf16[4,128,256]{2,1,0:T(8,128)(2,1)S(1)}, u32[]{:S(2)}, u32[]{:S(2)}) collective-permute-start(bf16[4,128,256]{2,1,0:T(8,128)(2,1)} %get-tuple-element.102), channel_id=1, source_target_pairs={{0,4},{4,0},{8,12},{12,8},{16,20},{20,16},{24,28},{28,24},{1,5},{5... | collective-permute-start | bytes 786440 | tf_op jit(solution)/shard_map/ppermute | solution.py:166
  167.5 33.0 %collective-permute-start.50 = (bf16[4,128,256]{2,1,0:T(8,128)(2,1)}, bf16[4,128,256]{2,1,0:T(8,128)(2,1)S(1)}, u32[]{:S(2)}, u32[]{:S(2)}) collective-permute-start(bf16[4,128,256]{2,1,0:T(8,128)(2,1)} %get-tuple-element.104), channel_id=1, source_target_pairs={{0,12},{4,8},{8,4},{12,0},{16,28},{20,24},{24,20},{28,16},{1,13},{... | collective-permute-start | bytes 786440 | tf_op jit(solution)/shard_map/ppermute | solution.py:166
  172.0 28.5 %collective-permute-start.51 = (bf16[4,128,256]{2,1,0:T(8,128)(2,1)}, bf16[4,128,256]{2,1,0:T(8,128)(2,1)S(1)}, u32[]{:S(2)}, u32[]{:S(2)}) collective-permute-start(bf16[4,128,256]{2,1,0:T(8,128)(2,1)} %get-tuple-element.105), channel_id=1, source_target_pairs={{0,16},{4,20},{8,24},{12,28},{16,0},{20,4},{24,8},{28,12},{1,17},{... | collective-permute-start | bytes 786440 | tf_op jit(solution)/shard_map/ppermute | solution.py:166
  174.5 27.4 %collective-permute-start.52 = (bf16[4,128,256]{2,1,0:T(8,128)(2,1)}, bf16[4,128,256]{2,1,0:T(8,128)(2,1)S(1)}, u32[]{:S(2)}, u32[]{:S(2)}) collective-permute-start(bf16[4,128,256]{2,1,0:T(8,128)(2,1)} %get-tuple-element.106), channel_id=1, source_target_pairs={{0,20},{4,16},{8,28},{12,24},{16,4},{20,0},{24,12},{28,8},{1,21},{... | collective-permute-start | bytes 786440 | tf_op jit(solution)/shard_map/ppermute | solution.py:166
  177.4 26.6 %collective-permute-start.53 = (bf16[4,128,256]{2,1,0:T(8,128)(2,1)}, bf16[4,128,256]{2,1,0:T(8,128)(2,1)S(1)}, u32[]{:S(2)}, u32[]{:S(2)}) collective-permute-start(bf16[4,128,256]{2,1,0:T(8,128)(2,1)} %get-tuple-element.107), channel_id=1, source_target_pairs={{0,24},{4,28},{8,16},{12,20},{16,8},{20,12},{24,0},{28,4},{1,25},{... | collective-permute-start | bytes 786440 | tf_op jit(solution)/shard_map/ppermute | solution.py:166
  178.4 38.4 %collective-permute-start.54 = (bf16[4,128,256]{2,1,0:T(8,128)(2,1)}, bf16[4,128,256]{2,1,0:T(8,128)(2,1)}, u32[]{:S(2)}, u32[]{:S(2)}) collective-permute-start(bf16[4,128,256]{2,1,0:T(8,128)(2,1)} %get-tuple-element.108), channel_id=1, source_target_pairs={{0,28},{4,24},{8,20},{12,16},{16,12},{20,8},{24,4},{28,0},{1,29},{... | collective-permute-start | bytes 786440 | tf_op jit(solution)/shard_map/ppermute | solution.py:166
  200.5 52.7 %collective-permute-start.22 = (bf16[2,128,256]{2,1,0:T(8,128)(2,1)}, bf16[2,128,256]{2,1,0:T(8,128)(2,1)S(1)}, u32[]{:S(2)}, u32[]{:S(2)}) collective-permute-start(bf16[2,128,256]{2,1,0:T(8,128)(2,1)} %get-tuple-element.72), channel_id=1, source_target_pairs={{0,12},{4,8},{8,4},{12,0},{16,28},{20,24},{24,20},{28,16},{1,13},{... | collective-permute-start | bytes 393224 | tf_op jit(solution)/shard_map/ppermute | solution.py:166
  200.5 52.7 %collective-permute-start.23 = (bf16[2,128,256]{2,1,0:T(8,128)(2,1)}, bf16[2,128,256]{2,1,0:T(8,128)(2,1)S(1)}, u32[]{:S(2)}, u32[]{:S(2)}) collective-permute-start(bf16[2,128,256]{2,1,0:T(8,128)(2,1)} %get-tuple-element.73), channel_id=1, source_target_pairs={{0,16},{4,20},{8,24},{12,28},{16,0},{20,4},{24,8},{28,12},{1,17},{... | collective-permute-start | bytes 393224 | tf_op jit(solution)/shard_map/ppermute | solution.py:166
  201.9 51.3 %collective-permute-start.24 = (bf16[2,128,256]{2,1,0:T(8,128)(2,1)}, bf16[2,128,256]{2,1,0:T(8,128)(2,1)S(1)}, u32[]{:S(2)}, u32[]{:S(2)}) collective-permute-start(bf16[2,128,256]{2,1,0:T(8,128)(2,1)} %get-tuple-element.74), channel_id=1, source_target_pairs={{0,20},{4,16},{8,28},{12,24},{16,4},{20,0},{24,12},{28,8},{1,21},{... | collective-permute-start | bytes 393224 | tf_op jit(solution)/shard_map/ppermute | solution.py:166
  204.0 49.3 %collective-permute-start.25 = (bf16[2,128,256]{2,1,0:T(8,128)(2,1)S(1)}, bf16[2,128,256]{2,1,0:T(8,128)(2,1)S(1)}, u32[]{:S(2)}, u32[]{:S(2)}) collective-permute-start(bf16[2,128,256]{2,1,0:T(8,128)(2,1)S(1)} %copy-done.37), channel_id=1, source_target_pairs={{0,24},{4,28},{8,16},{12,20},{16,8},{20,12},{24,0},{28,4},{1,25},{... | collective-permute-start | bytes 393224 | tf_op jit(solution)/shard_map/ppermute | solution.py:166
  216.8 36.4 %collective-permute-start.26 = (bf16[2,128,256]{2,1,0:T(8,128)(2,1)S(1)}, bf16[2,128,256]{2,1,0:T(8,128)(2,1)S(1)}, u32[]{:S(2)}, u32[]{:S(2)}) collective-permute-start(bf16[2,128,256]{2,1,0:T(8,128)(2,1)S(1)} %copy-done.36), channel_id=1, source_target_pairs={{0,28},{4,24},{8,20},{12,16},{16,12},{20,8},{24,4},{28,0},{1,29},{... | collective-permute-start | bytes 393224 | tf_op jit(solution)/shard_map/ppermute | solution.py:166
  (89 other events, 2220.5 us)

commit v3 on v2

--- a/solution.py
+++ b/solution.py
@@ -1,4 +1,5 @@
 import functools
+from typing import NamedTuple
 
 import jax
 import jax.numpy as jnp
@@ -10,7 +11,7 @@
 
 TERMS = 8
 GROUP = ("half", "grp")
-SIDE = 16
+LANES = 256
 BF = jnp.bfloat16
 F32 = jnp.float32
 
@@ -91,12 +92,18 @@
 SMEM = pl.BlockSpec(memory_space=pltpu.SMEM)
 
 
-def swap_matrix():
-    count = SIDE * SIDE
-    row = lax.broadcasted_iota(jnp.int32, (count, count), 0)
-    col = lax.broadcasted_iota(jnp.int32, (count, count), 1)
-    hit = (row // SIDE == col % SIDE) & (row % SIDE == col // SIDE)
-    return jnp.where(hit, 1.0, 0.0).astype(BF)
+def place_matrix(me, flips, side, turned):
+    groups = side.groups
+    per, step = side.rows // groups, side.points
+    count = len(flips) * per * step
+    shape = (step * side.rows, count) if turned else (count, step * side.rows)
+    to = lax.broadcasted_iota(jnp.int32, shape, 1 if turned else 0)
+    source = lax.broadcasted_iota(jnp.int32, shape, 0 if turned else 1)
+    flip = jnp.zeros(shape, jnp.int32)
+    for at, value in enumerate(flips):
+        flip = jnp.where(to // (per * step) == at, value, flip)
+    wanted = (to % step) * side.rows + (me ^ flip) * per + (to // step) % per
+    return jnp.where(wanted == source, 1.0, 0.0).astype(BF)
 
 
 def slot_kernel(terms_ref, oper_ref, core_ref, out_ref, core_f, core_t, core_p, mixed):
@@ -279,32 +286,60 @@
     return action.reshape(rows_x, rows_y, width)
 
 
-def split_kernel(groups, me_ref, orb_ref, *refs):
-    outs, rows = refs[:groups], refs[groups]
-    step_x, side, width = orb_ref.shape
-    per = side // groups
-    swap = swap_matrix()
-    for start in range(0, step_x, SIDE):
-        block = orb_ref[start : start + SIDE].reshape(SIDE * SIDE, width)
-        turned = jnp.dot(swap, block, preferred_element_type=F32).astype(BF)
-        rows[:, start : start + SIDE, :] = turned.reshape(SIDE, SIDE, width)
-    me = me_ref[0]
-    for flip in range(groups):
-        outs[flip][...] = rows[pl.ds((me ^ flip) * per, per)]
-
-
-def split_chunk(me, orbitals, first_row, chunk, groups):
+class Side(NamedTuple):
+    groups: int
+    rows: int
+    points: int
+
+
+def side_of(groups):
+    rows = max(8, groups)
+    return Side(groups, rows, LANES // rows)
+
+
+def block_rows(first_row, chunk, side):
+    rows = side.rows
+    while chunk % (2 * rows) == 0 and first_row % (2 * rows) == 0 and rows < 32:
+        rows *= 2
+    return rows
+
+
+def split_kernel(flips, side, me_ref, orb_ref, *refs):
+    outs, matrix = refs[:-1], refs[-1]
+    rows_x, rows, width = orb_ref.shape
+    per, step = side.rows // side.groups, side.points
+
+    @pl.when(pl.program_id(0) == 0)
+    def _():
+        matrix[...] = place_matrix(me_ref[0], flips, side, False)
+
+    for part in range(rows // side.rows):
+        for start in range(0, rows_x, step):
+            block = orb_ref[start : start + step, part * side.rows : (part + 1) * side.rows, :]
+            moved = jnp.dot(
+                matrix[...], block.reshape(step * side.rows, width), preferred_element_type=F32
+            )
+            moved = moved.astype(BF).reshape(len(flips), per, step, width)
+            for at in range(len(flips)):
+                outs[at][part * per : (part + 1) * per, start : start + step, :] = moved[at]
+
+
+def split_chunk(me, orbitals, first_row, chunk, flips, side):
     rows_x, _, width = orbitals.shape
-    first, per, step_x = first_row // SIDE, SIDE // groups, rows_x // 2
+    rows = block_rows(first_row, chunk, side)
+    piece = (rows // side.groups, rows_x, width)
     return pl.pallas_call(
-        functools.partial(split_kernel, groups),
-        grid=(chunk // SIDE, rows_x // step_x),
-        out_shape=[jax.ShapeDtypeStruct((chunk // groups, rows_x, width), BF)] * groups,
-        in_specs=[SMEM, pl.BlockSpec((step_x, SIDE, width), lambda p, i: (i, first + p, 0))],
-        out_specs=[pl.BlockSpec((per, step_x, width), lambda p, i: (p, i, 0))] * groups,
-        scratch_shapes=[pltpu.VMEM((SIDE, step_x, width), BF)],
+        functools.partial(split_kernel, tuple(flips), side),
+        grid=(chunk // rows,),
+        out_shape=[jax.ShapeDtypeStruct((chunk // side.groups, rows_x, width), BF)] * len(flips),
+        in_specs=[
+            SMEM,
+            pl.BlockSpec((rows_x, rows, width), lambda p: (0, first_row // rows + p, 0)),
+        ],
+        out_specs=[pl.BlockSpec(piece, lambda p: (p, 0, 0))] * len(flips),
+        scratch_shapes=[pltpu.VMEM((len(flips) * LANES // side.groups, LANES), BF)],
         cost_estimate=pl.CostEstimate(
-            flops=2 * rows_x * chunk * width * SIDE * SIDE,
+            flops=2 * rows_x * chunk * width * LANES,
             bytes_accessed=4 * rows_x * chunk * width,
             transcendentals=0,
         ),
@@ -352,29 +387,41 @@
     )(me, kinetic, *pieces)
 
 
-def join_kernel(groups, me_ref, action_ref, *refs):
-    pieces = refs[:groups]
-    out_ref, rows = refs[-2:]
-    per = pieces[0].shape[0]
-    step_x, _, width = out_ref.shape
-    me = me_ref[0]
-    for flip in range(groups):
-        rows[pl.ds((me ^ flip) * per, per)] = pieces[flip][...]
-    swap = swap_matrix()
-    for start in range(0, step_x, SIDE):
-        block = rows[:, start : start + SIDE, :].reshape(SIDE * SIDE, width)
-        turned = jnp.dot(swap, block, preferred_element_type=F32).reshape(SIDE, SIDE, width)
-        out_ref[start : start + SIDE] = (turned + action_ref[start : start + SIDE]).astype(BF)
-
-
-def join_chunk(me, action, pieces, first_row, before):
+def join_kernel(side, me_ref, action_ref, *refs):
+    pieces = refs[: side.groups]
+    out_ref, matrix = refs[-2:]
+    step_x, rows, width = out_ref.shape
+    per, step = side.rows // side.groups, side.points
+
+    @pl.when((pl.program_id(0) == 0) & (pl.program_id(1) == 0))
+    def _():
+        matrix[...] = place_matrix(me_ref[0], range(side.groups), side, True)
+
+    for part in range(rows // side.rows):
+        here = slice(part * side.rows, (part + 1) * side.rows)
+        for start in range(0, step_x, step):
+            block = jnp.concatenate(
+                [
+                    piece[part * per : (part + 1) * per, start : start + step, :]
+                    for piece in pieces
+                ],
+                axis=0,
+            ).reshape(step * side.rows, width)
+            moved = jnp.dot(matrix[...], block, preferred_element_type=F32)
+            total = moved.reshape(step, side.rows, width) + action_ref[start : start + step, here, :]
+            out_ref[start : start + step, here, :] = total.astype(BF)
+
+
+def join_chunk(me, action, pieces, first_row, before, side):
     groups = len(pieces)
     _, rows_x, width = pieces[0].shape
     chunk = pieces[0].shape[0] * groups
     rows_y = action.shape[1]
-    first, per, step_x = first_row // SIDE, SIDE // groups, rows_x // 2
-    block = pl.BlockSpec((step_x, SIDE, width), lambda p, i: (i, first + p, 0))
-    in_specs = [SMEM, block] + [pl.BlockSpec((per, step_x, width), lambda p, i: (p, i, 0))] * groups
+    rows = block_rows(first_row, chunk, side)
+    step_x = rows_x // 2 if chunk == rows else rows_x
+    block = pl.BlockSpec((step_x, rows, width), lambda p, i: (i, first_row // rows + p, 0))
+    piece = pl.BlockSpec((rows // groups, step_x, width), lambda p, i: (p, i, 0))
+    in_specs = [SMEM, block] + [piece] * groups
     operands = [me, action, *pieces]
     aliases = {}
     if before is not None:
@@ -382,15 +429,15 @@
         aliases = {len(operands): 0}
         operands.append(before)
     return pl.pallas_call(
-        functools.partial(join_kernel, groups),
-        grid=(chunk // SIDE, rows_x // step_x),
+        functools.partial(join_kernel, side),
+        grid=(chunk // rows, rows_x // step_x),
         out_shape=jax.ShapeDtypeStruct((rows_x, rows_y, width), BF),
         in_specs=in_specs,
         out_specs=block,
-        scratch_shapes=[pltpu.VMEM((SIDE, step_x, width), BF)],
+        scratch_shapes=[pltpu.VMEM((LANES, LANES), BF)],
         input_output_aliases=aliases,
         cost_estimate=pl.CostEstimate(
-            flops=2 * rows_x * chunk * width * SIDE * SIDE,
+            flops=2 * rows_x * chunk * width * LANES,
             bytes_accessed=8 * rows_x * chunk * width,
             transcendentals=0,
         ),
@@ -398,40 +445,55 @@
     )(*operands)
 
 
-def exchange_all(pieces):
-    groups = len(pieces)
-    far = lax.axis_size("grp") // 2
-    order = sorted(range(1, groups), key=lambda flip: (flip & far == 0, flip))
-    arrived = list(pieces)
-    for flip in order:
-        arrived[flip] = exchange(pieces[flip], GROUP, flip)
-    return arrived
-
-
-def chunk_sizes(rows_y):
-    if rows_y < 3 * SIDE:
-        return [SIDE] * (rows_y // SIDE)
-    return [rows_y - 2 * SIDE, SIDE, SIDE]
+def far_flip():
+    return lax.axis_size("grp") // 2
+
+
+def exchange_some(pieces, flips):
+    return {flip: exchange(pieces[flip], GROUP, flip) if flip else pieces[0] for flip in flips}
+
+
+def exchange_all(pieces, near_first):
+    far = far_flip()
+    order = sorted(range(len(pieces)), key=lambda flip: (bool(flip & far) == near_first, flip))
+    arrived = exchange_some(pieces, order)
+    return [arrived[flip] for flip in range(len(pieces))]
+
+
+def chunk_sizes(rows_y, side):
+    if rows_y % (4 * side.rows):
+        return [side.rows] * (rows_y // side.rows)
+    return [rows_y // 2, rows_y // 4, rows_y // 4]
 
 
 def chunked_body(core_tensor, term_operators, block_terms, orbitals, potential, kinetic):
     _, rows_y, _ = orbitals.shape
     groups = lax.axis_size(GROUP)
-    sizes = chunk_sizes(rows_y)
+    side = side_of(groups)
+    sizes = chunk_sizes(rows_y, side)
     first_rows = [sum(sizes[:index]) for index in range(len(sizes))]
+    far = [flip for flip in range(groups) if flip & far_flip()]
+    near = [flip for flip in range(groups) if flip not in far]
     me = lax.axis_index(GROUP).astype(jnp.int32).reshape(1)
     returned = []
-    for first, size in zip(first_rows, sizes):
-        pieces = split_chunk(me, orbitals, first, size, groups)
-        pieces = exchange_all(pieces)
+    for index, (first, size) in enumerate(zip(first_rows, sizes)):
+        if index == 0:
+            arrived = {}
+            for flips in (far, near):
+                cut = split_chunk(me, orbitals, first, size, flips, side)
+                arrived.update(exchange_some(dict(zip(flips, cut)), flips))
+            pieces = [arrived[flip] for flip in range(groups)]
+        else:
+            pieces = split_chunk(me, orbitals, first, size, range(groups), side)
+            pieces = exchange_all(pieces, True)
         pieces = apply_chunk(me, kinetic, pieces)
-        returned.append(exchange_all(pieces))
+        returned.append(exchange_all(pieces, True))
     partial = tile_mean_fields(core_tensor, term_operators, block_terms)
     mean, potential = total_mean_fields(partial, potential)
     action = action_of(orbitals, potential, mean)
     result = None
     for index, first in enumerate(first_rows):
-        result = join_chunk(me, action, returned[index], first, result)
+        result = join_chunk(me, action, returned[index], first, result, side)
     return result
 
 
@@ -446,8 +508,9 @@
         and groups & (groups - 1) == 0
         and tiles & (tiles - 1) == 0
         and tiles > 1
-        and SIDE % groups == 0
-        and rows_y % SIDE == 0
+        and groups % 8 == 0
+        and LANES % (2 * groups) == 0
+        and rows_y % groups == 0
         and rows_x % 128 == 0
         and width == width_a + width_b
         and width % 256 == 0

time: 258 us -> 255 us (0.988)
  the two profiles are of different devices: /device:TPU:12 before, /device:TPU:20 now
where the time goes in v3:
time: 255 us
  waiting for transfers between devices  99.1 us (39%)
  starting transfers between devices  77 us (30%)
  Pallas kernels  68.5 us (27%)
  local copies, waits for them, and re-layouts  8.28 us (3%)
    ppermute x55, waiting for transfers between devices, exchange(): return lax.ppermute(array, axes, [(i, i ^ flip) for i in range(count)])  99.1 us
    ppermute x55, starting transfers between devices, exchange(): return lax.ppermute(array, axes, [(i, i ^ flip) for i in range(count)])  77 us
    pallas_call x1, Pallas kernels, action_of(): pl.pallas_call(action_kernel, grid=(count // step,), out_shape=jax.ShapeD...  25.5 us
    pallas_call x3, Pallas kernels, apply_chunk(): pl.pallas_call(functools.partial(apply_kernel, groups), grid=(per,), out_...  15.5 us
    pallas_call x4, Pallas kernels, split_chunk(): pl.pallas_call(functools.partial(split_kernel, tuple(flips), side), grid=...  11.4 us
    pallas_call x3, Pallas kernels, join_chunk(): pl.pallas_call(functools.partial(join_kernel, side), grid=(chunk // rows,...  10 us
    pallas_call x1, Pallas kernels, tile_mean_fields(): pl.pallas_call(slot_kernel, out_shape=jax.ShapeDtypeStruct((TERMS, width_...  6.18 us
  transfers between devices with their start and end apart: 55, of which 15 were waited for; matrix products, arithmetic and copies ran while one was open for 3% of the time, Pallas kernels for 25%

profile of v3, /device:TPU:20, one launch (start us, length us, event | category | flops | bytes accessed | tf_op | source)
XLA Modules:
  0.0 254.7 jit_solution(1367955083966023118)
XLA Ops:
  7.9 6.2 %slot_sums.1 = bf16[8,160,256]{2,1,0:T(8,128)(2,1)} custom-call(s32[1,8]{1,0:T(1,128)} %terms_ref.1, f32[8,64]{1,0:T(8,128)} %reshape.30.oper_ref, bf16[8,96,160]{2,1,0:T(8,128)(2,1)} %copy.11.core_ref), custom_call_target="tpu_custom_call" | custom-call | flops 1000000000 | bytes 2000000 | tf_op jit(solution)/shard_map/slot_sums/pallas_call | solution.py:155
  16.2 3.6 %collective-permute-start.1 = (bf16[320,256]{1,0:T(8,128)(2,1)S(1)}, bf16[320,256]{1,0:T(8,128)(2,1)S(1)}, u32[]{:S(2)}, u32[]{:S(2)}) collective-permute-start(bf16[320,256]{1,0:T(8,128)(2,1)S(1)} %get-tuple-element.113), channel_id=1, source_target_pairs={{0,2},{1,3},{2,0},{3,1},{4,6},{5,7},{6,4},{7,5},{8,10},{9,11},{10,... | collective-permute-start | bytes 491528 | tf_op jit(solution)/shard_map/ppermute | solution.py:173
  25.4 3.0 %split.6 = (bf16[4,128,256]{2,1,0:T(8,128)(2,1)}, bf16[4,128,256]{2,1,0:T(8,128)(2,1)}, bf16[4,128,256]{2,1,0:T(8,128)(2,1)}, bf16[4,128,256]{2,1,0:T(8,128)(2,1)}) custom-call(s32[1]{0:T(128)} %bitcast.me_ref, bf16[128,64,256]{2,1,0:T(8,128)(2,1)} %orb_ref.7), custom_call_target="tpu_custom_call" | custom-call | flops 536870912 | bytes 4194304 | tf_op jit(solution)/shard_map/split/pallas_call | solution.py:331
  28.7 3.9 %collective-permute-start.33 = (bf16[2,128,256]{2,1,0:T(8,128)(2,1)S(1)}, bf16[2,128,256]{2,1,0:T(8,128)(2,1)S(1)}, u32[]{:S(2)}, u32[]{:S(2)}) collective-permute-start(bf16[2,128,256]{2,1,0:T(8,128)(2,1)S(1)} %copy-done.41), channel_id=1, source_target_pairs={{0,28},{4,24},{8,20},{12,16},{16,12},{20,8},{24,4},{28,0},{1,29},{... | collective-permute-start | bytes 393224 | tf_op jit(solution)/shard_map/ppermute | solution.py:173
  40.6 9.4 %collective-permute-done.33.refs_7_ = bf16[2,128,256]{2,1,0:T(8,128)(2,1)S(1)} collective-permute-done((bf16[2,128,256]{2,1,0:T(8,128)(2,1)S(1)}, bf16[2,128,256]{2,1,0:T(8,128)(2,1)S(1)}, u32[]{:S(2)}, u32[]{:S(2)}) %collective-permute-start.33) | collective-permute-done | bytes 131104 | tf_op jit(solution)/shard_map/ppermute | solution.py:173
  55.8 3.0 %split.7 = (bf16[4,128,256]{2,1,0:T(8,128)(2,1)}, bf16[4,128,256]{2,1,0:T(8,128)(2,1)}, bf16[4,128,256]{2,1,0:T(8,128)(2,1)}, bf16[4,128,256]{2,1,0:T(8,128)(2,1)}) custom-call(s32[1]{0:T(128)} %bitcast.me_ref, bf16[128,64,256]{2,1,0:T(8,128)(2,1)} %orb_ref.7), custom_call_target="tpu_custom_call" | custom-call | flops 536870912 | bytes 4194304 | tf_op jit(solution)/shard_map/split/pallas_call | solution.py:331
  67.4 25.4 %collective-permute-done.18.refs_6_ = bf16[2,128,256]{2,1,0:T(8,128)(2,1)} collective-permute-done((bf16[2,128,256]{2,1,0:T(8,128)(2,1)}, bf16[2,128,256]{2,1,0:T(8,128)(2,1)}, u32[]{:S(2)}, u32[]{:S(2)}) %collective-permute-start.18) | collective-permute-done | bytes 131104 | tf_op jit(solution)/shard_map/ppermute | solution.py:173
  92.8 4.3 %collective-permute-start.6 = (bf16[80,256]{1,0:T(8,128)(2,1)S(1)}, bf16[80,256]{1,0:T(8,128)(2,1)S(1)}, u32[]{:S(2)}, u32[]{:S(2)}) collective-permute-start(bf16[80,256]{1,0:T(8,128)(2,1)S(1)} %add_convert_fusion.2), channel_id=1, source_target_pairs={{0,8},{4,12},{8,0},{12,4},{16,24},{20,28},{24,16},{28,20},{1,9},{5... | collective-permute-start | bytes 122888 | tf_op jit(solution)/shard_map/ppermute | solution.py:173
  97.2 4.6 %apply.4 = (bf16[2,128,256]{2,1,0:T(8,128)(2,1)}, bf16[2,128,256]{2,1,0:T(8,128)(2,1)}, bf16[2,128,256]{2,1,0:T(8,128)(2,1)}, bf16[2,128,256]{2,1,0:T(8,128)(2,1...) custom-call(s32[1]{0:T(128)} %bitcast.me_ref, ...), custom_call_target="tpu_custom_call" | custom-call | flops 1073741824 | bytes 4000000 | tf_op jit(solution)/shard_map/apply/pallas_call | solution.py:376
  107.8 4.4 %apply.3 = (bf16[2,128,256]{2,1,0:T(8,128)(2,1)}, bf16[2,128,256]{2,1,0:T(8,128)(2,1)}, bf16[2,128,256]{2,1,0:T(8,128)(2,1)}, bf16[2,128,256]{2,1,0:T(8,128)(2,1...) custom-call(s32[1]{0:T(128)} %bitcast.me_ref, ...), custom_call_target="tpu_custom_call" | custom-call | flops 1073741824 | bytes 4000000 | tf_op jit(solution)/shard_map/apply/pallas_call | solution.py:376
  113.9 5.7 %collective-permute-done.44.refs_4_ = bf16[4,128,256]{2,1,0:T(8,128)(2,1)S(1)} collective-permute-done((bf16[4,128,256]{2,1,0:T(8,128)(2,1)S(1)}, bf16[4,128,256]{2,1,0:T(8,128)(2,1)S(1)}, u32[]{:S(2)}, u32[]{:S(2)}) %collective-permute-start.44) | collective-permute-done | bytes 262176 | tf_op jit(solution)/shard_map/ppermute | solution.py:173
  122.1 5.9 %collective-permute-done.46.refs_6_ = bf16[4,128,256]{2,1,0:T(8,128)(2,1)} collective-permute-done((bf16[4,128,256]{2,1,0:T(8,128)(2,1)S(1)}, bf16[4,128,256]{2,1,0:T(8,128)(2,1)}, u32[]{:S(2)}, u32[]{:S(2)}) %collective-permute-start.46) | collective-permute-done | bytes 262176 | tf_op jit(solution)/shard_map/ppermute | solution.py:173
  129.2 6.4 %collective-permute-done.47.refs_7_ = bf16[4,128,256]{2,1,0:T(8,128)(2,1)} collective-permute-done((bf16[4,128,256]{2,1,0:T(8,128)(2,1)S(1)}, bf16[4,128,256]{2,1,0:T(8,128)(2,1)}, u32[]{:S(2)}, u32[]{:S(2)}) %collective-permute-start.47) | collective-permute-done | bytes 262176 | tf_op jit(solution)/shard_map/ppermute | solution.py:173
  135.7 3.7 %collective-permute-start.7 = (bf16[80,256]{1,0:T(8,128)(2,1)S(1)}, bf16[80,256]{1,0:T(8,128)(2,1)S(1)}, u32[]{:S(2)}, u32[]{:S(2)}) collective-permute-start(bf16[80,256]{1,0:T(8,128)(2,1)S(1)} %get-tuple-element.110), channel_id=1, source_target_pairs={{0,4},{4,0},{8,12},{12,8},{16,20},{20,16},{24,28},{28,24},{1,5},{5... | collective-permute-start | bytes 122888 | tf_op jit(solution)/shard_map/ppermute | solution.py:173
  139.4 6.5 %apply.5 = (bf16[4,128,256]{2,1,0:T(8,128)(2,1)}, bf16[4,128,256]{2,1,0:T(8,128)(2,1)}, bf16[4,128,256]{2,1,0:T(8,128)(2,1)}, bf16[4,128,256]{2,1,0:T(8,128)(2,1...) custom-call(s32[1]{0:T(128)} %bitcast.me_ref, ...), custom_call_target="tpu_custom_call" | custom-call | flops 2147483648 | bytes 4000000 | tf_op jit(solution)/shard_map/apply/pallas_call | solution.py:376
  156.1 6.5 %collective-permute-done.9 = bf16[80,256]{1,0:T(8,128)(2,1)S(1)} collective-permute-done((bf16[80,256]{1,0:T(8,128)(2,1)S(1)}, bf16[80,256]{1,0:T(8,128)(2,1)S(1)}, u32[]{:S(2)}, u32[]{:S(2)}) %collective-permute-start.9) | collective-permute-done | bytes 40992 | tf_op jit(solution)/shard_map/ppermute | solution.py:173
  166.7 3.1 %collective-permute-done.11 = bf16[320,256]{1,0:T(8,128)(2,1)S(1)} collective-permute-done((bf16[320,256]{1,0:T(8,128)(2,1)S(1)}, bf16[320,256]{1,0:T(8,128)(2,1)S(1)}, u32[]{:S(2)}, u32[]{:S(2)}) %collective-permute-start.11) | collective-permute-done | bytes 163872 | tf_op jit(solution)/shard_map/ppermute | solution.py:173
  172.4 3.2 %collective-permute-start.52 = (bf16[4,128,256]{2,1,0:T(8,128)(2,1)}, bf16[4,128,256]{2,1,0:T(8,128)(2,1)S(1)}, u32[]{:S(2)}, u32[]{:S(2)}) collective-permute-start(bf16[4,128,256]{2,1,0:T(8,128)(2,1)} %get-tuple-element.106), channel_id=1, source_target_pairs={{0,20},{4,16},{8,28},{12,24},{16,4},{20,0},{24,12},{28,8},{1,21},{... | collective-permute-start | bytes 786440 | tf_op jit(solution)/shard_map/ppermute | solution.py:173
  180.3 17.0 %collective-permute-done.50.refs_3_ = bf16[4,128,256]{2,1,0:T(8,128)(2,1)S(1)} collective-permute-done((bf16[4,128,256]{2,1,0:T(8,128)(2,1)}, bf16[4,128,256]{2,1,0:T(8,128)(2,1)S(1)}, u32[]{:S(2)}, u32[]{:S(2)}) %collective-permute-start.50) | collective-permute-done | bytes 262176 | tf_op jit(solution)/shard_map/ppermute | solution.py:173
  199.7 3.1 %collective-permute-done.53.refs_6_ = bf16[4,128,256]{2,1,0:T(8,128)(2,1)S(1)} collective-permute-done((bf16[4,128,256]{2,1,0:T(8,128)(2,1)}, bf16[4,128,256]{2,1,0:T(8,128)(2,1)S(1)}, u32[]{:S(2)}, u32[]{:S(2)}) %collective-permute-start.53) | collective-permute-done | bytes 262176 | tf_op jit(solution)/shard_map/ppermute | solution.py:173
  202.8 4.2 %collective-permute-start.25 = (bf16[2,128,256]{2,1,0:T(8,128)(2,1)S(1)}, bf16[2,128,256]{2,1,0:T(8,128)(2,1)S(1)}, u32[]{:S(2)}, u32[]{:S(2)}) collective-permute-start(bf16[2,128,256]{2,1,0:T(8,128)(2,1)S(1)} %copy-done.38), channel_id=1, source_target_pairs={{0,24},{4,28},{8,16},{12,20},{16,8},{20,12},{24,0},{28,4},{1,25},{... | collective-permute-start | bytes 393224 | tf_op jit(solution)/shard_map/ppermute | solution.py:173
  207.0 8.9 %collective-permute-done.54.refs_7_ = bf16[4,128,256]{2,1,0:T(8,128)(2,1)} collective-permute-done((bf16[4,128,256]{2,1,0:T(8,128)(2,1)}, bf16[4,128,256]{2,1,0:T(8,128)(2,1)}, u32[]{:S(2)}, u32[]{:S(2)}) %collective-permute-start.54) | collective-permute-done | bytes 262176 | tf_op jit(solution)/shard_map/ppermute | solution.py:173
  218.3 25.5 %action.1 = f32[8192,256]{1,0:T(8,128)} custom-call(bf16[8192,256]{1,0:T(8,128)(2,1)} %bitcast.13, bf16[8192,16]{1,0:T(8,128)(2,1)} %bitcast.14, bf16[8,160,256]{2,1,0:T(8,128)(2,1)} %bitcast.15), custom_call_target="tpu_custom_call" | custom-call | flops 8589934592 | bytes 20000000 | tf_op jit(solution)/shard_map/action/pallas_call | solution.py:270
  243.8 4.2 %join.3.refs_8_ = bf16[128,64,256]{2,1,0:T(8,128)(2,1)} custom-call(s32[1]{0:T(128)} %bitcast.me_ref, f32[128,64,256]{2,1,0:T(8,128)} %bitcast.10, bf16[4,128,256]{2,1,0:T(8,128)(2,1)} %get-tuple-element.101.refs_0_, bf16[4,128,256]{2,1,0:T(8,128)(2,1)} %copy-done.3, bf16[4,128,256]{2,1,0:T(8,128)(2,1)} %copy-done.4, bf16[4,128,256]{2,1,0:T(8,128)(2,1)} %copy-done.5, ...), custom_call_target="tpu_custom_call" | custom-call | flops 536870912 | bytes 8388608 | tf_op jit(solution)/shard_map/join/pallas_call | solution.py:431
  (232 shorter events, 82.1 us)
Async XLA Ops:
  28.7 21.4 %collective-permute-start.33 = (bf16[2,128,256]{2,1,0:T(8,128)(2,1)S(1)}, bf16[2,128,256]{2,1,0:T(8,128)(2,1)S(1)}, u32[]{:S(2)}, u32[]{:S(2)}) collective-permute-start(bf16[2,128,256]{2,1,0:T(8,128)(2,1)S(1)} %copy-done.41), channel_id=1, source_target_pairs={{0,28},{4,24},{8,20},{12,16},{16,12},{20,8},{24,4},{28,0},{1,29},{... | collective-permute-start | bytes 393224 | tf_op jit(solution)/shard_map/ppermute | solution.py:173
  34.1 21.3 %collective-permute-start.15 = (bf16[2,128,256]{2,1,0:T(8,128)(2,1)}, bf16[2,128,256]{2,1,0:T(8,128)(2,1)S(1)}, u32[]{:S(2)}, u32[]{:S(2)}) collective-permute-start(bf16[2,128,256]{2,1,0:T(8,128)(2,1)} %get-tuple-element.64), channel_id=1, source_target_pairs={{0,12},{4,8},{8,4},{12,0},{16,28},{20,24},{24,20},{28,16},{1,13},{... | collective-permute-start | bytes 393224 | tf_op jit(solution)/shard_map/ppermute | solution.py:173
  58.9 45.0 %collective-permute-start.41 = (bf16[4,128,256]{2,1,0:T(8,128)(2,1)S(1)}, bf16[4,128,256]{2,1,0:T(8,128)(2,1)S(1)}, u32[]{:S(2)}, u32[]{:S(2)}) collective-permute-start(bf16[4,128,256]{2,1,0:T(8,128)(2,1)S(1)} %copy-done.26), channel_id=1, source_target_pairs={{0,4},{4,0},{8,12},{12,8},{16,20},{20,16},{24,28},{28,24},{1,5},{5... | collective-permute-start | bytes 786440 | tf_op jit(solution)/shard_map/ppermute | solution.py:173
  60.5 45.9 %collective-permute-start.42 = (bf16[4,128,256]{2,1,0:T(8,128)(2,1)}, bf16[4,128,256]{2,1,0:T(8,128)(2,1)S(1)}, u32[]{:S(2)}, u32[]{:S(2)}) collective-permute-start(bf16[4,128,256]{2,1,0:T(8,128)(2,1)} %get-tuple-element.95), channel_id=1, source_target_pairs={{0,8},{4,12},{8,0},{12,4},{16,24},{20,28},{24,16},{28,20},{1,9},{5... | collective-permute-start | bytes 786440 | tf_op jit(solution)/shard_map/ppermute | solution.py:173
  61.2 51.1 %collective-permute-start.43 = (bf16[4,128,256]{2,1,0:T(8,128)(2,1)}, bf16[4,128,256]{2,1,0:T(8,128)(2,1)S(1)}, u32[]{:S(2)}, u32[]{:S(2)}) collective-permute-start(bf16[4,128,256]{2,1,0:T(8,128)(2,1)} %get-tuple-element.96), channel_id=1, source_target_pairs={{0,12},{4,8},{8,4},{12,0},{16,28},{20,24},{24,20},{28,16},{1,13},{... | collective-permute-start | bytes 786440 | tf_op jit(solution)/shard_map/ppermute | solution.py:173
  62.4 30.4 %collective-permute-start.18 = (bf16[2,128,256]{2,1,0:T(8,128)(2,1)}, bf16[2,128,256]{2,1,0:T(8,128)(2,1)}, u32[]{:S(2)}, u32[]{:S(2)}) collective-permute-start(bf16[2,128,256]{2,1,0:T(8,128)(2,1)} %get-tuple-element.67), channel_id=1, source_target_pairs={{0,24},{4,28},{8,16},{12,20},{16,8},{20,12},{24,0},{28,4},{1,25},{... | collective-permute-start | bytes 393224 | tf_op jit(solution)/shard_map/ppermute | solution.py:173
  65.0 36.8 %collective-permute-start.19 = (bf16[2,128,256]{2,1,0:T(8,128)(2,1)S(1)}, bf16[2,128,256]{2,1,0:T(8,128)(2,1)}, u32[]{:S(2)}, u32[]{:S(2)}) collective-permute-start(bf16[2,128,256]{2,1,0:T(8,128)(2,1)S(1)} %copy-done.50), channel_id=1, source_target_pairs={{0,28},{4,24},{8,20},{12,16},{16,12},{20,8},{24,4},{28,0},{1,29},{... | collective-permute-start | bytes 393224 | tf_op jit(solution)/shard_map/ppermute | solution.py:173
  103.9 24.1 %collective-permute-start.46 = (bf16[4,128,256]{2,1,0:T(8,128)(2,1)S(1)}, bf16[4,128,256]{2,1,0:T(8,128)(2,1)}, u32[]{:S(2)}, u32[]{:S(2)}) collective-permute-start(bf16[4,128,256]{2,1,0:T(8,128)(2,1)S(1)} %copy-done.31), channel_id=1, source_target_pairs={{0,24},{4,28},{8,16},{12,20},{16,8},{20,12},{24,0},{28,4},{1,25},{... | collective-permute-start | bytes 786440 | tf_op jit(solution)/shard_map/ppermute | solution.py:173
  106.4 29.2 %collective-permute-start.47 = (bf16[4,128,256]{2,1,0:T(8,128)(2,1)S(1)}, bf16[4,128,256]{2,1,0:T(8,128)(2,1)}, u32[]{:S(2)}, u32[]{:S(2)}) collective-permute-start(bf16[4,128,256]{2,1,0:T(8,128)(2,1)S(1)} %copy-done.30), channel_id=1, source_target_pairs={{0,28},{4,24},{8,20},{12,16},{16,12},{20,8},{24,4},{28,0},{1,29},{... | collective-permute-start | bytes 786440 | tf_op jit(solution)/shard_map/ppermute | solution.py:173
  112.3 23.3 %collective-permute-start.34 = (bf16[2,128,256]{2,1,0:T(8,128)(2,1)}, bf16[2,128,256]{2,1,0:T(8,128)(2,1)S(1)}, u32[]{:S(2)}, u32[]{:S(2)}) collective-permute-start(bf16[2,128,256]{2,1,0:T(8,128)(2,1)} %get-tuple-element.86), channel_id=1, source_target_pairs={{0,4},{4,0},{8,12},{12,8},{16,20},{20,16},{24,28},{28,24},{1,5},{5... | collective-permute-start | bytes 393224 | tf_op jit(solution)/shard_map/ppermute | solution.py:173
  119.6 26.3 %collective-permute-start.35 = (bf16[2,128,256]{2,1,0:T(8,128)(2,1)}, bf16[2,128,256]{2,1,0:T(8,128)(2,1)S(1)}, u32[]{:S(2)}, u32[]{:S(2)}) collective-permute-start(bf16[2,128,256]{2,1,0:T(8,128)(2,1)} %get-tuple-element.87), channel_id=1, source_target_pairs={{0,8},{4,12},{8,0},{12,4},{16,24},{20,28},{24,16},{28,20},{1,9},{5... | collective-permute-start | bytes 393224 | tf_op jit(solution)/shard_map/ppermute | solution.py:173
  119.8 28.1 %collective-permute-start.36 = (bf16[2,128,256]{2,1,0:T(8,128)(2,1)}, bf16[2,128,256]{2,1,0:T(8,128)(2,1)S(1)}, u32[]{:S(2)}, u32[]{:S(2)}) collective-permute-start(bf16[2,128,256]{2,1,0:T(8,128)(2,1)} %get-tuple-element.88), channel_id=1, source_target_pairs={{0,12},{4,8},{8,4},{12,0},{16,28},{20,24},{24,20},{28,16},{1,13},{... | collective-permute-start | bytes 393224 | tf_op jit(solution)/shard_map/ppermute | solution.py:173
  128.0 21.2 %collective-permute-start.37 = (bf16[2,128,256]{2,1,0:T(8,128)(2,1)}, bf16[2,128,256]{2,1,0:T(8,128)(2,1)S(1)}, u32[]{:S(2)}, u32[]{:S(2)}) collective-permute-start(bf16[2,128,256]{2,1,0:T(8,128)(2,1)} %get-tuple-element.89), channel_id=1, source_target_pairs={{0,16},{4,20},{8,24},{12,28},{16,0},{20,4},{24,8},{28,12},{1,17},{... | collective-permute-start | bytes 393224 | tf_op jit(solution)/shard_map/ppermute | solution.py:173
  154.8 20.8 %collective-permute-start.48 = (bf16[4,128,256]{2,1,0:T(8,128)(2,1)}, bf16[4,128,256]{2,1,0:T(8,128)(2,1)S(1)}, u32[]{:S(2)}, u32[]{:S(2)}) collective-permute-start(bf16[4,128,256]{2,1,0:T(8,128)(2,1)} %get-tuple-element.102), channel_id=1, source_target_pairs={{0,4},{4,0},{8,12},{12,8},{16,20},{20,16},{24,28},{28,24},{1,5},{5... | collective-permute-start | bytes 786440 | tf_op jit(solution)/shard_map/ppermute | solution.py:173
  165.4 31.9 %collective-permute-start.50 = (bf16[4,128,256]{2,1,0:T(8,128)(2,1)}, bf16[4,128,256]{2,1,0:T(8,128)(2,1)S(1)}, u32[]{:S(2)}, u32[]{:S(2)}) collective-permute-start(bf16[4,128,256]{2,1,0:T(8,128)(2,1)} %get-tuple-element.104), channel_id=1, source_target_pairs={{0,12},{4,8},{8,4},{12,0},{16,28},{20,24},{24,20},{28,16},{1,13},{... | collective-permute-start | bytes 786440 | tf_op jit(solution)/shard_map/ppermute | solution.py:173
  169.9 29.8 %collective-permute-start.51 = (bf16[4,128,256]{2,1,0:T(8,128)(2,1)}, bf16[4,128,256]{2,1,0:T(8,128)(2,1)S(1)}, u32[]{:S(2)}, u32[]{:S(2)}) collective-permute-start(bf16[4,128,256]{2,1,0:T(8,128)(2,1)} %get-tuple-element.105), channel_id=1, source_target_pairs={{0,16},{4,20},{8,24},{12,28},{16,0},{20,4},{24,8},{28,12},{1,17},{... | collective-permute-start | bytes 786440 | tf_op jit(solution)/shard_map/ppermute | solution.py:173
  172.4 27.3 %collective-permute-start.52 = (bf16[4,128,256]{2,1,0:T(8,128)(2,1)}, bf16[4,128,256]{2,1,0:T(8,128)(2,1)S(1)}, u32[]{:S(2)}, u32[]{:S(2)}) collective-permute-start(bf16[4,128,256]{2,1,0:T(8,128)(2,1)} %get-tuple-element.106), channel_id=1, source_target_pairs={{0,20},{4,16},{8,28},{12,24},{16,4},{20,0},{24,12},{28,8},{1,21},{... | collective-permute-start | bytes 786440 | tf_op jit(solution)/shard_map/ppermute | solution.py:173
  175.6 27.2 %collective-permute-start.53 = (bf16[4,128,256]{2,1,0:T(8,128)(2,1)}, bf16[4,128,256]{2,1,0:T(8,128)(2,1)S(1)}, u32[]{:S(2)}, u32[]{:S(2)}) collective-permute-start(bf16[4,128,256]{2,1,0:T(8,128)(2,1)} %get-tuple-element.107), channel_id=1, source_target_pairs={{0,24},{4,28},{8,16},{12,20},{16,8},{20,12},{24,0},{28,4},{1,25},{... | collective-permute-start | bytes 786440 | tf_op jit(solution)/shard_map/ppermute | solution.py:173
  177.5 38.5 %collective-permute-start.54 = (bf16[4,128,256]{2,1,0:T(8,128)(2,1)}, bf16[4,128,256]{2,1,0:T(8,128)(2,1)}, u32[]{:S(2)}, u32[]{:S(2)}) collective-permute-start(bf16[4,128,256]{2,1,0:T(8,128)(2,1)} %get-tuple-element.108), channel_id=1, source_target_pairs={{0,28},{4,24},{8,20},{12,16},{16,12},{20,8},{24,4},{28,0},{1,29},{... | collective-permute-start | bytes 786440 | tf_op jit(solution)/shard_map/ppermute | solution.py:173
  197.3 53.6 %collective-permute-start.22 = (bf16[2,128,256]{2,1,0:T(8,128)(2,1)}, bf16[2,128,256]{2,1,0:T(8,128)(2,1)S(1)}, u32[]{:S(2)}, u32[]{:S(2)}) collective-permute-start(bf16[2,128,256]{2,1,0:T(8,128)(2,1)} %get-tuple-element.72), channel_id=1, source_target_pairs={{0,12},{4,8},{8,4},{12,0},{16,28},{20,24},{24,20},{28,16},{1,13},{... | collective-permute-start | bytes 393224 | tf_op jit(solution)/shard_map/ppermute | solution.py:173
  199.6 51.3 %collective-permute-start.23 = (bf16[2,128,256]{2,1,0:T(8,128)(2,1)}, bf16[2,128,256]{2,1,0:T(8,128)(2,1)S(1)}, u32[]{:S(2)}, u32[]{:S(2)}) collective-permute-start(bf16[2,128,256]{2,1,0:T(8,128)(2,1)} %get-tuple-element.73), channel_id=1, source_target_pairs={{0,16},{4,20},{8,24},{12,28},{16,0},{20,4},{24,8},{28,12},{1,17},{... | collective-permute-start | bytes 393224 | tf_op jit(solution)/shard_map/ppermute | solution.py:173
  199.6 51.3 %collective-permute-start.24 = (bf16[2,128,256]{2,1,0:T(8,128)(2,1)}, bf16[2,128,256]{2,1,0:T(8,128)(2,1)S(1)}, u32[]{:S(2)}, u32[]{:S(2)}) collective-permute-start(bf16[2,128,256]{2,1,0:T(8,128)(2,1)} %get-tuple-element.74), channel_id=1, source_target_pairs={{0,20},{4,16},{8,28},{12,24},{16,4},{20,0},{24,12},{28,8},{1,21},{... | collective-permute-start | bytes 393224 | tf_op jit(solution)/shard_map/ppermute | solution.py:173
  202.8 48.1 %collective-permute-start.25 = (bf16[2,128,256]{2,1,0:T(8,128)(2,1)S(1)}, bf16[2,128,256]{2,1,0:T(8,128)(2,1)S(1)}, u32[]{:S(2)}, u32[]{:S(2)}) collective-permute-start(bf16[2,128,256]{2,1,0:T(8,128)(2,1)S(1)} %copy-done.38), channel_id=1, source_target_pairs={{0,24},{4,28},{8,16},{12,20},{16,8},{20,12},{24,0},{28,4},{1,25},{... | collective-permute-start | bytes 393224 | tf_op jit(solution)/shard_map/ppermute | solution.py:173
  216.0 35.0 %collective-permute-start.26 = (bf16[2,128,256]{2,1,0:T(8,128)(2,1)S(1)}, bf16[2,128,256]{2,1,0:T(8,128)(2,1)S(1)}, u32[]{:S(2)}, u32[]{:S(2)}) collective-permute-start(bf16[2,128,256]{2,1,0:T(8,128)(2,1)S(1)} %copy-done.37), channel_id=1, source_target_pairs={{0,28},{4,24},{8,20},{12,16},{16,12},{20,8},{24,4},{28,0},{1,29},{... | collective-permute-start | bytes 393224 | tf_op jit(solution)/shard_map/ppermute | solution.py:173
  (88 other events, 1902.7 us)

commit v4 on v3

--- a/solution.py
+++ b/solution.py
@@ -230,9 +230,9 @@
     return array.reshape(terms, width_a, width), potential
 
 
-def action_kernel(points_ref, weight_ref, mean_ref, out_ref, blocks):
+def action_kernel(on_chip, points_ref, weight_ref, mean_ref, out_ref, blocks):
     width_a = mean_ref.shape[1]
-    rows, width = points_ref.shape
+    count_x, rows, width = points_ref.shape
     width_b = width - width_a
 
     @pl.when(pl.program_id(0) == 0)
@@ -245,45 +245,54 @@
                 lane[:width_b] < width_a, 0.0, packed[:width_b]
             ).astype(BF)
 
-    step = 256
-    for start in range(0, rows, step):
-        points = points_ref[start : start + step, :]
-        on_a = lax.broadcasted_iota(jnp.int32, (step, width), 1) < width_a
+    step = 16
+    while count_x % step or step * rows > 512:
+        step //= 2
+    base = pl.program_id(0) * count_x if on_chip else 0
+    count = step * rows
+    on_a = lax.broadcasted_iota(jnp.int32, (count, width), 1) < width_a
+    for start in range(0, count_x, step):
+        points = points_ref[start : start + step].reshape(count, width)
+        weight = weight_ref[start : start + step].reshape(count, 2 * TERMS)
         scaled = []
         for term in range(TERMS):
-            weight_a = weight_ref[start : start + step, term : term + 1]
-            weight_b = weight_ref[start : start + step, TERMS + term : TERMS + term + 1]
+            weight_a = weight[:, term : term + 1]
+            weight_b = weight[:, TERMS + term : TERMS + term + 1]
             scaled.append(points * jnp.where(on_a, weight_a, weight_b))
-        out_ref[start : start + step, :] = jnp.dot(
+        total = jnp.dot(
             jnp.concatenate(scaled, axis=1),
             blocks[...].reshape(TERMS * width, width),
             preferred_element_type=F32,
         )
-
-
-def action_of(orbitals, potential, mean):
-    rows_x, rows_y, width = orbitals.shape
-    count = rows_x * rows_y
-    points = orbitals.reshape(count, width)
-    weights = potential.reshape(2 * TERMS, count).T.astype(BF)
-    step = 512
-    action = pl.pallas_call(
-        action_kernel,
-        grid=(count // step,),
-        out_shape=jax.ShapeDtypeStruct((count, width), F32),
+        out_ref[pl.ds(base + start, step)] = total.reshape(step, rows, width)
+
+
+def action_rows(orbitals, weights, mean, first_row, rows, on_chip):
+    rows_x, _, width = orbitals.shape
+    step = min(rows_x, 1024 // rows // 8 * 8)
+    while rows_x % step:
+        step -= 8
+    at = first_row // rows
+    out = (rows_x, rows, width)
+    block = pl.BlockSpec((step, rows, width), lambda i: (i, 0, 0))
+    return pl.pallas_call(
+        functools.partial(action_kernel, on_chip),
+        grid=(rows_x // step,),
+        out_shape=pltpu.VMEM(out, F32) if on_chip else jax.ShapeDtypeStruct(out, F32),
         in_specs=[
-            pl.BlockSpec((step, width), lambda i: (i, 0)),
-            pl.BlockSpec((step, 2 * TERMS), lambda i: (i, 0)),
+            pl.BlockSpec((step, rows, width), lambda i: (i, at, 0)),
+            pl.BlockSpec((step, rows, 2 * TERMS), lambda i: (i, at, 0)),
             pl.BlockSpec(mean.shape, lambda i: (0, 0, 0)),
         ],
-        out_specs=pl.BlockSpec((step, width), lambda i: (i, 0)),
+        out_specs=VMEM if on_chip else block,
         scratch_shapes=[pltpu.VMEM((TERMS, width, width), BF)],
         cost_estimate=pl.CostEstimate(
-            flops=2 * count * width * width * TERMS, bytes_accessed=2 * 10**7, transcendentals=0
+            flops=2 * rows_x * rows * width * width * TERMS,
+            bytes_accessed=8 * rows_x * rows * width,
+            transcendentals=0,
         ),
         name="action",
-    )(points, weights, mean)
-    return action.reshape(rows_x, rows_y, width)
+    )(orbitals, weights, mean)
 
 
 class Side(NamedTuple):
@@ -328,15 +337,17 @@
     rows_x, _, width = orbitals.shape
     rows = block_rows(first_row, chunk, side)
     piece = (rows // side.groups, rows_x, width)
+    on_chip = rows == chunk and len(flips) < side.groups
+    kind = pltpu.VMEM if on_chip else jax.ShapeDtypeStruct
     return pl.pallas_call(
         functools.partial(split_kernel, tuple(flips), side),
         grid=(chunk // rows,),
-        out_shape=[jax.ShapeDtypeStruct((chunk // side.groups, rows_x, width), BF)] * len(flips),
+        out_shape=[kind((chunk // side.groups, rows_x, width), BF)] * len(flips),
         in_specs=[
             SMEM,
             pl.BlockSpec((rows_x, rows, width), lambda p: (0, first_row // rows + p, 0)),
         ],
-        out_specs=[pl.BlockSpec(piece, lambda p: (p, 0, 0))] * len(flips),
+        out_specs=[VMEM if on_chip else pl.BlockSpec(piece, lambda p: (p, 0, 0))] * len(flips),
         scratch_shapes=[pltpu.VMEM((len(flips) * LANES // side.groups, LANES), BF)],
         cost_estimate=pl.CostEstimate(
             flops=2 * rows_x * chunk * width * LANES,
@@ -412,11 +423,10 @@
             out_ref[start : start + step, here, :] = total.astype(BF)
 
 
-def join_chunk(me, action, pieces, first_row, before, side):
+def join_chunk(me, action, pieces, first_row, before, rows_y, side):
     groups = len(pieces)
     _, rows_x, width = pieces[0].shape
     chunk = pieces[0].shape[0] * groups
-    rows_y = action.shape[1]
     rows = block_rows(first_row, chunk, side)
     step_x = rows_x // 2 if chunk == rows else rows_x
     block = pl.BlockSpec((step_x, rows, width), lambda p, i: (i, first_row // rows + p, 0))
@@ -445,6 +455,59 @@
     )(*operands)
 
 
+def last_join_kernel(side, first_row, me_ref, action_ref, *refs):
+    pieces = refs[: side.groups]
+    out_ref, matrix, parts, sems = refs[-4:]
+    rows_x, rows, width = action_ref.shape
+    per, step = side.rows // side.groups, side.points
+    matrix[...] = place_matrix(me_ref[0], range(side.groups), side, True)
+    copies = []
+    for at, start in enumerate(range(0, rows_x, step)):
+        for part in range(rows // side.rows):
+            here = slice(part * side.rows, (part + 1) * side.rows)
+            block = jnp.concatenate(
+                [
+                    piece[part * per : (part + 1) * per, start : start + step, :]
+                    for piece in pieces
+                ],
+                axis=0,
+            ).reshape(step * side.rows, width)
+            moved = jnp.dot(matrix[...], block, preferred_element_type=F32)
+            total = moved.reshape(step, side.rows, width) + action_ref[start : start + step, here, :]
+            parts[at, :, here, :] = total.astype(BF)
+        where = out_ref.at[pl.ds(start, step), pl.ds(first_row, rows), :]
+        copies.append(pltpu.make_async_copy(parts.at[at], where, sems.at[at]))
+        copies[-1].start()
+    for copy in copies:
+        copy.wait()
+
+
+def last_join(me, action, pieces, first_row, before, side):
+    rows_x, rows, width = action.shape
+    blocks = rows_x // side.points
+    pieces = [pltpu.with_memory_space_constraint(piece, pltpu.VMEM) for piece in pieces]
+    action = pltpu.with_memory_space_constraint(action, pltpu.VMEM)
+    hbm = pl.BlockSpec(memory_space=pl.ANY)
+    return pl.pallas_call(
+        functools.partial(last_join_kernel, side, first_row),
+        out_shape=jax.ShapeDtypeStruct(before.shape, BF),
+        in_specs=[SMEM] + [VMEM] * (1 + len(pieces)) + [hbm],
+        out_specs=hbm,
+        scratch_shapes=[
+            pltpu.VMEM((LANES, LANES), BF),
+            pltpu.VMEM((blocks, side.points, rows, width), BF),
+            pltpu.SemaphoreType.DMA((blocks,)),
+        ],
+        input_output_aliases={2 + len(pieces): 0},
+        cost_estimate=pl.CostEstimate(
+            flops=2 * rows_x * rows * width * LANES,
+            bytes_accessed=2 * rows_x * rows * width,
+            transcendentals=0,
+        ),
+        name="join",
+    )(me, action, *pieces, before)
+
+
 def far_flip():
     return lax.axis_size("grp") // 2
 
@@ -467,7 +530,7 @@
 
 
 def chunked_body(core_tensor, term_operators, block_terms, orbitals, potential, kinetic):
-    _, rows_y, _ = orbitals.shape
+    rows_x, rows_y, _ = orbitals.shape
     groups = lax.axis_size(GROUP)
     side = side_of(groups)
     sizes = chunk_sizes(rows_y, side)
@@ -490,10 +553,15 @@
         returned.append(exchange_all(pieces, True))
     partial = tile_mean_fields(core_tensor, term_operators, block_terms)
     mean, potential = total_mean_fields(partial, potential)
-    action = action_of(orbitals, potential, mean)
+    last_row, last_rows = first_rows[-1], sizes[-1]
+    weights = potential.reshape(2 * TERMS, rows_x * rows_y).T.astype(BF)
+    weights = weights.reshape(rows_x, rows_y, 2 * TERMS)
+    action = action_rows(orbitals, weights, mean, 0, last_row, False)
+    action_last = action_rows(orbitals, weights, mean, last_row, last_rows, True)
     result = None
-    for index, first in enumerate(first_rows):
-        result = join_chunk(me, action, returned[index], first, result, side)
+    for index, first in enumerate(first_rows[:-1]):
+        result = join_chunk(me, action, returned[index], first, result, rows_y, side)
+    result = last_join(me, action_last, returned[-1], last_row, result, side)
     return result
 
 

time: 255 us -> 235 us (0.922)
  the two profiles are of different devices: /device:TPU:20 before, /device:TPU:0 now
where the time goes in v4:
time: 235 us; the launch traced here: 234 us
  starting transfers between devices  94.1 us (40%)
  waiting for transfers between devices  64.2 us (27%)
  Pallas kernels  62.7 us (27%)
  local copies, waits for them, and re-layouts  11 us (5%)
    ppermute x55, starting transfers between devices, exchange(): return lax.ppermute(array, axes, [(i, i ^ flip) for i in range(count)])  94.1 us
    ppermute x55, waiting for transfers between devices, exchange(): return lax.ppermute(array, axes, [(i, i ^ flip) for i in range(count)])  64.2 us
    pallas_call x2, Pallas kernels, action_rows(): pl.pallas_call(functools.partial(action_kernel, on_chip), grid=(rows_x //...  24.9 us
    pallas_call x3, Pallas kernels, apply_chunk(): pl.pallas_call(functools.partial(apply_kernel, groups), grid=(per,), out_...  15.6 us
    pallas_call x4, Pallas kernels, split_chunk(): pl.pallas_call(functools.partial(split_kernel, tuple(flips), side), grid=...  9.5 us
    pallas_call x2, Pallas kernels, join_chunk(): pl.pallas_call(functools.partial(join_kernel, side), grid=(chunk // rows,...  7.33 us
    unnamed x97, local copies, waits for them, and re-layouts  5.91 us
  transfers between devices with their start and end apart: 55, of which 9 were waited for; matrix products, arithmetic and copies ran while one was open for 2% of the time, Pallas kernels for 24%

profile of v4, /device:TPU:0, one launch (start us, length us, event | category | flops | bytes accessed | tf_op | source)
XLA Modules:
  0.0 234.0 jit_solution(18295521999202006381)
XLA Ops:
  3.3 4.2 %slot_sums.1 = bf16[8,160,256]{2,1,0:T(8,128)(2,1)} custom-call(s32[1,8]{1,0:T(1,128)} %terms_ref.1, f32[8,64]{1,0:T(8,128)} %reshape.26.oper_ref, bf16[8,96,160]{2,1,0:T(8,128)(2,1)} %copy.10.core_ref), custom_call_target="tpu_custom_call" | custom-call | flops 1000000000 | bytes 2000000 | tf_op jit(solution)/shard_map/slot_sums/pallas_call | solution.py:155
  8.7 7.0 %collective-permute-start.1 = (bf16[320,256]{1,0:T(8,128)(2,1)S(1)}, bf16[320,256]{1,0:T(8,128)(2,1)S(1)}, u32[]{:S(2)}, u32[]{:S(2)}) collective-permute-start(bf16[320,256]{1,0:T(8,128)(2,1)S(1)} %get-tuple-element.113), channel_id=1, source_target_pairs={{0,2},{1,3},{2,0},{3,1},{4,6},{5,7},{6,4},{7,5},{8,10},{9,11},{10,... | collective-permute-start | bytes 491528 | tf_op jit(solution)/shard_map/ppermute | solution.py:173
  18.7 4.6 %collective-permute-start.28 = (bf16[2,128,256]{2,1,0:T(8,128)(2,1)}, bf16[2,128,256]{2,1,0:T(8,128)(2,1)S(1)}, u32[]{:S(2)}, u32[]{:S(2)}) collective-permute-start(bf16[2,128,256]{2,1,0:T(8,128)(2,1)} %get-tuple-element.79), channel_id=1, source_target_pairs={{0,8},{4,12},{8,0},{12,4},{16,24},{20,28},{24,16},{28,20},{1,9},{5... | collective-permute-start | bytes 393224 | tf_op jit(solution)/shard_map/ppermute | solution.py:173
  23.3 2.7 %split.4 = (bf16[2,128,256]{2,1,0:T(8,128)(2,1)}, bf16[2,128,256]{2,1,0:T(8,128)(2,1)}, bf16[2,128,256]{2,1,0:T(8,128)(2,1)}, bf16[2,128,256]{2,1,0:T(8,128)(2,1...) custom-call(s32[1]{0:T(128)} %bitcast.me_ref, ...), custom_call_target="tpu_custom_call" | custom-call | flops 268435456 | bytes 2097152 | tf_op jit(solution)/shard_map/split/pallas_call | solution.py:342
  33.4 3.4 %collective-permute-start.32 = (bf16[2,128,256]{2,1,0:T(8,128)(2,1)S(1)}, bf16[2,128,256]{2,1,0:T(8,128)(2,1)}, u32[]{:S(2)}, u32[]{:S(2)}) collective-permute-start(bf16[2,128,256]{2,1,0:T(8,128)(2,1)S(1)} %copy-done.35), channel_id=1, source_target_pairs={{0,24},{4,28},{8,16},{12,20},{16,8},{20,12},{24,0},{28,4},{1,25},{... | collective-permute-start | bytes 393224 | tf_op jit(solution)/shard_map/ppermute | solution.py:173
  47.0 3.6 %collective-permute-start.14 = (bf16[2,128,256]{2,1,0:T(8,128)(2,1)S(1)}, bf16[2,128,256]{2,1,0:T(8,128)(2,1)S(1)}, u32[]{:S(2)}, u32[]{:S(2)}) collective-permute-start(bf16[2,128,256]{2,1,0:T(8,128)(2,1)S(1)} %copy-done.36), channel_id=1, source_target_pairs={{0,8},{4,12},{8,0},{12,4},{16,24},{20,28},{24,16},{28,20},{1,9},{5... | collective-permute-start | bytes 393224 | tf_op jit(solution)/shard_map/ppermute | solution.py:173
  56.5 4.7 %apply.4 = (bf16[2,128,256]{2,1,0:T(8,128)(2,1)}, bf16[2,128,256]{2,1,0:T(8,128)(2,1)}, bf16[2,128,256]{2,1,0:T(8,128)(2,1)}, bf16[2,128,256]{2,1,0:T(8,128)(2,1...) custom-call(s32[1]{0:T(128)} %bitcast.me_ref, ...), custom_call_target="tpu_custom_call" | custom-call | flops 1073741824 | bytes 4000000 | tf_op jit(solution)/shard_map/apply/pallas_call | solution.py:387
  69.5 28.0 %collective-permute-done.18.refs_6_ = bf16[2,128,256]{2,1,0:T(8,128)(2,1)S(1)} collective-permute-done((bf16[2,128,256]{2,1,0:T(8,128)(2,1)}, bf16[2,128,256]{2,1,0:T(8,128)(2,1)S(1)}, u32[]{:S(2)}, u32[]{:S(2)}) %collective-permute-start.18) | collective-permute-done | bytes 131104 | tf_op jit(solution)/shard_map/ppermute | solution.py:173
  98.2 4.4 %apply.3 = (bf16[2,128,256]{2,1,0:T(8,128)(2,1)}, bf16[2,128,256]{2,1,0:T(8,128)(2,1)}, bf16[2,128,256]{2,1,0:T(8,128)(2,1)}, bf16[2,128,256]{2,1,0:T(8,128)(2,1...) custom-call(s32[1]{0:T(128)} %bitcast.me_ref, ...), custom_call_target="tpu_custom_call" | custom-call | flops 1073741824 | bytes 4000000 | tf_op jit(solution)/shard_map/apply/pallas_call | solution.py:387
  112.0 9.6 %collective-permute-done.9 = bf16[80,256]{1,0:T(8,128)(2,1)S(1)} collective-permute-done((bf16[80,256]{1,0:T(8,128)(2,1)S(1)}, bf16[80,256]{1,0:T(8,128)(2,1)S(1)}, u32[]{:S(2)}, u32[]{:S(2)}) %collective-permute-start.9) | collective-permute-done | bytes 40992 | tf_op jit(solution)/shard_map/ppermute | solution.py:173
  121.6 4.3 %collective-permute-start.34 = (bf16[2,128,256]{2,1,0:T(8,128)(2,1)}, bf16[2,128,256]{2,1,0:T(8,128)(2,1)S(1)}, u32[]{:S(2)}, u32[]{:S(2)}) collective-permute-start(bf16[2,128,256]{2,1,0:T(8,128)(2,1)} %get-tuple-element.86), channel_id=1, source_target_pairs={{0,4},{4,0},{8,12},{12,8},{16,20},{20,16},{24,28},{28,24},{1,5},{5... | collective-permute-start | bytes 393224 | tf_op jit(solution)/shard_map/ppermute | solution.py:173
  131.1 8.5 %collective-permute-start.38 = (bf16[2,128,256]{2,1,0:T(8,128)(2,1)S(1)}, bf16[2,128,256]{2,1,0:T(8,128)(2,1)S(1)}, u32[]{:S(2)}, u32[]{:S(2)}) collective-permute-start(bf16[2,128,256]{2,1,0:T(8,128)(2,1)S(1)} %copy-done.27), channel_id=1, source_target_pairs={{0,20},{4,16},{8,28},{12,24},{16,4},{20,0},{24,12},{28,8},{1,21},{... | collective-permute-start | bytes 393224 | tf_op jit(solution)/shard_map/ppermute | solution.py:173
  139.7 6.5 %apply.5 = (bf16[4,128,256]{2,1,0:T(8,128)(2,1)}, bf16[4,128,256]{2,1,0:T(8,128)(2,1)}, bf16[4,128,256]{2,1,0:T(8,128)(2,1)}, bf16[4,128,256]{2,1,0:T(8,128)(2,1...) custom-call(s32[1]{0:T(128)} %bitcast.me_ref, ...), custom_call_target="tpu_custom_call" | custom-call | flops 2147483648 | bytes 4000000 | tf_op jit(solution)/shard_map/apply/pallas_call | solution.py:387
  148.6 3.4 %collective-permute-start.48 = (bf16[4,128,256]{2,1,0:T(8,128)(2,1)}, bf16[4,128,256]{2,1,0:T(8,128)(2,1)S(1)}, u32[]{:S(2)}, u32[]{:S(2)}) collective-permute-start(bf16[4,128,256]{2,1,0:T(8,128)(2,1)} %get-tuple-element.102), channel_id=1, source_target_pairs={{0,4},{4,0},{8,12},{12,8},{16,20},{20,16},{24,28},{28,24},{1,5},{5... | collective-permute-start | bytes 786440 | tf_op jit(solution)/shard_map/ppermute | solution.py:173
  152.1 5.0 %collective-permute-done.39.refs_6_ = bf16[2,128,256]{2,1,0:T(8,128)(2,1)S(1)} collective-permute-done((bf16[2,128,256]{2,1,0:T(8,128)(2,1)}, bf16[2,128,256]{2,1,0:T(8,128)(2,1)S(1)}, u32[]{:S(2)}, u32[]{:S(2)}) %collective-permute-start.39) | collective-permute-done | bytes 131104 | tf_op jit(solution)/shard_map/ppermute | solution.py:173
  163.6 5.8 %collective-permute-done.40.refs_7_ = bf16[2,128,256]{2,1,0:T(8,128)(2,1)S(1)} collective-permute-done((bf16[2,128,256]{2,1,0:T(8,128)(2,1)S(1)}, bf16[2,128,256]{2,1,0:T(8,128)(2,1)S(1)}, u32[]{:S(2)}, u32[]{:S(2)}) %collective-permute-start.40) | collective-permute-done | bytes 131104 | tf_op jit(solution)/shard_map/ppermute | solution.py:173
  173.8 10.3 %collective-permute-done.21.refs_2_ = bf16[2,128,256]{2,1,0:T(8,128)(2,1)S(1)} collective-permute-done((bf16[2,128,256]{2,1,0:T(8,128)(2,1)}, bf16[2,128,256]{2,1,0:T(8,128)(2,1)S(1)}, u32[]{:S(2)}, u32[]{:S(2)}) %collective-permute-start.21) | collective-permute-done | bytes 131104 | tf_op jit(solution)/shard_map/ppermute | solution.py:173
  187.4 3.2 %collective-permute-start.54 = (bf16[4,128,256]{2,1,0:T(8,128)(2,1)S(1)}, bf16[4,128,256]{2,1,0:T(8,128)(2,1)S(1)}, u32[]{:S(2)}, u32[]{:S(2)}) collective-permute-start(bf16[4,128,256]{2,1,0:T(8,128)(2,1)S(1)} %copy-done.20), channel_id=1, source_target_pairs={{0,28},{4,24},{8,20},{12,16},{16,12},{20,8},{24,4},{28,0},{1,29},{... | collective-permute-start | bytes 786440 | tf_op jit(solution)/shard_map/ppermute | solution.py:173
  190.6 18.3 %action.3.action_ref = f32[128,48,256]{2,1,0:T(8,128)} custom-call(bf16[128,64,256]{2,1,0:T(8,128)(2,1)} %orb_ref.7, bf16[128,64,16]{2,1,0:T(8,128)(2,1)} %bitcast.9, bf16[8,160,256]{2,1,0:T(8,128)(2,1)} %bitcast.11), custom_call_target="tpu_custom_call" | custom-call | flops 6442450944 | bytes 12582912 | tf_op jit(solution)/shard_map/action/pallas_call | solution.py:278
  211.3 3.5 %collective-permute-start.25 = (bf16[2,128,256]{2,1,0:T(8,128)(2,1)}, bf16[2,128,256]{2,1,0:T(8,128)(2,1)S(1)}, u32[]{:S(2)}, u32[]{:S(2)}) collective-permute-start(bf16[2,128,256]{2,1,0:T(8,128)(2,1)} %get-tuple-element.75), channel_id=1, source_target_pairs={{0,24},{4,28},{8,16},{12,20},{16,8},{20,12},{24,0},{28,4},{1,25},{... | collective-permute-start | bytes 393224 | tf_op jit(solution)/shard_map/ppermute | solution.py:173
  215.5 3.1 %collective-permute-start.26 = (bf16[2,128,256]{2,1,0:T(8,128)(2,1)}, bf16[2,128,256]{2,1,0:T(8,128)(2,1)S(1)}, u32[]{:S(2)}, u32[]{:S(2)}) collective-permute-start(bf16[2,128,256]{2,1,0:T(8,128)(2,1)} %get-tuple-element.76), channel_id=1, source_target_pairs={{0,28},{4,24},{8,20},{12,16},{16,12},{20,8},{24,4},{28,0},{1,29},{... | collective-permute-start | bytes 393224 | tf_op jit(solution)/shard_map/ppermute | solution.py:173
  218.7 6.6 %action.2.action_ref = f32[128,16,256]{2,1,0:T(8,128)S(1)} custom-call(bf16[128,64,256]{2,1,0:T(8,128)(2,1)} %orb_ref.7, bf16[128,64,16]{2,1,0:T(8,128)(2,1)} %bitcast.10, bf16[8,160,256]{2,1,0:T(8,128)(2,1)} %bitcast.12), custom_call_target="tpu_custom_call" | custom-call | flops 2147483648 | bytes 4194304 | tf_op jit(solution)/shard_map/action/pallas_call | solution.py:278
  225.2 4.4 %join.3.refs_8_ = bf16[128,64,256]{2,1,0:T(8,128)(2,1)} custom-call(s32[1]{0:T(128)} %bitcast.me_ref, f32[128,48,256]{2,1,0:T(8,128)} %action.3.action_ref, bf16[4,128,256]{2,1,0:T(8,128)(2,1)} %get-tuple-element.101.refs_0_, bf16[4,128,256]{2,1,0:T(8,128)(2,1)} %copy-done.4, bf16[4,128,256]{2,1,0:T(8,128)(2,1)} %copy-done.5, ...), custom_call_target="tpu_custom_call" | custom-call | flops 536870912 | bytes 8388608 | tf_op jit(solution)/shard_map/join/pallas_call | solution.py:441
  229.6 3.0 %join.4.refs_8_ = bf16[128,64,256]{2,1,0:T(8,128)(2,1)} custom-call(s32[1]{0:T(128)} %bitcast.me_ref, f32[128,48,256]{2,1,0:T(8,128)} %action.3.action_ref, bf16[2,128,256]{2,1,0:T(8,128)(2,1)} %get-tuple-element.85.refs_0_, bf16[2,128,256]{2,1,0:T(8,128)(2,1)} %copy-done.11, bf16[2,128,256]{2,1,0:T(8,128)(2,1)} %copy-done.12, ...), custom_call_target="tpu_custom_call", output_to_operand_aliasing={{}: (10, {})} | custom-call | flops 268435456 | bytes 4194304 | tf_op jit(solution)/shard_map/join/pallas_call | solution.py:441
  (215 shorter events, 75.3 us)
Async XLA Ops:
  8.7 21.6 %collective-permute-start.1 = (bf16[320,256]{1,0:T(8,128)(2,1)S(1)}, bf16[320,256]{1,0:T(8,128)(2,1)S(1)}, u32[]{:S(2)}, u32[]{:S(2)}) collective-permute-start(bf16[320,256]{1,0:T(8,128)(2,1)S(1)} %get-tuple-element.113), channel_id=1, source_target_pairs={{0,2},{1,3},{2,0},{3,1},{4,6},{5,7},{6,4},{7,5},{8,10},{9,11},{10,... | collective-permute-start | bytes 491528 | tf_op jit(solution)/shard_map/ppermute | solution.py:173
  61.9 40.8 %collective-permute-start.41 = (bf16[4,128,256]{2,1,0:T(8,128)(2,1)S(1)}, bf16[4,128,256]{2,1,0:T(8,128)(2,1)S(1)}, u32[]{:S(2)}, u32[]{:S(2)}) collective-permute-start(bf16[4,128,256]{2,1,0:T(8,128)(2,1)S(1)} %get-tuple-element.94), channel_id=1, source_target_pairs={{0,4},{4,0},{8,12},{12,8},{16,20},{20,16},{24,28},{28,24},{1,5},{5... | collective-permute-start | bytes 786440 | tf_op jit(solution)/shard_map/ppermute | solution.py:173
  61.9 42.8 %collective-permute-start.42 = (bf16[4,128,256]{2,1,0:T(8,128)(2,1)S(1)}, bf16[4,128,256]{2,1,0:T(8,128)(2,1)S(1)}, u32[]{:S(2)}, u32[]{:S(2)}) collective-permute-start(bf16[4,128,256]{2,1,0:T(8,128)(2,1)S(1)} %get-tuple-element.95), channel_id=1, source_target_pairs={{0,8},{4,12},{8,0},{12,4},{16,24},{20,28},{24,16},{28,20},{1,9},{5... | collective-permute-start | bytes 786440 | tf_op jit(solution)/shard_map/ppermute | solution.py:173
  64.1 42.1 %collective-permute-start.43 = (bf16[4,128,256]{2,1,0:T(8,128)(2,1)S(1)}, bf16[4,128,256]{2,1,0:T(8,128)(2,1)S(1)}, u32[]{:S(2)}, u32[]{:S(2)}) collective-permute-start(bf16[4,128,256]{2,1,0:T(8,128)(2,1)S(1)} %get-tuple-element.96), channel_id=1, source_target_pairs={{0,12},{4,8},{8,4},{12,0},{16,28},{20,24},{24,20},{28,16},{1,13},{... | collective-permute-start | bytes 786440 | tf_op jit(solution)/shard_map/ppermute | solution.py:173
  66.3 31.1 %collective-permute-start.18 = (bf16[2,128,256]{2,1,0:T(8,128)(2,1)}, bf16[2,128,256]{2,1,0:T(8,128)(2,1)S(1)}, u32[]{:S(2)}, u32[]{:S(2)}) collective-permute-start(bf16[2,128,256]{2,1,0:T(8,128)(2,1)} %get-tuple-element.67), channel_id=1, source_target_pairs={{0,24},{4,28},{8,16},{12,20},{16,8},{20,12},{24,0},{28,4},{1,25},{... | collective-permute-start | bytes 393224 | tf_op jit(solution)/shard_map/ppermute | solution.py:173
  66.9 30.6 %collective-permute-start.19 = (bf16[2,128,256]{2,1,0:T(8,128)(2,1)S(1)}, bf16[2,128,256]{2,1,0:T(8,128)(2,1)S(1)}, u32[]{:S(2)}, u32[]{:S(2)}) collective-permute-start(bf16[2,128,256]{2,1,0:T(8,128)(2,1)S(1)} %copy-done.31), channel_id=1, source_target_pairs={{0,28},{4,24},{8,20},{12,16},{16,12},{20,8},{24,4},{28,0},{1,29},{... | collective-permute-start | bytes 393224 | tf_op jit(solution)/shard_map/ppermute | solution.py:173
  102.7 23.2 %collective-permute-start.44 = (bf16[4,128,256]{2,1,0:T(8,128)(2,1)S(1)}, bf16[4,128,256]{2,1,0:T(8,128)(2,1)S(1)}, u32[]{:S(2)}, u32[]{:S(2)}) collective-permute-start(bf16[4,128,256]{2,1,0:T(8,128)(2,1)S(1)} %get-tuple-element.97), channel_id=1, source_target_pairs={{0,16},{4,20},{8,24},{12,28},{16,0},{20,4},{24,8},{28,12},{1,17},{... | collective-permute-start | bytes 786440 | tf_op jit(solution)/shard_map/ppermute | solution.py:173
  104.7 21.6 %collective-permute-start.45 = (bf16[4,128,256]{2,1,0:T(8,128)(2,1)S(1)}, bf16[4,128,256]{2,1,0:T(8,128)(2,1)S(1)}, u32[]{:S(2)}, u32[]{:S(2)}) collective-permute-start(bf16[4,128,256]{2,1,0:T(8,128)(2,1)S(1)} %get-tuple-element.98), channel_id=1, source_target_pairs={{0,20},{4,16},{8,28},{12,24},{16,4},{20,0},{24,12},{28,8},{1,21},{... | collective-permute-start | bytes 786440 | tf_op jit(solution)/shard_map/ppermute | solution.py:173
  106.2 23.4 %collective-permute-start.46 = (bf16[4,128,256]{2,1,0:T(8,128)(2,1)S(1)}, bf16[4,128,256]{2,1,0:T(8,128)(2,1)S(1)}, u32[]{:S(2)}, u32[]{:S(2)}) collective-permute-start(bf16[4,128,256]{2,1,0:T(8,128)(2,1)S(1)} %get-tuple-element.99), channel_id=1, source_target_pairs={{0,24},{4,28},{8,16},{12,20},{16,8},{20,12},{24,0},{28,4},{1,25},{... | collective-permute-start | bytes 786440 | tf_op jit(solution)/shard_map/ppermute | solution.py:173
  107.9 23.2 %collective-permute-start.47 = (bf16[4,128,256]{2,1,0:T(8,128)(2,1)S(1)}, bf16[4,128,256]{2,1,0:T(8,128)(2,1)S(1)}, u32[]{:S(2)}, u32[]{:S(2)}) collective-permute-start(bf16[4,128,256]{2,1,0:T(8,128)(2,1)S(1)} %get-tuple-element.100), channel_id=1, source_target_pairs={{0,28},{4,24},{8,20},{12,16},{16,12},{20,8},{24,4},{28,0},{1,29},{... | collective-permute-start | bytes 786440 | tf_op jit(solution)/shard_map/ppermute | solution.py:173
  125.9 20.3 %collective-permute-start.35 = (bf16[2,128,256]{2,1,0:T(8,128)(2,1)}, bf16[2,128,256]{2,1,0:T(8,128)(2,1)S(1)}, u32[]{:S(2)}, u32[]{:S(2)}) collective-permute-start(bf16[2,128,256]{2,1,0:T(8,128)(2,1)} %get-tuple-element.87), channel_id=1, source_target_pairs={{0,8},{4,12},{8,0},{12,4},{16,24},{20,28},{24,16},{28,20},{1,9},{5... | collective-permute-start | bytes 393224 | tf_op jit(solution)/shard_map/ppermute | solution.py:173
  126.4 21.1 %collective-permute-start.36 = (bf16[2,128,256]{2,1,0:T(8,128)(2,1)}, bf16[2,128,256]{2,1,0:T(8,128)(2,1)S(1)}, u32[]{:S(2)}, u32[]{:S(2)}) collective-permute-start(bf16[2,128,256]{2,1,0:T(8,128)(2,1)} %get-tuple-element.88), channel_id=1, source_target_pairs={{0,12},{4,8},{8,4},{12,0},{16,28},{20,24},{24,20},{28,16},{1,13},{... | collective-permute-start | bytes 393224 | tf_op jit(solution)/shard_map/ppermute | solution.py:173
  148.6 37.0 %collective-permute-start.48 = (bf16[4,128,256]{2,1,0:T(8,128)(2,1)}, bf16[4,128,256]{2,1,0:T(8,128)(2,1)S(1)}, u32[]{:S(2)}, u32[]{:S(2)}) collective-permute-start(bf16[4,128,256]{2,1,0:T(8,128)(2,1)} %get-tuple-element.102), channel_id=1, source_target_pairs={{0,4},{4,0},{8,12},{12,8},{16,20},{20,16},{24,28},{28,24},{1,5},{5... | collective-permute-start | bytes 786440 | tf_op jit(solution)/shard_map/ppermute | solution.py:173
  152.0 35.3 %collective-permute-start.49 = (bf16[4,128,256]{2,1,0:T(8,128)(2,1)}, bf16[4,128,256]{2,1,0:T(8,128)(2,1)S(1)}, u32[]{:S(2)}, u32[]{:S(2)}) collective-permute-start(bf16[4,128,256]{2,1,0:T(8,128)(2,1)} %get-tuple-element.103), channel_id=1, source_target_pairs={{0,8},{4,12},{8,0},{12,4},{16,24},{20,28},{24,16},{28,20},{1,9},{5... | collective-permute-start | bytes 786440 | tf_op jit(solution)/shard_map/ppermute | solution.py:173
  158.7 25.5 %collective-permute-start.21 = (bf16[2,128,256]{2,1,0:T(8,128)(2,1)}, bf16[2,128,256]{2,1,0:T(8,128)(2,1)S(1)}, u32[]{:S(2)}, u32[]{:S(2)}) collective-permute-start(bf16[2,128,256]{2,1,0:T(8,128)(2,1)} %get-tuple-element.71), channel_id=1, source_target_pairs={{0,8},{4,12},{8,0},{12,4},{16,24},{20,28},{24,16},{28,20},{1,9},{5... | collective-permute-start | bytes 393224 | tf_op jit(solution)/shard_map/ppermute | solution.py:173
  169.4 39.5 %collective-permute-start.50 = (bf16[4,128,256]{2,1,0:T(8,128)(2,1)}, bf16[4,128,256]{2,1,0:T(8,128)(2,1)S(1)}, u32[]{:S(2)}, u32[]{:S(2)}) collective-permute-start(bf16[4,128,256]{2,1,0:T(8,128)(2,1)} %get-tuple-element.104), channel_id=1, source_target_pairs={{0,12},{4,8},{8,4},{12,0},{16,28},{20,24},{24,20},{28,16},{1,13},{... | collective-permute-start | bytes 786440 | tf_op jit(solution)/shard_map/ppermute | solution.py:173
  172.5 38.7 %collective-permute-start.51 = (bf16[4,128,256]{2,1,0:T(8,128)(2,1)}, bf16[4,128,256]{2,1,0:T(8,128)(2,1)S(1)}, u32[]{:S(2)}, u32[]{:S(2)}) collective-permute-start(bf16[4,128,256]{2,1,0:T(8,128)(2,1)} %get-tuple-element.105), channel_id=1, source_target_pairs={{0,16},{4,20},{8,24},{12,28},{16,0},{20,4},{24,8},{28,12},{1,17},{... | collective-permute-start | bytes 786440 | tf_op jit(solution)/shard_map/ppermute | solution.py:173
  184.2 27.0 %collective-permute-start.52 = (bf16[4,128,256]{2,1,0:T(8,128)(2,1)}, bf16[4,128,256]{2,1,0:T(8,128)(2,1)S(1)}, u32[]{:S(2)}, u32[]{:S(2)}) collective-permute-start(bf16[4,128,256]{2,1,0:T(8,128)(2,1)} %get-tuple-element.106), channel_id=1, source_target_pairs={{0,20},{4,16},{8,28},{12,24},{16,4},{20,0},{24,12},{28,8},{1,21},{... | collective-permute-start | bytes 786440 | tf_op jit(solution)/shard_map/ppermute | solution.py:173
  185.7 25.6 %collective-permute-start.53 = (bf16[4,128,256]{2,1,0:T(8,128)(2,1)S(1)}, bf16[4,128,256]{2,1,0:T(8,128)(2,1)S(1)}, u32[]{:S(2)}, u32[]{:S(2)}) collective-permute-start(bf16[4,128,256]{2,1,0:T(8,128)(2,1)S(1)} %copy-done.21), channel_id=1, source_target_pairs={{0,24},{4,28},{8,16},{12,20},{16,8},{20,12},{24,0},{28,4},{1,25},{... | collective-permute-start | bytes 786440 | tf_op jit(solution)/shard_map/ppermute | solution.py:173
  187.4 27.4 %collective-permute-start.54 = (bf16[4,128,256]{2,1,0:T(8,128)(2,1)S(1)}, bf16[4,128,256]{2,1,0:T(8,128)(2,1)S(1)}, u32[]{:S(2)}, u32[]{:S(2)}) collective-permute-start(bf16[4,128,256]{2,1,0:T(8,128)(2,1)S(1)} %copy-done.20), channel_id=1, source_target_pairs={{0,28},{4,24},{8,20},{12,16},{16,12},{20,8},{24,4},{28,0},{1,29},{... | collective-permute-start | bytes 786440 | tf_op jit(solution)/shard_map/ppermute | solution.py:173
  208.9 23.7 %collective-permute-start.22 = (bf16[2,128,256]{2,1,0:T(8,128)(2,1)}, bf16[2,128,256]{2,1,0:T(8,128)(2,1)S(1)}, u32[]{:S(2)}, u32[]{:S(2)}) collective-permute-start(bf16[2,128,256]{2,1,0:T(8,128)(2,1)} %get-tuple-element.72), channel_id=1, source_target_pairs={{0,12},{4,8},{8,4},{12,0},{16,28},{20,24},{24,20},{28,16},{1,13},{... | collective-permute-start | bytes 393224 | tf_op jit(solution)/shard_map/ppermute | solution.py:173
  211.2 21.4 %collective-permute-start.23 = (bf16[2,128,256]{2,1,0:T(8,128)(2,1)}, bf16[2,128,256]{2,1,0:T(8,128)(2,1)S(1)}, u32[]{:S(2)}, u32[]{:S(2)}) collective-permute-start(bf16[2,128,256]{2,1,0:T(8,128)(2,1)} %get-tuple-element.73), channel_id=1, source_target_pairs={{0,16},{4,20},{8,24},{12,28},{16,0},{20,4},{24,8},{28,12},{1,17},{... | collective-permute-start | bytes 393224 | tf_op jit(solution)/shard_map/ppermute | solution.py:173
  211.2 21.4 %collective-permute-start.24 = (bf16[2,128,256]{2,1,0:T(8,128)(2,1)}, bf16[2,128,256]{2,1,0:T(8,128)(2,1)S(1)}, u32[]{:S(2)}, u32[]{:S(2)}) collective-permute-start(bf16[2,128,256]{2,1,0:T(8,128)(2,1)} %get-tuple-element.74), channel_id=1, source_target_pairs={{0,20},{4,16},{8,28},{12,24},{16,4},{20,0},{24,12},{28,8},{1,21},{... | collective-permute-start | bytes 393224 | tf_op jit(solution)/shard_map/ppermute | solution.py:173
  211.3 21.3 %collective-permute-start.25 = (bf16[2,128,256]{2,1,0:T(8,128)(2,1)}, bf16[2,128,256]{2,1,0:T(8,128)(2,1)S(1)}, u32[]{:S(2)}, u32[]{:S(2)}) collective-permute-start(bf16[2,128,256]{2,1,0:T(8,128)(2,1)} %get-tuple-element.75), channel_id=1, source_target_pairs={{0,24},{4,28},{8,16},{12,20},{16,8},{20,12},{24,0},{28,4},{1,25},{... | collective-permute-start | bytes 393224 | tf_op jit(solution)/shard_map/ppermute | solution.py:173
  (79 other events, 1195.8 us)

commit v5 on v4

--- a/solution.py
+++ b/solution.py
@@ -12,6 +12,7 @@
 TERMS = 8
 GROUP = ("half", "grp")
 LANES = 256
+HALF = 128
 BF = jnp.bfloat16
 F32 = jnp.float32
 
@@ -106,9 +107,19 @@
     return jnp.where(wanted == source, 1.0, 0.0).astype(BF)
 
 
-def slot_kernel(terms_ref, oper_ref, core_ref, out_ref, core_f, core_t, core_p, mixed):
+def packed_rows(width_a, width_b):
+    each = width_a + width_b
+    beside = HALF // (width_a - HALF)
+    return each, TERMS * each + TERMS // beside * (width_a - width_b)
+
+
+def slot_kernel(terms_ref, oper_ref, core_ref, out_ref, core_f, core_t, core_p, mixed, rest):
     rows, width_b, width_a = core_ref.shape
-    width = out_ref.shape[2]
+    width = width_a + width_b
+    each, _ = packed_rows(width_a, width_b)
+    extra = width_a - HALF
+    beside = HALF // extra
+    rest[...] = jnp.zeros_like(rest)
     slots = terms_ref.shape[1]
     out_ref[...] = jnp.zeros_like(out_ref)
     mixed[...] = jnp.zeros_like(mixed)
@@ -140,11 +151,17 @@
                 core_p[q], mixed[q], (((1,), (1,)), ((), ())), preferred_element_type=F32
             )
         term = terms_ref[0, slot]
-        out_ref[term, :width_b, :] = (gram_a[:width_b] + gram_b).astype(BF)
-        out_ref[term, width_b:, :] = gram_a[width_b:].astype(BF)
+        at = pl.multiple_of(term * each, 16)
+        out_ref[pl.ds(at, width_a), :] = gram_a[:, :HALF].astype(BF)
+        both = gram_a[:width_b, HALF:] + gram_b[:, HALF:]
+        out_ref[pl.ds(at + width_a, width_b), :] = both.astype(BF)
+        moved = pltpu.roll(gram_a[width_b:, HALF:], (term % beside) * extra, 1)
+        rest[term // beside] = rest[term // beside] + moved
         return carry
 
     lax.fori_loop(0, live, one_slot, 0)
+    count, tail, _ = rest.shape
+    out_ref[TERMS * each :, :] = rest[...].reshape(count * tail, HALF).astype(BF)
 
 
 def tile_mean_fields(core_tensor, term_operators, block_terms):
@@ -154,7 +171,7 @@
     operators = term_operators.astype(F32).reshape(slots, rows * rows)
     return pl.pallas_call(
         slot_kernel,
-        out_shape=jax.ShapeDtypeStruct((TERMS, width_a, width), BF),
+        out_shape=jax.ShapeDtypeStruct((packed_rows(width_a, width_b)[1], HALF), BF),
         in_specs=[SMEM, SMEM, VMEM],
         out_specs=VMEM,
         scratch_shapes=[
@@ -162,6 +179,7 @@
             pltpu.VMEM((width, rows * width_b), BF),
             pltpu.VMEM((rows, width_b, width), BF),
             pltpu.VMEM((rows, width, width), BF),
+            pltpu.VMEM((TERMS * (width_a - HALF) // HALF, width_a - width_b, HALF), F32),
         ],
         cost_estimate=pl.CostEstimate(flops=10**9, bytes_accessed=2 * 10**6, transcendentals=0),
         name="slot_sums",
@@ -212,7 +230,6 @@
 
 
 def total_mean_fields(partial, potential):
-    terms, width_a, width = partial.shape
     group_index = lax.axis_index(GROUP)
     tile_index = lax.axis_index("tile")
     tile_bits = list(range(lax.axis_size("tile").bit_length() - 1))
@@ -220,30 +237,37 @@
     far = lax.axis_size("grp").bit_length() - 2
     near = [bit for bit in group_bits if bit != far]
     stages = [("tile", tile_index, tile_bits), (GROUP, group_index, near)]
-    array = partial.reshape(terms * width_a, width)
+    array = partial
     for axes, index, bits in stages:
         array = scatter_sum(array, axes, place_of(index, bits), bit_flips(bits))
     array = (array.astype(F32) + exchange(array, GROUP, 1 << far).astype(F32)).astype(BF)
     for axes, index, bits in reversed(stages):
         array = gather_blocks(array, axes, place_of(index, bits), bit_flips(bits))
         array, potential = lax.optimization_barrier((array, potential))
-    return array.reshape(terms, width_a, width), potential
-
-
-def action_kernel(on_chip, points_ref, weight_ref, mean_ref, out_ref, blocks):
-    width_a = mean_ref.shape[1]
+    return array, potential
+
+
+def action_kernel(width_a, on_chip, points_ref, weight_ref, mean_ref, out_ref, blocks):
     count_x, rows, width = points_ref.shape
     width_b = width - width_a
+    each, _ = packed_rows(width_a, width_b)
+    extra = width_a - HALF
+    beside, tail = HALF // extra, width_a - width_b
 
     @pl.when(pl.program_id(0) == 0)
     def _():
-        lane = lax.broadcasted_iota(jnp.int32, (width_a, width), 1)
+        blocks[...] = jnp.zeros_like(blocks)
         for term in range(TERMS):
-            packed = mean_ref[term].astype(F32)
-            blocks[term, :width_a, :] = jnp.where(lane < width_a, packed, 0.0).astype(BF)
-            blocks[term, width_a:, :] = jnp.where(
-                lane[:width_b] < width_a, 0.0, packed[:width_b]
-            ).astype(BF)
+            at = term * each
+            blocks[term, :width_a, :HALF] = mean_ref[at : at + width_a, :]
+            both = mean_ref[at + width_a : at + each, :].astype(F32)
+            lane = lax.broadcasted_iota(jnp.int32, (width_b, HALF), 1)
+            blocks[term, :width_b, HALF:] = jnp.where(lane < extra, both, 0.0).astype(BF)
+            blocks[term, width_a:, HALF:] = jnp.where(lane < extra, 0.0, both).astype(BF)
+            start = TERMS * each + term // beside * tail
+            other = mean_ref[start : start + tail, :].astype(F32)
+            other = pltpu.roll(other, (HALF - term % beside * extra) % HALF, 1)
+            blocks[term, width_b:width_a, HALF:] = jnp.where(lane[:tail] < extra, other, 0.0).astype(BF)
 
     step = 16
     while count_x % step or step * rows > 512:
@@ -267,7 +291,7 @@
         out_ref[pl.ds(base + start, step)] = total.reshape(step, rows, width)
 
 
-def action_rows(orbitals, weights, mean, first_row, rows, on_chip):
+def action_rows(width_a, orbitals, weights, mean, first_row, rows, on_chip):
     rows_x, _, width = orbitals.shape
     step = min(rows_x, 1024 // rows // 8 * 8)
     while rows_x % step:
@@ -276,13 +300,13 @@
     out = (rows_x, rows, width)
     block = pl.BlockSpec((step, rows, width), lambda i: (i, 0, 0))
     return pl.pallas_call(
-        functools.partial(action_kernel, on_chip),
+        functools.partial(action_kernel, width_a, on_chip),
         grid=(rows_x // step,),
         out_shape=pltpu.VMEM(out, F32) if on_chip else jax.ShapeDtypeStruct(out, F32),
         in_specs=[
             pl.BlockSpec((step, rows, width), lambda i: (i, at, 0)),
             pl.BlockSpec((step, rows, 2 * TERMS), lambda i: (i, at, 0)),
-            pl.BlockSpec(mean.shape, lambda i: (0, 0, 0)),
+            pl.BlockSpec(mean.shape, lambda i: (0, 0)),
         ],
         out_specs=VMEM if on_chip else block,
         scratch_shapes=[pltpu.VMEM((TERMS, width, width), BF)],
@@ -556,8 +580,11 @@
     last_row, last_rows = first_rows[-1], sizes[-1]
     weights = potential.reshape(2 * TERMS, rows_x * rows_y).T.astype(BF)
     weights = weights.reshape(rows_x, rows_y, 2 * TERMS)
-    action = action_rows(orbitals, weights, mean, 0, last_row, False)
-    action_last = action_rows(orbitals, weights, mean, last_row, last_rows, True)
+    width_a = core_tensor.shape[2]
+    action = action_rows(width_a, orbitals, weights, mean, 0, last_row, False)
+    action_last = action_rows(
+        width_a, orbitals, weights, mean, last_row, last_rows, True
+    )
     result = None
     for index, first in enumerate(first_rows[:-1]):
         result = join_chunk(me, action, returned[index], first, result, rows_y, side)
@@ -585,7 +612,12 @@
         and width_b % 16 == 0
         and width_a % 16 == 0
         and width_b <= width_a
-        and TERMS * width_a % (groups * tiles * 8) == 0
+        and width == 2 * HALF
+        and width_a > HALF
+        and HALF % (width_a - HALF) == 0
+        and TERMS % (HALF // (width_a - HALF)) == 0
+        and width_a - width_b <= width_b
+        and packed_rows(width_a, width_b)[1] % (groups // 2 * tiles * 8) == 0
     )
 
 

time: 235 us -> 234 us (level)
  waiting for transfers between devices: 64.2 us -> 48.9 us
  starting transfers between devices: 94.1 us -> 109 us
    ppermute x55, waiting for transfers between devices: 64.2 us -> 48.9 us  [exchange(): return lax.ppermute(array, axes, [(i, i ^ flip) for i in range(count)])]
    ppermute x55, starting transfers between devices: 94.1 us -> 109 us  [exchange(): return lax.ppermute(array, axes, [(i, i ^ flip) for i in range(count)])]
    unnamed x97 -> x85, local copies, waits for them, and re-layouts: 5.91 us -> 5.53 us
  transfers between devices with their start and end apart: 55 -> 55, of which waited for: 9 -> 7; matrix products, arithmetic and copies ran while one was open for 2% -> 2% of each run, Pallas kernels for 24% -> 25%
where the time goes in v5:
time: 234 us; the launch traced here: 233 us
  starting transfers between devices  109 us (47%)
  Pallas kernels  62.5 us (27%)
  waiting for transfers between devices  48.9 us (21%)
  local copies, waits for them, and re-layouts  10.7 us (5%)
    ppermute x55, starting transfers between devices, exchange(): return lax.ppermute(array, axes, [(i, i ^ flip) for i in range(count)])  109 us
    ppermute x55, waiting for transfers between devices, exchange(): return lax.ppermute(array, axes, [(i, i ^ flip) for i in range(count)])  48.9 us
    pallas_call x2, Pallas kernels, action_rows(): pl.pallas_call(functools.partial(action_kernel, width_a, on_chip), grid=(...  25 us
    pallas_call x3, Pallas kernels, apply_chunk(): pl.pallas_call(functools.partial(apply_kernel, groups), grid=(per,), out_...  15.5 us
    pallas_call x4, Pallas kernels, split_chunk(): pl.pallas_call(functools.partial(split_kernel, tuple(flips), side), grid=...  9.32 us
    pallas_call x2, Pallas kernels, join_chunk(): pl.pallas_call(functools.partial(join_kernel, side), grid=(chunk // rows,...  7.26 us
    unnamed x85, local copies, waits for them, and re-layouts  5.53 us
  transfers between devices with their start and end apart: 55, of which 7 were waited for; matrix products, arithmetic and copies ran while one was open for 2% of the time, Pallas kernels for 25%

profile of v5, /device:TPU:0, one launch (start us, length us, event | category | flops | bytes accessed | tf_op | source)
XLA Modules:
  0.0 233.0 jit_solution(2950372343732385798)
XLA Ops:
  3.3 4.2 %slot_sums.1 = bf16[2176,128]{1,0:T(8,128)(2,1)} custom-call(s32[1,8]{1,0:T(1,128)} %terms_ref.1, f32[8,64]{1,0:T(8,128)} %reshape.18.oper_ref, bf16[8,96,160]{2,1,0:T(8,128)(2,1)} %copy.10.core_ref), custom_call_target="tpu_custom_call" | custom-call | flops 1000000000 | bytes 2000000 | tf_op jit(solution)/shard_map/slot_sums/pallas_call | solution.py:172
  8.6 7.0 %collective-permute-start.1 = (bf16[544,128]{1,0:T(8,128)(2,1)S(1)}, bf16[544,128]{1,0:T(8,128)(2,1)S(1)}, u32[]{:S(2)}, u32[]{:S(2)}) collective-permute-start(bf16[544,128]{1,0:T(8,128)(2,1)S(1)} %get-tuple-element.113), channel_id=1, source_target_pairs={{0,2},{1,3},{2,0},{3,1},{4,6},{5,7},{6,4},{7,5},{8,10},{9,11},{10,... | collective-permute-start | bytes 417800 | tf_op jit(solution)/shard_map/ppermute | solution.py:191
  18.6 4.6 %collective-permute-start.28 = (bf16[2,128,256]{2,1,0:T(8,128)(2,1)}, bf16[2,128,256]{2,1,0:T(8,128)(2,1)S(1)}, u32[]{:S(2)}, u32[]{:S(2)}) collective-permute-start(bf16[2,128,256]{2,1,0:T(8,128)(2,1)} %get-tuple-element.79), channel_id=1, source_target_pairs={{0,8},{4,12},{8,0},{12,4},{16,24},{20,28},{24,16},{28,20},{1,9},{5... | collective-permute-start | bytes 393224 | tf_op jit(solution)/shard_map/ppermute | solution.py:191
  29.2 5.6 %collective-permute-start.4 = (bf16[136,128]{1,0:T(8,128)(2,1)S(1)}, bf16[136,128]{1,0:T(8,128)(2,1)S(1)}, u32[]{:S(2)}, u32[]{:S(2)}) collective-permute-start(bf16[136,128]{1,0:T(8,128)(2,1)S(1)} %get-tuple-element.116), channel_id=1, source_target_pairs={{0,16},{4,20},{8,24},{12,28},{16,0},{20,4},{24,8},{28,12},{1,17},{... | collective-permute-start | bytes 104456 | tf_op jit(solution)/shard_map/ppermute | solution.py:191
  50.8 11.0 %collective-permute-done.32.refs_6_ = bf16[2,128,256]{2,1,0:T(8,128)(2,1)S(1)} collective-permute-done((bf16[2,128,256]{2,1,0:T(8,128)(2,1)S(1)}, bf16[2,128,256]{2,1,0:T(8,128)(2,1)S(1)}, u32[]{:S(2)}, u32[]{:S(2)}) %collective-permute-start.32) | collective-permute-done | bytes 131104 | tf_op jit(solution)/shard_map/ppermute | solution.py:191
  67.6 3.7 %collective-permute-start.18 = (bf16[2,128,256]{2,1,0:T(8,128)(2,1)}, bf16[2,128,256]{2,1,0:T(8,128)(2,1)S(1)}, u32[]{:S(2)}, u32[]{:S(2)}) collective-permute-start(bf16[2,128,256]{2,1,0:T(8,128)(2,1)} %get-tuple-element.67), channel_id=1, source_target_pairs={{0,24},{4,28},{8,16},{12,20},{16,8},{20,12},{24,0},{28,4},{1,25},{... | collective-permute-start | bytes 393224 | tf_op jit(solution)/shard_map/ppermute | solution.py:191
  73.9 5.3 %collective-permute-done.17.refs_5_ = bf16[2,128,256]{2,1,0:T(8,128)(2,1)S(1)} collective-permute-done((bf16[2,128,256]{2,1,0:T(8,128)(2,1)}, bf16[2,128,256]{2,1,0:T(8,128)(2,1)S(1)}, u32[]{:S(2)}, u32[]{:S(2)}) %collective-permute-start.17) | collective-permute-done | bytes 131104 | tf_op jit(solution)/shard_map/ppermute | solution.py:191
  79.2 8.4 %collective-permute-done.18.refs_6_ = bf16[2,128,256]{2,1,0:T(8,128)(2,1)S(1)} collective-permute-done((bf16[2,128,256]{2,1,0:T(8,128)(2,1)}, bf16[2,128,256]{2,1,0:T(8,128)(2,1)S(1)}, u32[]{:S(2)}, u32[]{:S(2)}) %collective-permute-start.18) | collective-permute-done | bytes 131104 | tf_op jit(solution)/shard_map/ppermute | solution.py:191
  90.5 4.6 %apply.4 = (bf16[2,128,256]{2,1,0:T(8,128)(2,1)}, bf16[2,128,256]{2,1,0:T(8,128)(2,1)}, bf16[2,128,256]{2,1,0:T(8,128)(2,1)}, bf16[2,128,256]{2,1,0:T(8,128)(2,1...) custom-call(s32[1]{0:T(128)} %bitcast.me_ref, ...), custom_call_target="tpu_custom_call" | custom-call | flops 1073741824 | bytes 4000000 | tf_op jit(solution)/shard_map/apply/pallas_call | solution.py:411
  102.4 4.4 %apply.3 = (bf16[2,128,256]{2,1,0:T(8,128)(2,1)}, bf16[2,128,256]{2,1,0:T(8,128)(2,1)}, bf16[2,128,256]{2,1,0:T(8,128)(2,1)}, bf16[2,128,256]{2,1,0:T(8,128)(2,1...) custom-call(s32[1]{0:T(128)} %bitcast.me_ref, ...), custom_call_target="tpu_custom_call" | custom-call | flops 1073741824 | bytes 4000000 | tf_op jit(solution)/shard_map/apply/pallas_call | solution.py:411
  108.9 13.4 %collective-permute-start.34 = (bf16[2,128,256]{2,1,0:T(8,128)(2,1)}, bf16[2,128,256]{2,1,0:T(8,128)(2,1)S(1)}, u32[]{:S(2)}, u32[]{:S(2)}) collective-permute-start(bf16[2,128,256]{2,1,0:T(8,128)(2,1)} %get-tuple-element.86), channel_id=1, source_target_pairs={{0,4},{4,0},{8,12},{12,8},{16,20},{20,16},{24,28},{28,24},{1,5},{5... | collective-permute-start | bytes 393224 | tf_op jit(solution)/shard_map/ppermute | solution.py:191
  124.7 5.0 %collective-permute-done.46.refs_6_ = bf16[4,128,256]{2,1,0:T(8,128)(2,1)S(1)} collective-permute-done((bf16[4,128,256]{2,1,0:T(8,128)(2,1)S(1)}, bf16[4,128,256]{2,1,0:T(8,128)(2,1)S(1)}, u32[]{:S(2)}, u32[]{:S(2)}) %collective-permute-start.46) | collective-permute-done | bytes 262176 | tf_op jit(solution)/shard_map/ppermute | solution.py:191
  130.5 8.0 %collective-permute-start.38 = (bf16[2,128,256]{2,1,0:T(8,128)(2,1)}, bf16[2,128,256]{2,1,0:T(8,128)(2,1)S(1)}, u32[]{:S(2)}, u32[]{:S(2)}) collective-permute-start(bf16[2,128,256]{2,1,0:T(8,128)(2,1)} %get-tuple-element.90), channel_id=1, source_target_pairs={{0,20},{4,16},{8,28},{12,24},{16,4},{20,0},{24,12},{28,8},{1,21},{... | collective-permute-start | bytes 393224 | tf_op jit(solution)/shard_map/ppermute | solution.py:191
  141.9 6.5 %apply.5 = (bf16[4,128,256]{2,1,0:T(8,128)(2,1)}, bf16[4,128,256]{2,1,0:T(8,128)(2,1)}, bf16[4,128,256]{2,1,0:T(8,128)(2,1)}, bf16[4,128,256]{2,1,0:T(8,128)(2,1...) custom-call(s32[1]{0:T(128)} %bitcast.me_ref, ...), custom_call_target="tpu_custom_call" | custom-call | flops 2147483648 | bytes 4000000 | tf_op jit(solution)/shard_map/apply/pallas_call | solution.py:411
  151.8 3.5 %collective-permute-start.40 = (bf16[2,128,256]{2,1,0:T(8,128)(2,1)}, bf16[2,128,256]{2,1,0:T(8,128)(2,1)S(1)}, u32[]{:S(2)}, u32[]{:S(2)}) collective-permute-start(bf16[2,128,256]{2,1,0:T(8,128)(2,1)} %get-tuple-element.92), channel_id=1, source_target_pairs={{0,28},{4,24},{8,20},{12,16},{16,12},{20,8},{24,4},{28,0},{1,29},{... | collective-permute-start | bytes 393224 | tf_op jit(solution)/shard_map/ppermute | solution.py:191
  159.9 8.8 %collective-permute-done.40.refs_7_ = bf16[2,128,256]{2,1,0:T(8,128)(2,1)S(1)} collective-permute-done((bf16[2,128,256]{2,1,0:T(8,128)(2,1)}, bf16[2,128,256]{2,1,0:T(8,128)(2,1)S(1)}, u32[]{:S(2)}, u32[]{:S(2)}) %collective-permute-start.40) | collective-permute-done | bytes 131104 | tf_op jit(solution)/shard_map/ppermute | solution.py:191
  168.8 3.7 %collective-permute-start.50 = (bf16[4,128,256]{2,1,0:T(8,128)(2,1)}, bf16[4,128,256]{2,1,0:T(8,128)(2,1)S(1)}, u32[]{:S(2)}, u32[]{:S(2)}) collective-permute-start(bf16[4,128,256]{2,1,0:T(8,128)(2,1)} %get-tuple-element.104), channel_id=1, source_target_pairs={{0,12},{4,8},{8,4},{12,0},{16,28},{20,24},{24,20},{28,16},{1,13},{... | collective-permute-start | bytes 786440 | tf_op jit(solution)/shard_map/ppermute | solution.py:191
  172.5 9.6 %collective-permute-done.21.refs_2_ = bf16[2,128,256]{2,1,0:T(8,128)(2,1)S(1)} collective-permute-done((bf16[2,128,256]{2,1,0:T(8,128)(2,1)}, bf16[2,128,256]{2,1,0:T(8,128)(2,1)S(1)}, u32[]{:S(2)}, u32[]{:S(2)}) %collective-permute-start.21) | collective-permute-done | bytes 131104 | tf_op jit(solution)/shard_map/ppermute | solution.py:191
  182.1 3.4 %collective-permute-start.52 = (bf16[4,128,256]{2,1,0:T(8,128)(2,1)}, bf16[4,128,256]{2,1,0:T(8,128)(2,1)S(1)}, u32[]{:S(2)}, u32[]{:S(2)}) collective-permute-start(bf16[4,128,256]{2,1,0:T(8,128)(2,1)} %get-tuple-element.106), channel_id=1, source_target_pairs={{0,20},{4,16},{8,28},{12,24},{16,4},{20,0},{24,12},{28,8},{1,21},{... | collective-permute-start | bytes 786440 | tf_op jit(solution)/shard_map/ppermute | solution.py:191
  186.5 4.4 %collective-permute-start.54 = (bf16[4,128,256]{2,1,0:T(8,128)(2,1)S(1)}, bf16[4,128,256]{2,1,0:T(8,128)(2,1)S(1)}, u32[]{:S(2)}, u32[]{:S(2)}) collective-permute-start(bf16[4,128,256]{2,1,0:T(8,128)(2,1)S(1)} %copy-done.22), channel_id=1, source_target_pairs={{0,28},{4,24},{8,20},{12,16},{16,12},{20,8},{24,4},{28,0},{1,29},{... | collective-permute-start | bytes 786440 | tf_op jit(solution)/shard_map/ppermute | solution.py:191
  191.0 18.4 %action.3.action_ref = f32[128,48,256]{2,1,0:T(8,128)} custom-call(bf16[128,64,256]{2,1,0:T(8,128)(2,1)} %orb_ref.7, bf16[128,64,16]{2,1,0:T(8,128)(2,1)} %bitcast.7, bf16[2176,128]{1,0:T(8,128)(2,1)} %copy-done.2), custom_call_target="tpu_custom_call" | custom-call | flops 6442450944 | bytes 12582912 | tf_op jit(solution)/shard_map/action/pallas_call | solution.py:302
  212.0 4.1 %collective-permute-start.25 = (bf16[2,128,256]{2,1,0:T(8,128)(2,1)}, bf16[2,128,256]{2,1,0:T(8,128)(2,1)S(1)}, u32[]{:S(2)}, u32[]{:S(2)}) collective-permute-start(bf16[2,128,256]{2,1,0:T(8,128)(2,1)} %get-tuple-element.75), channel_id=1, source_target_pairs={{0,24},{4,28},{8,16},{12,20},{16,8},{20,12},{24,0},{28,4},{1,25},{... | collective-permute-start | bytes 393224 | tf_op jit(solution)/shard_map/ppermute | solution.py:191
  217.7 6.6 %action.2.action_ref = f32[128,16,256]{2,1,0:T(8,128)S(1)} custom-call(bf16[128,64,256]{2,1,0:T(8,128)(2,1)} %orb_ref.7, bf16[128,64,16]{2,1,0:T(8,128)(2,1)} %bitcast.8, bf16[2176,128]{1,0:T(8,128)(2,1)} %copy-done.2), custom_call_target="tpu_custom_call" | custom-call | flops 2147483648 | bytes 4194304 | tf_op jit(solution)/shard_map/action/pallas_call | solution.py:302
  224.3 4.3 %join.3.refs_8_ = bf16[128,64,256]{2,1,0:T(8,128)(2,1)} custom-call(s32[1]{0:T(128)} %bitcast.me_ref, f32[128,48,256]{2,1,0:T(8,128)} %action.3.action_ref, bf16[4,128,256]{2,1,0:T(8,128)(2,1)} %get-tuple-element.101.refs_0_, bf16[4,128,256]{2,1,0:T(8,128)(2,1)} %copy-done.4, bf16[4,128,256]{2,1,0:T(8,128)(2,1)} %copy-done.5, ...), custom_call_target="tpu_custom_call" | custom-call | flops 536870912 | bytes 8388608 | tf_op jit(solution)/shard_map/join/pallas_call | solution.py:465
  (203 shorter events, 73.7 us)
Async XLA Ops:
  24.9 19.9 %collective-permute-start.31 = (bf16[2,128,256]{2,1,0:T(8,128)(2,1)}, bf16[2,128,256]{2,1,0:T(8,128)(2,1)S(1)}, u32[]{:S(2)}, u32[]{:S(2)}) collective-permute-start(bf16[2,128,256]{2,1,0:T(8,128)(2,1)} %get-tuple-element.82), channel_id=1, source_target_pairs={{0,20},{4,16},{8,28},{12,24},{16,4},{20,0},{24,12},{28,8},{1,21},{... | collective-permute-start | bytes 393224 | tf_op jit(solution)/shard_map/ppermute | solution.py:191
  42.3 19.5 %collective-permute-start.32 = (bf16[2,128,256]{2,1,0:T(8,128)(2,1)S(1)}, bf16[2,128,256]{2,1,0:T(8,128)(2,1)S(1)}, u32[]{:S(2)}, u32[]{:S(2)}) collective-permute-start(bf16[2,128,256]{2,1,0:T(8,128)(2,1)S(1)} %copy-done.31), channel_id=1, source_target_pairs={{0,24},{4,28},{8,16},{12,20},{16,8},{20,12},{24,0},{28,4},{1,25},{... | collective-permute-start | bytes 393224 | tf_op jit(solution)/shard_map/ppermute | solution.py:191
  44.8 19.1 %collective-permute-start.33 = (bf16[2,128,256]{2,1,0:T(8,128)(2,1)S(1)}, bf16[2,128,256]{2,1,0:T(8,128)(2,1)S(1)}, u32[]{:S(2)}, u32[]{:S(2)}) collective-permute-start(bf16[2,128,256]{2,1,0:T(8,128)(2,1)S(1)} %copy-done.30), channel_id=1, source_target_pairs={{0,28},{4,24},{8,20},{12,16},{16,12},{20,8},{24,4},{28,0},{1,29},{... | collective-permute-start | bytes 393224 | tf_op jit(solution)/shard_map/ppermute | solution.py:191
  47.0 19.3 %collective-permute-start.14 = (bf16[2,128,256]{2,1,0:T(8,128)(2,1)}, bf16[2,128,256]{2,1,0:T(8,128)(2,1)S(1)}, u32[]{:S(2)}, u32[]{:S(2)}) collective-permute-start(bf16[2,128,256]{2,1,0:T(8,128)(2,1)} %get-tuple-element.63), channel_id=1, source_target_pairs={{0,8},{4,12},{8,0},{12,4},{16,24},{20,28},{24,16},{28,20},{1,9},{5... | collective-permute-start | bytes 393224 | tf_op jit(solution)/shard_map/ppermute | solution.py:191
  63.9 35.1 %collective-permute-start.41 = (bf16[4,128,256]{2,1,0:T(8,128)(2,1)S(1)}, bf16[4,128,256]{2,1,0:T(8,128)(2,1)S(1)}, u32[]{:S(2)}, u32[]{:S(2)}) collective-permute-start(bf16[4,128,256]{2,1,0:T(8,128)(2,1)S(1)} %get-tuple-element.94), channel_id=1, source_target_pairs={{0,4},{4,0},{8,12},{12,8},{16,20},{20,16},{24,28},{28,24},{1,5},{5... | collective-permute-start | bytes 786440 | tf_op jit(solution)/shard_map/ppermute | solution.py:191
  67.6 20.0 %collective-permute-start.18 = (bf16[2,128,256]{2,1,0:T(8,128)(2,1)}, bf16[2,128,256]{2,1,0:T(8,128)(2,1)S(1)}, u32[]{:S(2)}, u32[]{:S(2)}) collective-permute-start(bf16[2,128,256]{2,1,0:T(8,128)(2,1)} %get-tuple-element.67), channel_id=1, source_target_pairs={{0,24},{4,28},{8,16},{12,20},{16,8},{20,12},{24,0},{28,4},{1,25},{... | collective-permute-start | bytes 393224 | tf_op jit(solution)/shard_map/ppermute | solution.py:191
  73.4 33.4 %collective-permute-start.42 = (bf16[4,128,256]{2,1,0:T(8,128)(2,1)S(1)}, bf16[4,128,256]{2,1,0:T(8,128)(2,1)S(1)}, u32[]{:S(2)}, u32[]{:S(2)}) collective-permute-start(bf16[4,128,256]{2,1,0:T(8,128)(2,1)S(1)} %get-tuple-element.95), channel_id=1, source_target_pairs={{0,8},{4,12},{8,0},{12,4},{16,24},{20,28},{24,16},{28,20},{1,9},{5... | collective-permute-start | bytes 786440 | tf_op jit(solution)/shard_map/ppermute | solution.py:191
  97.5 24.7 %collective-permute-start.44 = (bf16[4,128,256]{2,1,0:T(8,128)(2,1)S(1)}, bf16[4,128,256]{2,1,0:T(8,128)(2,1)S(1)}, u32[]{:S(2)}, u32[]{:S(2)}) collective-permute-start(bf16[4,128,256]{2,1,0:T(8,128)(2,1)S(1)} %get-tuple-element.97), channel_id=1, source_target_pairs={{0,16},{4,20},{8,24},{12,28},{16,0},{20,4},{24,8},{28,12},{1,17},{... | collective-permute-start | bytes 786440 | tf_op jit(solution)/shard_map/ppermute | solution.py:191
  99.1 23.7 %collective-permute-start.45 = (bf16[4,128,256]{2,1,0:T(8,128)(2,1)S(1)}, bf16[4,128,256]{2,1,0:T(8,128)(2,1)S(1)}, u32[]{:S(2)}, u32[]{:S(2)}) collective-permute-start(bf16[4,128,256]{2,1,0:T(8,128)(2,1)S(1)} %get-tuple-element.98), channel_id=1, source_target_pairs={{0,20},{4,16},{8,28},{12,24},{16,4},{20,0},{24,12},{28,8},{1,21},{... | collective-permute-start | bytes 786440 | tf_op jit(solution)/shard_map/ppermute | solution.py:191
  99.1 30.6 %collective-permute-start.46 = (bf16[4,128,256]{2,1,0:T(8,128)(2,1)S(1)}, bf16[4,128,256]{2,1,0:T(8,128)(2,1)S(1)}, u32[]{:S(2)}, u32[]{:S(2)}) collective-permute-start(bf16[4,128,256]{2,1,0:T(8,128)(2,1)S(1)} %get-tuple-element.99), channel_id=1, source_target_pairs={{0,24},{4,28},{8,16},{12,20},{16,8},{20,12},{24,0},{28,4},{1,25},{... | collective-permute-start | bytes 786440 | tf_op jit(solution)/shard_map/ppermute | solution.py:191
  106.8 23.7 %collective-permute-start.47 = (bf16[4,128,256]{2,1,0:T(8,128)(2,1)S(1)}, bf16[4,128,256]{2,1,0:T(8,128)(2,1)S(1)}, u32[]{:S(2)}, u32[]{:S(2)}) collective-permute-start(bf16[4,128,256]{2,1,0:T(8,128)(2,1)S(1)} %get-tuple-element.100), channel_id=1, source_target_pairs={{0,28},{4,24},{8,20},{12,16},{16,12},{20,8},{24,4},{28,0},{1,29},{... | collective-permute-start | bytes 786440 | tf_op jit(solution)/shard_map/ppermute | solution.py:191
  108.9 29.6 %collective-permute-start.34 = (bf16[2,128,256]{2,1,0:T(8,128)(2,1)}, bf16[2,128,256]{2,1,0:T(8,128)(2,1)S(1)}, u32[]{:S(2)}, u32[]{:S(2)}) collective-permute-start(bf16[2,128,256]{2,1,0:T(8,128)(2,1)} %get-tuple-element.86), channel_id=1, source_target_pairs={{0,4},{4,0},{8,12},{12,8},{16,20},{20,16},{24,28},{28,24},{1,5},{5... | collective-permute-start | bytes 393224 | tf_op jit(solution)/shard_map/ppermute | solution.py:191
  148.4 37.0 %collective-permute-start.48 = (bf16[4,128,256]{2,1,0:T(8,128)(2,1)}, bf16[4,128,256]{2,1,0:T(8,128)(2,1)S(1)}, u32[]{:S(2)}, u32[]{:S(2)}) collective-permute-start(bf16[4,128,256]{2,1,0:T(8,128)(2,1)} %get-tuple-element.102), channel_id=1, source_target_pairs={{0,4},{4,0},{8,12},{12,8},{16,20},{20,16},{24,28},{28,24},{1,5},{5... | collective-permute-start | bytes 786440 | tf_op jit(solution)/shard_map/ppermute | solution.py:191
  150.0 36.5 %collective-permute-start.49 = (bf16[4,128,256]{2,1,0:T(8,128)(2,1)}, bf16[4,128,256]{2,1,0:T(8,128)(2,1)S(1)}, u32[]{:S(2)}, u32[]{:S(2)}) collective-permute-start(bf16[4,128,256]{2,1,0:T(8,128)(2,1)} %get-tuple-element.103), channel_id=1, source_target_pairs={{0,8},{4,12},{8,0},{12,4},{16,24},{20,28},{24,16},{28,20},{1,9},{5... | collective-permute-start | bytes 786440 | tf_op jit(solution)/shard_map/ppermute | solution.py:191
  156.4 25.7 %collective-permute-start.21 = (bf16[2,128,256]{2,1,0:T(8,128)(2,1)}, bf16[2,128,256]{2,1,0:T(8,128)(2,1)S(1)}, u32[]{:S(2)}, u32[]{:S(2)}) collective-permute-start(bf16[2,128,256]{2,1,0:T(8,128)(2,1)} %get-tuple-element.71), channel_id=1, source_target_pairs={{0,8},{4,12},{8,0},{12,4},{16,24},{20,28},{24,16},{28,20},{1,9},{5... | collective-permute-start | bytes 393224 | tf_op jit(solution)/shard_map/ppermute | solution.py:191
  168.8 40.6 %collective-permute-start.50 = (bf16[4,128,256]{2,1,0:T(8,128)(2,1)}, bf16[4,128,256]{2,1,0:T(8,128)(2,1)S(1)}, u32[]{:S(2)}, u32[]{:S(2)}) collective-permute-start(bf16[4,128,256]{2,1,0:T(8,128)(2,1)} %get-tuple-element.104), channel_id=1, source_target_pairs={{0,12},{4,8},{8,4},{12,0},{16,28},{20,24},{24,20},{28,16},{1,13},{... | collective-permute-start | bytes 786440 | tf_op jit(solution)/shard_map/ppermute | solution.py:191
  172.5 37.6 %collective-permute-start.51 = (bf16[4,128,256]{2,1,0:T(8,128)(2,1)}, bf16[4,128,256]{2,1,0:T(8,128)(2,1)S(1)}, u32[]{:S(2)}, u32[]{:S(2)}) collective-permute-start(bf16[4,128,256]{2,1,0:T(8,128)(2,1)} %get-tuple-element.105), channel_id=1, source_target_pairs={{0,16},{4,20},{8,24},{12,28},{16,0},{20,4},{24,8},{28,12},{1,17},{... | collective-permute-start | bytes 786440 | tf_op jit(solution)/shard_map/ppermute | solution.py:191
  182.1 28.9 %collective-permute-start.52 = (bf16[4,128,256]{2,1,0:T(8,128)(2,1)}, bf16[4,128,256]{2,1,0:T(8,128)(2,1)S(1)}, u32[]{:S(2)}, u32[]{:S(2)}) collective-permute-start(bf16[4,128,256]{2,1,0:T(8,128)(2,1)} %get-tuple-element.106), channel_id=1, source_target_pairs={{0,20},{4,16},{8,28},{12,24},{16,4},{20,0},{24,12},{28,8},{1,21},{... | collective-permute-start | bytes 786440 | tf_op jit(solution)/shard_map/ppermute | solution.py:191
  185.5 26.5 %collective-permute-start.53 = (bf16[4,128,256]{2,1,0:T(8,128)(2,1)}, bf16[4,128,256]{2,1,0:T(8,128)(2,1)S(1)}, u32[]{:S(2)}, u32[]{:S(2)}) collective-permute-start(bf16[4,128,256]{2,1,0:T(8,128)(2,1)} %get-tuple-element.107), channel_id=1, source_target_pairs={{0,24},{4,28},{8,16},{12,20},{16,8},{20,12},{24,0},{28,4},{1,25},{... | collective-permute-start | bytes 786440 | tf_op jit(solution)/shard_map/ppermute | solution.py:191
  186.5 29.6 %collective-permute-start.54 = (bf16[4,128,256]{2,1,0:T(8,128)(2,1)S(1)}, bf16[4,128,256]{2,1,0:T(8,128)(2,1)S(1)}, u32[]{:S(2)}, u32[]{:S(2)}) collective-permute-start(bf16[4,128,256]{2,1,0:T(8,128)(2,1)S(1)} %copy-done.22), channel_id=1, source_target_pairs={{0,28},{4,24},{8,20},{12,16},{16,12},{20,8},{24,4},{28,0},{1,29},{... | collective-permute-start | bytes 786440 | tf_op jit(solution)/shard_map/ppermute | solution.py:191
  210.1 21.5 %collective-permute-start.22 = (bf16[2,128,256]{2,1,0:T(8,128)(2,1)}, bf16[2,128,256]{2,1,0:T(8,128)(2,1)S(1)}, u32[]{:S(2)}, u32[]{:S(2)}) collective-permute-start(bf16[2,128,256]{2,1,0:T(8,128)(2,1)} %get-tuple-element.72), channel_id=1, source_target_pairs={{0,12},{4,8},{8,4},{12,0},{16,28},{20,24},{24,20},{28,16},{1,13},{... | collective-permute-start | bytes 393224 | tf_op jit(solution)/shard_map/ppermute | solution.py:191
  210.1 21.5 %collective-permute-start.23 = (bf16[2,128,256]{2,1,0:T(8,128)(2,1)}, bf16[2,128,256]{2,1,0:T(8,128)(2,1)S(1)}, u32[]{:S(2)}, u32[]{:S(2)}) collective-permute-start(bf16[2,128,256]{2,1,0:T(8,128)(2,1)} %get-tuple-element.73), channel_id=1, source_target_pairs={{0,16},{4,20},{8,24},{12,28},{16,0},{20,4},{24,8},{28,12},{1,17},{... | collective-permute-start | bytes 393224 | tf_op jit(solution)/shard_map/ppermute | solution.py:191
  211.0 20.6 %collective-permute-start.24 = (bf16[2,128,256]{2,1,0:T(8,128)(2,1)}, bf16[2,128,256]{2,1,0:T(8,128)(2,1)S(1)}, u32[]{:S(2)}, u32[]{:S(2)}) collective-permute-start(bf16[2,128,256]{2,1,0:T(8,128)(2,1)} %get-tuple-element.74), channel_id=1, source_target_pairs={{0,20},{4,16},{8,28},{12,24},{16,4},{20,0},{24,12},{28,8},{1,21},{... | collective-permute-start | bytes 393224 | tf_op jit(solution)/shard_map/ppermute | solution.py:191
  212.0 19.6 %collective-permute-start.25 = (bf16[2,128,256]{2,1,0:T(8,128)(2,1)}, bf16[2,128,256]{2,1,0:T(8,128)(2,1)S(1)}, u32[]{:S(2)}, u32[]{:S(2)}) collective-permute-start(bf16[2,128,256]{2,1,0:T(8,128)(2,1)} %get-tuple-element.75), channel_id=1, source_target_pairs={{0,24},{4,28},{8,16},{12,20},{16,8},{20,12},{24,0},{28,4},{1,25},{... | collective-permute-start | bytes 393224 | tf_op jit(solution)/shard_map/ppermute | solution.py:191
  (73 other events, 1118.6 us)

commit v6 on v4

--- a/solution.py
+++ b/solution.py
@@ -358,34 +358,35 @@
     )(me, orbitals)
 
 
-def apply_kernel(groups, me_ref, kin_ref, *refs):
+def apply_kernel(order, me_ref, kin_ref, *refs):
+    groups = len(order)
     pieces, outs = refs[:groups], refs[groups : 2 * groups]
     gathered, result = refs[2 * groups :]
     _, rows_x, _ = pieces[0].shape
     size_x = kin_ref.shape[0]
     me = me_ref[0]
-    for flip in range(groups):
+    for slot, flip in enumerate(order):
         start = pl.multiple_of((me ^ flip) * rows_x, rows_x)
-        gathered[pl.ds(start, rows_x), :] = pieces[flip][0]
+        gathered[pl.ds(start, rows_x), :] = pieces[slot][0]
     step = 512
     for start in range(0, size_x, step):
         applied = jnp.dot(
             kin_ref[start : start + step, :], gathered[...], preferred_element_type=F32
         )
         result[start : start + step, :] = applied.astype(BF)
-    for flip in range(groups):
+    for slot, flip in enumerate(order):
         start = pl.multiple_of((me ^ flip) * rows_x, rows_x)
-        outs[flip][0] = result[pl.ds(start, rows_x), :]
-
-
-def apply_chunk(me, kinetic, pieces):
+        outs[slot][0] = result[pl.ds(start, rows_x), :]
+
+
+def apply_chunk(me, kinetic, pieces, order):
     groups = len(pieces)
     per, rows_x, width = pieces[0].shape
     size_x = kinetic.shape[0]
     block = pl.BlockSpec((1, rows_x, width), lambda i: (i, 0, 0))
     whole = pl.BlockSpec((size_x, size_x), lambda i: (0, 0), pipeline_mode=pl.Buffered(1))
     return pl.pallas_call(
-        functools.partial(apply_kernel, groups),
+        functools.partial(apply_kernel, order),
         grid=(per,),
         out_shape=[jax.ShapeDtypeStruct((per, rows_x, width), BF)] * groups,
         in_specs=[SMEM, whole] + [block] * groups,
@@ -398,7 +399,7 @@
     )(me, kinetic, *pieces)
 
 
-def join_kernel(side, me_ref, action_ref, *refs):
+def join_kernel(side, order, me_ref, action_ref, *refs):
     pieces = refs[: side.groups]
     out_ref, matrix = refs[-2:]
     step_x, rows, width = out_ref.shape
@@ -406,7 +407,7 @@
 
     @pl.when((pl.program_id(0) == 0) & (pl.program_id(1) == 0))
     def _():
-        matrix[...] = place_matrix(me_ref[0], range(side.groups), side, True)
+        matrix[...] = place_matrix(me_ref[0], order, side, True)
 
     for part in range(rows // side.rows):
         here = slice(part * side.rows, (part + 1) * side.rows)
@@ -423,7 +424,7 @@
             out_ref[start : start + step, here, :] = total.astype(BF)
 
 
-def join_chunk(me, action, pieces, first_row, before, rows_y, side):
+def join_chunk(me, action, pieces, first_row, before, rows_y, side, order):
     groups = len(pieces)
     _, rows_x, width = pieces[0].shape
     chunk = pieces[0].shape[0] * groups
@@ -439,7 +440,7 @@
         aliases = {len(operands): 0}
         operands.append(before)
     return pl.pallas_call(
-        functools.partial(join_kernel, side),
+        functools.partial(join_kernel, side, order),
         grid=(chunk // rows, rows_x // step_x),
         out_shape=jax.ShapeDtypeStruct((rows_x, rows_y, width), BF),
         in_specs=in_specs,
@@ -455,12 +456,12 @@
     )(*operands)
 
 
-def last_join_kernel(side, first_row, me_ref, action_ref, *refs):
+def last_join_kernel(side, order, first_row, me_ref, action_ref, *refs):
     pieces = refs[: side.groups]
     out_ref, matrix, parts, sems = refs[-4:]
     rows_x, rows, width = action_ref.shape
     per, step = side.rows // side.groups, side.points
-    matrix[...] = place_matrix(me_ref[0], range(side.groups), side, True)
+    matrix[...] = place_matrix(me_ref[0], order, side, True)
     copies = []
     for at, start in enumerate(range(0, rows_x, step)):
         for part in range(rows // side.rows):
@@ -482,14 +483,14 @@
         copy.wait()
 
 
-def last_join(me, action, pieces, first_row, before, side):
+def last_join(me, action, pieces, first_row, before, side, order):
     rows_x, rows, width = action.shape
     blocks = rows_x // side.points
     pieces = [pltpu.with_memory_space_constraint(piece, pltpu.VMEM) for piece in pieces]
     action = pltpu.with_memory_space_constraint(action, pltpu.VMEM)
     hbm = pl.BlockSpec(memory_space=pl.ANY)
     return pl.pallas_call(
-        functools.partial(last_join_kernel, side, first_row),
+        functools.partial(last_join_kernel, side, order, first_row),
         out_shape=jax.ShapeDtypeStruct(before.shape, BF),
         in_specs=[SMEM] + [VMEM] * (1 + len(pieces)) + [hbm],
         out_specs=hbm,
@@ -516,11 +517,8 @@
     return {flip: exchange(pieces[flip], GROUP, flip) if flip else pieces[0] for flip in flips}
 
 
-def exchange_all(pieces, near_first):
-    far = far_flip()
-    order = sorted(range(len(pieces)), key=lambda flip: (bool(flip & far) == near_first, flip))
-    arrived = exchange_some(pieces, order)
-    return [arrived[flip] for flip in range(len(pieces))]
+def exchange_all(pieces, order):
+    return [exchange(piece, GROUP, flip) if flip else piece for piece, flip in zip(pieces, order)]
 
 
 def chunk_sizes(rows_y, side):
@@ -537,6 +535,7 @@
     first_rows = [sum(sizes[:index]) for index in range(len(sizes))]
     far = [flip for flip in range(groups) if flip & far_flip()]
     near = [flip for flip in range(groups) if flip not in far]
+    order = tuple(far + near)
     me = lax.axis_index(GROUP).astype(jnp.int32).reshape(1)
     returned = []
     for index, (first, size) in enumerate(zip(first_rows, sizes)):
@@ -545,12 +544,12 @@
             for flips in (far, near):
                 cut = split_chunk(me, orbitals, first, size, flips, side)
                 arrived.update(exchange_some(dict(zip(flips, cut)), flips))
-            pieces = [arrived[flip] for flip in range(groups)]
+            pieces = [arrived[flip] for flip in order]
         else:
-            pieces = split_chunk(me, orbitals, first, size, range(groups), side)
-            pieces = exchange_all(pieces, True)
-        pieces = apply_chunk(me, kinetic, pieces)
-        returned.append(exchange_all(pieces, True))
+            pieces = split_chunk(me, orbitals, first, size, order, side)
+            pieces = exchange_all(pieces, order)
+        pieces = apply_chunk(me, kinetic, pieces, order)
+        returned.append(exchange_all(pieces, order))
     partial = tile_mean_fields(core_tensor, term_operators, block_terms)
     mean, potential = total_mean_fields(partial, potential)
     last_row, last_rows = first_rows[-1], sizes[-1]
@@ -560,8 +559,10 @@
     action_last = action_rows(orbitals, weights, mean, last_row, last_rows, True)
     result = None
     for index, first in enumerate(first_rows[:-1]):
-        result = join_chunk(me, action, returned[index], first, result, rows_y, side)
-    result = last_join(me, action_last, returned[-1], last_row, result, side)
+        result = join_chunk(
+            me, action, returned[index], first, result, rows_y, side, order
+        )
+    result = last_join(me, action_last, returned[-1], last_row, result, side, order)
     return result
 
 

time: 235 us -> 250 us (1.064)
  waiting for transfers between devices: 64.2 us -> 73.3 us
  starting transfers between devices: 94.1 us -> 102 us
    ppermute x55, waiting for transfers between devices: 64.2 us -> 73.3 us  [exchange(): return lax.ppermute(array, axes, [(i, i ^ flip) for i in range(count)])]
    ppermute x55, starting transfers between devices: 94.1 us -> 102 us  [exchange(): return lax.ppermute(array, axes, [(i, i ^ flip) for i in range(count)])]
    unnamed x97 -> x89, local copies, waits for them, and re-layouts: 5.91 us -> 4.69 us
  transfers between devices with their start and end apart: 55 -> 55, of which waited for: 9 -> 9; matrix products, arithmetic and copies ran while one was open for 2% -> 1% of each run, Pallas kernels for 24% -> 23%
where the time goes in v6:
time: 250 us
  starting transfers between devices  102 us (41%)
  waiting for transfers between devices  73.3 us (29%)
  Pallas kernels  62.5 us (25%)
  local copies, waits for them, and re-layouts  9.79 us (4%)
    ppermute x55, starting transfers between devices, exchange(): return lax.ppermute(array, axes, [(i, i ^ flip) for i in range(count)])  102 us
    ppermute x55, waiting for transfers between devices, exchange(): return lax.ppermute(array, axes, [(i, i ^ flip) for i in range(count)])  73.3 us
    pallas_call x2, Pallas kernels, action_rows(): pl.pallas_call(functools.partial(action_kernel, on_chip), grid=(rows_x //...  24.9 us
    pallas_call x3, Pallas kernels, apply_chunk(): pl.pallas_call(functools.partial(apply_kernel, order), grid=(per,), out_s...  15.6 us
    pallas_call x4, Pallas kernels, split_chunk(): pl.pallas_call(functools.partial(split_kernel, tuple(flips), side), grid=...  9.43 us
    pallas_call x2, Pallas kernels, join_chunk(): pl.pallas_call(functools.partial(join_kernel, side, order), grid=(chunk /...  7.16 us
  transfers between devices with their start and end apart: 55, of which 9 were waited for; matrix products, arithmetic and copies ran while one was open for 1% of the time, Pallas kernels for 23%

profile of v6, /device:TPU:0, one launch (start us, length us, event | category | flops | bytes accessed | tf_op | source)
XLA Modules:
  0.0 249.8 jit_solution(10246543248897289848)
XLA Ops:
  3.3 4.2 %slot_sums.1 = bf16[8,160,256]{2,1,0:T(8,128)(2,1)} custom-call(s32[1,8]{1,0:T(1,128)} %terms_ref.1, f32[8,64]{1,0:T(8,128)} %reshape.26.oper_ref, bf16[8,96,160]{2,1,0:T(8,128)(2,1)} %copy.10.core_ref), custom_call_target="tpu_custom_call" | custom-call | flops 1000000000 | bytes 2000000 | tf_op jit(solution)/shard_map/slot_sums/pallas_call | solution.py:155
  8.7 7.0 %collective-permute-start.1 = (bf16[320,256]{1,0:T(8,128)(2,1)S(1)}, bf16[320,256]{1,0:T(8,128)(2,1)S(1)}, u32[]{:S(2)}, u32[]{:S(2)}) collective-permute-start(bf16[320,256]{1,0:T(8,128)(2,1)S(1)} %get-tuple-element.113), channel_id=1, source_target_pairs={{0,2},{1,3},{2,0},{3,1},{4,6},{5,7},{6,4},{7,5},{8,10},{9,11},{10,... | collective-permute-start | bytes 491528 | tf_op jit(solution)/shard_map/ppermute | solution.py:173
  15.7 2.6 %split.5 = (bf16[2,128,256]{2,1,0:T(8,128)(2,1)}, bf16[2,128,256]{2,1,0:T(8,128)(2,1)}, bf16[2,128,256]{2,1,0:T(8,128)(2,1)}, bf16[2,128,256]{2,1,0:T(8,128)(2,1...) custom-call(s32[1]{0:T(128)} %bitcast.me_ref, ...), custom_call_target="tpu_custom_call" | custom-call | flops 268435456 | bytes 2097152 | tf_op jit(solution)/shard_map/split/pallas_call | solution.py:342
  18.4 4.8 %collective-permute-start.27 = (bf16[2,128,256]{2,1,0:T(8,128)(2,1)}, bf16[2,128,256]{2,1,0:T(8,128)(2,1)S(1)}, u32[]{:S(2)}, u32[]{:S(2)}) collective-permute-start(bf16[2,128,256]{2,1,0:T(8,128)(2,1)} %get-tuple-element.77), channel_id=1, source_target_pairs={{0,8},{4,12},{8,0},{12,4},{16,24},{20,28},{24,16},{28,20},{1,9},{5... | collective-permute-start | bytes 393224 | tf_op jit(solution)/shard_map/ppermute | solution.py:173
  33.5 5.0 %collective-permute-start.32 = (bf16[2,128,256]{2,1,0:T(8,128)(2,1)S(1)}, bf16[2,128,256]{2,1,0:T(8,128)(2,1)}, u32[]{:S(2)}, u32[]{:S(2)}) collective-permute-start(bf16[2,128,256]{2,1,0:T(8,128)(2,1)S(1)} %copy-done.33), channel_id=1, source_target_pairs={{0,16},{4,20},{8,24},{12,28},{16,0},{20,4},{24,8},{28,12},{1,17},{... | collective-permute-start | bytes 393224 | tf_op jit(solution)/shard_map/ppermute | solution.py:173
  38.5 3.6 %collective-permute-start.33 = (bf16[2,128,256]{2,1,0:T(8,128)(2,1)S(1)}, bf16[2,128,256]{2,1,0:T(8,128)(2,1)}, u32[]{:S(2)}, u32[]{:S(2)}) collective-permute-start(bf16[2,128,256]{2,1,0:T(8,128)(2,1)S(1)} %copy-done.31), channel_id=1, source_target_pairs={{0,20},{4,16},{8,28},{12,24},{16,4},{20,0},{24,12},{28,8},{1,21},{... | collective-permute-start | bytes 393224 | tf_op jit(solution)/shard_map/ppermute | solution.py:173
  46.1 5.6 %collective-permute-start.5 = (bf16[80,256]{1,0:T(8,128)(2,1)S(1)}, bf16[80,256]{1,0:T(8,128)(2,1)S(1)}, u32[]{:S(2)}, u32[]{:S(2)}) collective-permute-start(bf16[80,256]{1,0:T(8,128)(2,1)S(1)} %get-tuple-element.115), channel_id=1, source_target_pairs={{0,20},{4,16},{8,28},{12,24},{16,4},{20,0},{24,12},{28,8},{1,21},{... | collective-permute-start | bytes 122888 | tf_op jit(solution)/shard_map/ppermute | solution.py:173
  61.0 9.6 %collective-permute-done.13.refs_0_ = bf16[2,128,256]{2,1,0:T(8,128)(2,1)S(1)} collective-permute-done((bf16[2,128,256]{2,1,0:T(8,128)(2,1)S(1)}, bf16[2,128,256]{2,1,0:T(8,128)(2,1)S(1)}, u32[]{:S(2)}, u32[]{:S(2)}) %collective-permute-start.13) | collective-permute-done | bytes 131104 | tf_op jit(solution)/shard_map/ppermute | solution.py:173
  70.6 4.6 %apply.4 = (bf16[2,128,256]{2,1,0:T(8,128)(2,1)}, bf16[2,128,256]{2,1,0:T(8,128)(2,1)}, bf16[2,128,256]{2,1,0:T(8,128)(2,1)}, bf16[2,128,256]{2,1,0:T(8,128)(2,1...) custom-call(s32[1]{0:T(128)} %bitcast.me_ref, ...), custom_call_target="tpu_custom_call" | custom-call | flops 1073741824 | bytes 4000000 | tf_op jit(solution)/shard_map/apply/pallas_call | solution.py:388
  75.9 2.9 %collective-permute-start.41 = (bf16[4,128,256]{2,1,0:T(8,128)(2,1)S(1)}, bf16[4,128,256]{2,1,0:T(8,128)(2,1)S(1)}, u32[]{:S(2)}, u32[]{:S(2)}) collective-permute-start(bf16[4,128,256]{2,1,0:T(8,128)(2,1)S(1)} %get-tuple-element.93), channel_id=1, source_target_pairs={{0,8},{4,12},{8,0},{12,4},{16,24},{20,28},{24,16},{28,20},{1,9},{5... | collective-permute-start | bytes 786440 | tf_op jit(solution)/shard_map/ppermute | solution.py:173
  83.8 8.2 %collective-permute-done.6 = bf16[80,256]{1,0:T(8,128)(2,1)S(1)} collective-permute-done((bf16[80,256]{1,0:T(8,128)(2,1)S(1)}, bf16[80,256]{1,0:T(8,128)(2,1)S(1)}, u32[]{:S(2)}, u32[]{:S(2)}) %collective-permute-start.6) | collective-permute-done | bytes 40992 | tf_op jit(solution)/shard_map/ppermute | solution.py:173
  92.9 12.0 %collective-permute-start.7 = (bf16[80,256]{1,0:T(8,128)(2,1)S(1)}, bf16[80,256]{1,0:T(8,128)(2,1)S(1)}, u32[]{:S(2)}, u32[]{:S(2)}) collective-permute-start(bf16[80,256]{1,0:T(8,128)(2,1)S(1)} %get-tuple-element.110), channel_id=1, source_target_pairs={{0,4},{4,0},{8,12},{12,8},{16,20},{20,16},{24,28},{28,24},{1,5},{5... | collective-permute-start | bytes 122888 | tf_op jit(solution)/shard_map/ppermute | solution.py:173
  107.3 4.5 %apply.3 = (bf16[2,128,256]{2,1,0:T(8,128)(2,1)}, bf16[2,128,256]{2,1,0:T(8,128)(2,1)}, bf16[2,128,256]{2,1,0:T(8,128)(2,1)}, bf16[2,128,256]{2,1,0:T(8,128)(2,1...) custom-call(s32[1]{0:T(128)} %bitcast.me_ref, ...), custom_call_target="tpu_custom_call" | custom-call | flops 1073741824 | bytes 4000000 | tf_op jit(solution)/shard_map/apply/pallas_call | solution.py:388
  116.0 2.8 %collective-permute-start.47 = (bf16[4,128,256]{2,1,0:T(8,128)(2,1)S(1)}, bf16[4,128,256]{2,1,0:T(8,128)(2,1)S(1)}, u32[]{:S(2)}, u32[]{:S(2)}) collective-permute-start(bf16[4,128,256]{2,1,0:T(8,128)(2,1)S(1)} %get-tuple-element.100), channel_id=1, source_target_pairs={{0,20},{4,16},{8,28},{12,24},{16,4},{20,0},{24,12},{28,8},{1,21},{... | collective-permute-start | bytes 786440 | tf_op jit(solution)/shard_map/ppermute | solution.py:173
  118.9 13.6 %collective-permute-done.9 = bf16[80,256]{1,0:T(8,128)(2,1)S(1)} collective-permute-done((bf16[80,256]{1,0:T(8,128)(2,1)S(1)}, bf16[80,256]{1,0:T(8,128)(2,1)S(1)}, u32[]{:S(2)}, u32[]{:S(2)}) %collective-permute-start.9) | collective-permute-done | bytes 40992 | tf_op jit(solution)/shard_map/ppermute | solution.py:173
  139.5 10.1 %collective-permute-done.34.refs_0_ = bf16[2,128,256]{2,1,0:T(8,128)(2,1)S(1)} collective-permute-done((bf16[2,128,256]{2,1,0:T(8,128)(2,1)}, bf16[2,128,256]{2,1,0:T(8,128)(2,1)S(1)}, u32[]{:S(2)}, u32[]{:S(2)}) %collective-permute-start.34) | collective-permute-done | bytes 131104 | tf_op jit(solution)/shard_map/ppermute | solution.py:173
  149.7 6.5 %apply.5 = (bf16[4,128,256]{2,1,0:T(8,128)(2,1)}, bf16[4,128,256]{2,1,0:T(8,128)(2,1)}, bf16[4,128,256]{2,1,0:T(8,128)(2,1)}, bf16[4,128,256]{2,1,0:T(8,128)(2,1...) custom-call(s32[1]{0:T(128)} %bitcast.me_ref, ...), custom_call_target="tpu_custom_call" | custom-call | flops 2147483648 | bytes 4000000 | tf_op jit(solution)/shard_map/apply/pallas_call | solution.py:388
  171.3 6.2 %collective-permute-done.40.refs_7_ = bf16[2,128,256]{2,1,0:T(8,128)(2,1)S(1)} collective-permute-done((bf16[2,128,256]{2,1,0:T(8,128)(2,1)}, bf16[2,128,256]{2,1,0:T(8,128)(2,1)S(1)}, u32[]{:S(2)}, u32[]{:S(2)}) %collective-permute-start.40) | collective-permute-done | bytes 131104 | tf_op jit(solution)/shard_map/ppermute | solution.py:173
  177.4 3.5 %collective-permute-start.50 = (bf16[4,128,256]{2,1,0:T(8,128)(2,1)}, bf16[4,128,256]{2,1,0:T(8,128)(2,1)S(1)}, u32[]{:S(2)}, u32[]{:S(2)}) collective-permute-start(bf16[4,128,256]{2,1,0:T(8,128)(2,1)} %get-tuple-element.103), channel_id=1, source_target_pairs={{0,24},{4,28},{8,16},{12,20},{16,8},{20,12},{24,0},{28,4},{1,25},{... | collective-permute-start | bytes 786440 | tf_op jit(solution)/shard_map/ppermute | solution.py:173
  180.9 20.9 %collective-permute-done.20.refs_0_ = bf16[2,128,256]{2,1,0:T(8,128)(2,1)S(1)} collective-permute-done((bf16[2,128,256]{2,1,0:T(8,128)(2,1)}, bf16[2,128,256]{2,1,0:T(8,128)(2,1)S(1)}, u32[]{:S(2)}, u32[]{:S(2)}) %collective-permute-start.20) | collective-permute-done | bytes 131104 | tf_op jit(solution)/shard_map/ppermute | solution.py:173
  207.7 18.3 %action.3.action_ref = f32[128,48,256]{2,1,0:T(8,128)} custom-call(bf16[128,64,256]{2,1,0:T(8,128)(2,1)} %orb_ref.7, bf16[128,64,16]{2,1,0:T(8,128)(2,1)} %bitcast.9, bf16[8,160,256]{2,1,0:T(8,128)(2,1)} %bitcast.11), custom_call_target="tpu_custom_call" | custom-call | flops 6442450944 | bytes 12582912 | tf_op jit(solution)/shard_map/action/pallas_call | solution.py:278
  234.7 6.6 %action.2.action_ref = f32[128,16,256]{2,1,0:T(8,128)S(1)} custom-call(bf16[128,64,256]{2,1,0:T(8,128)(2,1)} %orb_ref.7, bf16[128,64,16]{2,1,0:T(8,128)(2,1)} %bitcast.10, bf16[8,160,256]{2,1,0:T(8,128)(2,1)} %bitcast.12), custom_call_target="tpu_custom_call" | custom-call | flops 2147483648 | bytes 4194304 | tf_op jit(solution)/shard_map/action/pallas_call | solution.py:278
  241.2 4.2 %join.3.refs_8_ = bf16[128,64,256]{2,1,0:T(8,128)(2,1)} custom-call(s32[1]{0:T(128)} %bitcast.me_ref, f32[128,48,256]{2,1,0:T(8,128)} %action.3.action_ref, bf16[4,128,256]{2,1,0:T(8,128)(2,1)} %copy-done.4, bf16[4,128,256]{2,1,0:T(8,128)(2,1)} %copy-done.5, bf16[4,128,256]{2,1,0:T(8,128)(2,1)} %copy-done.6, bf16[4,128,256]{2,1,0:T(8,128)(2,1)} %copy-done.7, ...), custom_call_target="tpu_custom_call" | custom-call | flops 536870912 | bytes 8388608 | tf_op jit(solution)/shard_map/join/pallas_call | solution.py:442
  245.4 2.9 %join.4.refs_8_ = bf16[128,64,256]{2,1,0:T(8,128)(2,1)} custom-call(s32[1]{0:T(128)} %bitcast.me_ref, f32[128,48,256]{2,1,0:T(8,128)} %action.3.action_ref, bf16[2,128,256]{2,1,0:T(8,128)(2,1)} %copy-done.11, bf16[2,128,256]{2,1,0:T(8,128)(2,1)} %copy-done.12, bf16[2,128,256]{2,1,0:T(8,128)(2,1)} %copy-done.13, ...), custom_call_target="tpu_custom_call", output_to_operand_aliasing={{}: (10, {})} | custom-call | flops 268435456 | bytes 4194304 | tf_op jit(solution)/shard_map/join/pallas_call | solution.py:442
  (207 shorter events, 78.9 us)
Async XLA Ops:
  8.7 21.8 %collective-permute-start.1 = (bf16[320,256]{1,0:T(8,128)(2,1)S(1)}, bf16[320,256]{1,0:T(8,128)(2,1)S(1)}, u32[]{:S(2)}, u32[]{:S(2)}) collective-permute-start(bf16[320,256]{1,0:T(8,128)(2,1)S(1)} %get-tuple-element.113), channel_id=1, source_target_pairs={{0,2},{1,3},{2,0},{3,1},{4,6},{5,7},{6,4},{7,5},{8,10},{9,11},{10,... | collective-permute-start | bytes 491528 | tf_op jit(solution)/shard_map/ppermute | solution.py:173
  56.6 22.2 %collective-permute-start.15 = (bf16[2,128,256]{2,1,0:T(8,128)(2,1)S(1)}, bf16[2,128,256]{2,1,0:T(8,128)(2,1)}, u32[]{:S(2)}, u32[]{:S(2)}) collective-permute-start(bf16[2,128,256]{2,1,0:T(8,128)(2,1)S(1)} %copy-done.32), channel_id=1, source_target_pairs={{0,24},{4,28},{8,16},{12,20},{16,8},{20,12},{24,0},{28,4},{1,25},{... | collective-permute-start | bytes 393224 | tf_op jit(solution)/shard_map/ppermute | solution.py:173
  58.9 22.0 %collective-permute-start.16 = (bf16[2,128,256]{2,1,0:T(8,128)(2,1)}, bf16[2,128,256]{2,1,0:T(8,128)(2,1)}, u32[]{:S(2)}, u32[]{:S(2)}) collective-permute-start(bf16[2,128,256]{2,1,0:T(8,128)(2,1)} %get-tuple-element.64), channel_id=1, source_target_pairs={{0,28},{4,24},{8,20},{12,16},{16,12},{20,8},{24,4},{28,0},{1,29},{... | collective-permute-start | bytes 393224 | tf_op jit(solution)/shard_map/ppermute | solution.py:173
  75.9 35.9 %collective-permute-start.41 = (bf16[4,128,256]{2,1,0:T(8,128)(2,1)S(1)}, bf16[4,128,256]{2,1,0:T(8,128)(2,1)S(1)}, u32[]{:S(2)}, u32[]{:S(2)}) collective-permute-start(bf16[4,128,256]{2,1,0:T(8,128)(2,1)S(1)} %get-tuple-element.93), channel_id=1, source_target_pairs={{0,8},{4,12},{8,0},{12,4},{16,24},{20,28},{24,16},{28,20},{1,9},{5... | collective-permute-start | bytes 786440 | tf_op jit(solution)/shard_map/ppermute | solution.py:173
  78.8 34.2 %collective-permute-start.42 = (bf16[4,128,256]{2,1,0:T(8,128)(2,1)S(1)}, bf16[4,128,256]{2,1,0:T(8,128)(2,1)S(1)}, u32[]{:S(2)}, u32[]{:S(2)}) collective-permute-start(bf16[4,128,256]{2,1,0:T(8,128)(2,1)S(1)} %get-tuple-element.94), channel_id=1, source_target_pairs={{0,12},{4,8},{8,4},{12,0},{16,28},{20,24},{24,20},{28,16},{1,13},{... | collective-permute-start | bytes 786440 | tf_op jit(solution)/shard_map/ppermute | solution.py:173
  80.9 34.1 %collective-permute-start.43 = (bf16[4,128,256]{2,1,0:T(8,128)(2,1)S(1)}, bf16[4,128,256]{2,1,0:T(8,128)(2,1)S(1)}, u32[]{:S(2)}, u32[]{:S(2)}) collective-permute-start(bf16[4,128,256]{2,1,0:T(8,128)(2,1)S(1)} %get-tuple-element.95), channel_id=1, source_target_pairs={{0,24},{4,28},{8,16},{12,20},{16,8},{20,12},{24,0},{28,4},{1,25},{... | collective-permute-start | bytes 786440 | tf_op jit(solution)/shard_map/ppermute | solution.py:173
  92.9 23.1 %collective-permute-start.7 = (bf16[80,256]{1,0:T(8,128)(2,1)S(1)}, bf16[80,256]{1,0:T(8,128)(2,1)S(1)}, u32[]{:S(2)}, u32[]{:S(2)}) collective-permute-start(bf16[80,256]{1,0:T(8,128)(2,1)S(1)} %get-tuple-element.110), channel_id=1, source_target_pairs={{0,4},{4,0},{8,12},{12,8},{16,20},{20,16},{24,28},{28,24},{1,5},{5... | collective-permute-start | bytes 122888 | tf_op jit(solution)/shard_map/ppermute | solution.py:173
  111.8 22.2 %collective-permute-start.44 = (bf16[4,128,256]{2,1,0:T(8,128)(2,1)S(1)}, bf16[4,128,256]{2,1,0:T(8,128)(2,1)S(1)}, u32[]{:S(2)}, u32[]{:S(2)}) collective-permute-start(bf16[4,128,256]{2,1,0:T(8,128)(2,1)S(1)} %get-tuple-element.96), channel_id=1, source_target_pairs={{0,28},{4,24},{8,20},{12,16},{16,12},{20,8},{24,4},{28,0},{1,29},{... | collective-permute-start | bytes 786440 | tf_op jit(solution)/shard_map/ppermute | solution.py:173
  113.0 22.1 %collective-permute-start.45 = (bf16[4,128,256]{2,1,0:T(8,128)(2,1)S(1)}, bf16[4,128,256]{2,1,0:T(8,128)(2,1)S(1)}, u32[]{:S(2)}, u32[]{:S(2)}) collective-permute-start(bf16[4,128,256]{2,1,0:T(8,128)(2,1)S(1)} %get-tuple-element.98), channel_id=1, source_target_pairs={{0,4},{4,0},{8,12},{12,8},{16,20},{20,16},{24,28},{28,24},{1,5},{5... | collective-permute-start | bytes 786440 | tf_op jit(solution)/shard_map/ppermute | solution.py:173
  115.0 22.1 %collective-permute-start.46 = (bf16[4,128,256]{2,1,0:T(8,128)(2,1)S(1)}, bf16[4,128,256]{2,1,0:T(8,128)(2,1)S(1)}, u32[]{:S(2)}, u32[]{:S(2)}) collective-permute-start(bf16[4,128,256]{2,1,0:T(8,128)(2,1)S(1)} %get-tuple-element.99), channel_id=1, source_target_pairs={{0,16},{4,20},{8,24},{12,28},{16,0},{20,4},{24,8},{28,12},{1,17},{... | collective-permute-start | bytes 786440 | tf_op jit(solution)/shard_map/ppermute | solution.py:173
  116.0 23.4 %collective-permute-start.47 = (bf16[4,128,256]{2,1,0:T(8,128)(2,1)S(1)}, bf16[4,128,256]{2,1,0:T(8,128)(2,1)S(1)}, u32[]{:S(2)}, u32[]{:S(2)}) collective-permute-start(bf16[4,128,256]{2,1,0:T(8,128)(2,1)S(1)} %get-tuple-element.100), channel_id=1, source_target_pairs={{0,20},{4,16},{8,28},{12,24},{16,4},{20,0},{24,12},{28,8},{1,21},{... | collective-permute-start | bytes 786440 | tf_op jit(solution)/shard_map/ppermute | solution.py:173
  134.0 22.2 %collective-permute-start.35 = (bf16[2,128,256]{2,1,0:T(8,128)(2,1)}, bf16[2,128,256]{2,1,0:T(8,128)(2,1)S(1)}, u32[]{:S(2)}, u32[]{:S(2)}) collective-permute-start(bf16[2,128,256]{2,1,0:T(8,128)(2,1)} %get-tuple-element.86), channel_id=1, source_target_pairs={{0,12},{4,8},{8,4},{12,0},{16,28},{20,24},{24,20},{28,16},{1,13},{... | collective-permute-start | bytes 393224 | tf_op jit(solution)/shard_map/ppermute | solution.py:173
  135.1 22.4 %collective-permute-start.36 = (bf16[2,128,256]{2,1,0:T(8,128)(2,1)}, bf16[2,128,256]{2,1,0:T(8,128)(2,1)S(1)}, u32[]{:S(2)}, u32[]{:S(2)}) collective-permute-start(bf16[2,128,256]{2,1,0:T(8,128)(2,1)} %get-tuple-element.87), channel_id=1, source_target_pairs={{0,24},{4,28},{8,16},{12,20},{16,8},{20,12},{24,0},{28,4},{1,25},{... | collective-permute-start | bytes 393224 | tf_op jit(solution)/shard_map/ppermute | solution.py:173
  137.2 22.5 %collective-permute-start.37 = (bf16[2,128,256]{2,1,0:T(8,128)(2,1)}, bf16[2,128,256]{2,1,0:T(8,128)(2,1)S(1)}, u32[]{:S(2)}, u32[]{:S(2)}) collective-permute-start(bf16[2,128,256]{2,1,0:T(8,128)(2,1)} %get-tuple-element.88), channel_id=1, source_target_pairs={{0,28},{4,24},{8,20},{12,16},{16,12},{20,8},{24,4},{28,0},{1,29},{... | collective-permute-start | bytes 393224 | tf_op jit(solution)/shard_map/ppermute | solution.py:173
  160.9 44.2 %collective-permute-start.48 = (bf16[4,128,256]{2,1,0:T(8,128)(2,1)}, bf16[4,128,256]{2,1,0:T(8,128)(2,1)S(1)}, u32[]{:S(2)}, u32[]{:S(2)}) collective-permute-start(bf16[4,128,256]{2,1,0:T(8,128)(2,1)} %get-tuple-element.101), channel_id=1, source_target_pairs={{0,8},{4,12},{8,0},{12,4},{16,24},{20,28},{24,16},{28,20},{1,9},{5... | collective-permute-start | bytes 786440 | tf_op jit(solution)/shard_map/ppermute | solution.py:173
  162.0 43.4 %collective-permute-start.49 = (bf16[4,128,256]{2,1,0:T(8,128)(2,1)}, bf16[4,128,256]{2,1,0:T(8,128)(2,1)S(1)}, u32[]{:S(2)}, u32[]{:S(2)}) collective-permute-start(bf16[4,128,256]{2,1,0:T(8,128)(2,1)} %get-tuple-element.102), channel_id=1, source_target_pairs={{0,12},{4,8},{8,4},{12,0},{16,28},{20,24},{24,20},{28,16},{1,13},{... | collective-permute-start | bytes 786440 | tf_op jit(solution)/shard_map/ppermute | solution.py:173
  165.3 36.5 %collective-permute-start.20 = (bf16[2,128,256]{2,1,0:T(8,128)(2,1)}, bf16[2,128,256]{2,1,0:T(8,128)(2,1)S(1)}, u32[]{:S(2)}, u32[]{:S(2)}) collective-permute-start(bf16[2,128,256]{2,1,0:T(8,128)(2,1)} %get-tuple-element.69), channel_id=1, source_target_pairs={{0,8},{4,12},{8,0},{12,4},{16,24},{20,28},{24,16},{28,20},{1,9},{5... | collective-permute-start | bytes 393224 | tf_op jit(solution)/shard_map/ppermute | solution.py:173
  167.3 36.8 %collective-permute-start.21 = (bf16[2,128,256]{2,1,0:T(8,128)(2,1)}, bf16[2,128,256]{2,1,0:T(8,128)(2,1)S(1)}, u32[]{:S(2)}, u32[]{:S(2)}) collective-permute-start(bf16[2,128,256]{2,1,0:T(8,128)(2,1)} %get-tuple-element.70), channel_id=1, source_target_pairs={{0,12},{4,8},{8,4},{12,0},{16,28},{20,24},{24,20},{28,16},{1,13},{... | collective-permute-start | bytes 393224 | tf_op jit(solution)/shard_map/ppermute | solution.py:173
  177.4 48.6 %collective-permute-start.50 = (bf16[4,128,256]{2,1,0:T(8,128)(2,1)}, bf16[4,128,256]{2,1,0:T(8,128)(2,1)S(1)}, u32[]{:S(2)}, u32[]{:S(2)}) collective-permute-start(bf16[4,128,256]{2,1,0:T(8,128)(2,1)} %get-tuple-element.103), channel_id=1, source_target_pairs={{0,24},{4,28},{8,16},{12,20},{16,8},{20,12},{24,0},{28,4},{1,25},{... | collective-permute-start | bytes 786440 | tf_op jit(solution)/shard_map/ppermute | solution.py:173
  201.8 26.3 %collective-permute-start.51 = (bf16[4,128,256]{2,1,0:T(8,128)(2,1)}, bf16[4,128,256]{2,1,0:T(8,128)(2,1)S(1)}, u32[]{:S(2)}, u32[]{:S(2)}) collective-permute-start(bf16[4,128,256]{2,1,0:T(8,128)(2,1)} %get-tuple-element.104), channel_id=1, source_target_pairs={{0,28},{4,24},{8,20},{12,16},{16,12},{20,8},{24,4},{28,0},{1,29},{... | collective-permute-start | bytes 786440 | tf_op jit(solution)/shard_map/ppermute | solution.py:173
  204.1 26.4 %collective-permute-start.52 = (bf16[4,128,256]{2,1,0:T(8,128)(2,1)}, bf16[4,128,256]{2,1,0:T(8,128)(2,1)S(1)}, u32[]{:S(2)}, u32[]{:S(2)}) collective-permute-start(bf16[4,128,256]{2,1,0:T(8,128)(2,1)} %get-tuple-element.106), channel_id=1, source_target_pairs={{0,4},{4,0},{8,12},{12,8},{16,20},{20,16},{24,28},{28,24},{1,5},{5... | collective-permute-start | bytes 786440 | tf_op jit(solution)/shard_map/ppermute | solution.py:173
  205.1 25.4 %collective-permute-start.53 = (bf16[4,128,256]{2,1,0:T(8,128)(2,1)S(1)}, bf16[4,128,256]{2,1,0:T(8,128)(2,1)S(1)}, u32[]{:S(2)}, u32[]{:S(2)}) collective-permute-start(bf16[4,128,256]{2,1,0:T(8,128)(2,1)S(1)} %copy-done.22), channel_id=1, source_target_pairs={{0,16},{4,20},{8,24},{12,28},{16,0},{20,4},{24,8},{28,12},{1,17},{... | collective-permute-start | bytes 786440 | tf_op jit(solution)/shard_map/ppermute | solution.py:173
  205.4 26.2 %collective-permute-start.54 = (bf16[4,128,256]{2,1,0:T(8,128)(2,1)S(1)}, bf16[4,128,256]{2,1,0:T(8,128)(2,1)S(1)}, u32[]{:S(2)}, u32[]{:S(2)}) collective-permute-start(bf16[4,128,256]{2,1,0:T(8,128)(2,1)S(1)} %copy-done.21), channel_id=1, source_target_pairs={{0,20},{4,16},{8,28},{12,24},{16,4},{20,0},{24,12},{28,8},{1,21},{... | collective-permute-start | bytes 786440 | tf_op jit(solution)/shard_map/ppermute | solution.py:173
  226.1 22.3 %collective-permute-start.22 = (bf16[2,128,256]{2,1,0:T(8,128)(2,1)}, bf16[2,128,256]{2,1,0:T(8,128)(2,1)S(1)}, u32[]{:S(2)}, u32[]{:S(2)}) collective-permute-start(bf16[2,128,256]{2,1,0:T(8,128)(2,1)} %get-tuple-element.71), channel_id=1, source_target_pairs={{0,24},{4,28},{8,16},{12,20},{16,8},{20,12},{24,0},{28,4},{1,25},{... | collective-permute-start | bytes 393224 | tf_op jit(solution)/shard_map/ppermute | solution.py:173
  (75 other events, 1235.8 us)
